TPU v7x, 32 devices: a whole 2x2x4 slice. The times are simulated.
32 devices in a mesh: tok: 8 (over z, x), mdl: 4 (over y, core).
Axes of the slice: x: 2, y: 2, z: 4, core: 2. Of those that a mesh axis runs over, the one named last changes fastest.
Arguments:
- tokens: bfloat16 [10240, 1152], P('tok', 'mdl'), may hold values from -6 to 6
- cotangent: bfloat16 [10240, 1152], P('tok', 'mdl'), may hold values from -6 to 6
- lengths: int32 [8, 6], P('tok'), may hold values from 0 to 512, as said below
- padding: int32 [8, 6], P('tok'), may hold values from 0 to 63, as said below
- timesteps: int32 [8, 6], P('tok'), may hold values from 0 to 999
- labels: int32 [8, 6], P('tok'), may hold values from 0 to 999
- head_mask: int32 [8, 6, 16], P('tok', None, 'mdl'), may hold values 0 or 1
- chan_mask: int32 [8, 6, 16], P('tok', None, 'mdl'), may hold values 0 or 1
- keep_mask: int32 [10240], P('tok'), may hold values 0 or 1
- qkv_weight: bfloat16 [1152, 3, 1152], P('tok', None, 'mdl'), may hold values from -0.1875 to 0.1875
- qv_bias: bfloat16 [2, 1152], P(None, 'mdl'), may hold values from -3 to 3
- out_weight: bfloat16 [1152, 1152], P('mdl', 'tok'), may hold values from -0.375 to 0.375
- out_bias: bfloat16 [1152], P('mdl'), may hold values from -2 to 2
- up_weight: bfloat16 [1152, 4608], P('tok', 'mdl')
- up_bias: bfloat16 [4608], P('mdl'), may hold values from -3 to 3
- down_weight: bfloat16 [4608, 1152], P('mdl', 'tok'), may hold values from -0.125 to 0.125
- down_bias: bfloat16 [1152], P('mdl'), may hold values from -3 to 3
- ada_weight: bfloat16 [1152, 6, 1152], P('tok', None, 'mdl'), may hold values from -0.1875 to 0.1875
- ada_bias: bfloat16 [6, 1152], P(None, 'mdl'), may hold values from -3 to 3
- time_weight: bfloat16 [256, 1152], P('tok', 'mdl'), may hold values from -0.375 to 0.375
- class_table: bfloat16 [1000, 1152], P(None, 'mdl'), may hold values from -5 to 5
Outputs:
- output: bfloat16 [10240, 1152], P('tok', 'mdl')
- grad_tokens: float32 [10240, 1152], P('tok', 'mdl')
- grad_qkv_weight: float32 [1152, 3, 1152], P('tok', None, 'mdl')
- grad_qv_bias: float32 [2, 1152], P(None, 'mdl')
- grad_out_weight: float32 [1152, 1152], P('mdl', 'tok')
- grad_out_bias: float32 [1152], P('mdl')
- grad_up_weight: float32 [1152, 4608], P('tok', 'mdl')
- grad_up_bias: float32 [4608], P('mdl')
- grad_down_weight: float32 [4608, 1152], P('mdl', 'tok')
- grad_down_bias: float32 [1152], P('mdl')
- grad_ada_weight: float32 [1152, 6, 1152], P('tok', None, 'mdl')
- grad_ada_bias: float32 [6, 1152], P(None, 'mdl')
- grad_time_weight: float32 [256, 1152], P('tok', 'mdl')
- grad_class_table: float32 [1000, 1152], P(None, 'mdl')
Inputs may be any that keep to these rules, and one draw needn't show every extreme that they name: `lengths`: slot 0 of every row holds a crop; a slot's length is 0 (no crop) or 128 to 512. padding[r, j] tokens of padding follow crop slot j; the lengths and padding of a row sum to at most 1280, and the rest of the row is padding as well.
All inputs are finite; a program needn't handle non-finite values. No bound on the sum of `head_mask` or of `chan_mask` or of `keep_mask` on one device may be relied on, other than what follows from the above.
Results may differ from a plain program's by a relative error of at most 0.029.
The roundings to bfloat16 on the way count: a program that leaves them out, or rounds other values in their place, can miss the bound.
Values may be sent and summed in bfloat16 or wider, within the bound.
A program may use at most 192 MiB of HBM per device.

v0:
```python
import math

import jax
import jax.numpy as jnp
from jax import lax
from jax.sharding import PartitionSpec as P

norm_floor = 1e-06
unseen = -1e30


def exact_dot(left, right):
    return jnp.dot(left, right, precision=lax.Precision.HIGHEST, preferred_element_type=jnp.float32)


def timestep_features(steps, freq_count):
    half_freq = freq_count // 2
    freq_rates = jnp.exp(-math.log(10000.0) * jnp.arange(half_freq, dtype=jnp.float32) / half_freq)
    angles = steps.astype(jnp.float32)[:, None] * freq_rates[None, :]
    return jnp.concatenate([jnp.cos(angles), jnp.sin(angles)], axis=1)


def crop_layout(lengths, padding, row_len):
    span_sums = lengths + padding
    starts = jnp.cumsum(span_sums, axis=1) - span_sums
    positions = jnp.arange(row_len, dtype=jnp.int32)
    inside = (positions[None, :, None] >= starts[:, None, :]) & (
        positions[None, :, None] < (starts + lengths)[:, None, :]
    )
    slot_ids = jnp.arange(lengths.shape[1], dtype=jnp.int32)
    segment = jnp.min(jnp.where(inside, slot_ids[None, None, :], lengths.shape[1]), axis=2)
    return (inside, segment)


def layer_norm(values, full_width):
    totals = lax.psum((jnp.sum(values, axis=1), jnp.sum(values * values, axis=1)), "mdl")
    row_mean = totals[0] / full_width
    inverse = lax.rsqrt(totals[1] / full_width - row_mean * row_mean + norm_floor)
    return ((values - row_mean[:, None]) * inverse[:, None], inverse)


def norm_back(grad_norm, normed, inverse, full_width):
    totals = lax.psum((jnp.sum(grad_norm, axis=1), jnp.sum(grad_norm * normed, axis=1)), "mdl")
    return inverse[:, None] * (
        grad_norm - totals[0][:, None] / full_width - normed * totals[1][:, None] / full_width
    )


def spread_rows(rows_low):
    return lax.all_gather(rows_low, "mdl", axis=1, tiled=True)


def collect_branch(partial_rows):
    return lax.psum_scatter(
        partial_rows.astype(jnp.bfloat16), "mdl", scatter_dimension=1, tiled=True
    ).astype(jnp.float32)


def spread_grads(grad_low):
    return lax.all_gather(grad_low, "mdl", axis=1, tiled=True)


def reduce_grads(partial_grads):
    return lax.psum_scatter(
        partial_grads.astype(jnp.bfloat16), "mdl", scatter_dimension=1, tiled=True
    ).astype(jnp.float32)


def attend_row(queries, key_rows, value_rows, segment, score_scale):
    half_rows = queries.shape[0] // 2
    attend_parts = []
    logsum_parts = []
    for portion in range(2):
        row_start = portion * half_rows
        query_block = queries[row_start : row_start + half_rows]
        raw_scores = (
            jnp.einsum("qhd,khd->hqk", query_block, key_rows, preferred_element_type=jnp.float32)
            * score_scale
        )
        same_crop = segment[row_start : row_start + half_rows, None] == segment[None, :]
        raw_scores = jnp.where(same_crop[None], raw_scores, unseen)
        row_max = jnp.max(raw_scores, axis=2, keepdims=True)
        expo_terms = jnp.exp(raw_scores - row_max)
        row_total = jnp.sum(expo_terms, axis=2, keepdims=True)
        prob_low = (expo_terms / row_total).astype(jnp.bfloat16)
        attend_parts.append(
            jnp.einsum("hqk,khd->qhd", prob_low, value_rows, preferred_element_type=jnp.float32)
        )
        logsum_parts.append((row_max + jnp.log(row_total))[:, :, 0])
    return (jnp.concatenate(attend_parts, axis=0), jnp.concatenate(logsum_parts, axis=1))


def attend_back(queries, key_rows, value_rows, segment, logsum_rows, grad_att, score_scale):
    half_rows = queries.shape[0] // 2
    query_grads = []
    grad_keys = jnp.zeros(key_rows.shape, jnp.float32)
    grad_values = jnp.zeros(value_rows.shape, jnp.float32)
    for portion in range(2):
        row_start = portion * half_rows
        query_block = queries[row_start : row_start + half_rows]
        grad_block = grad_att[row_start : row_start + half_rows]
        raw_scores = (
            jnp.einsum("qhd,khd->hqk", query_block, key_rows, preferred_element_type=jnp.float32)
            * score_scale
        )
        same_crop = segment[row_start : row_start + half_rows, None] == segment[None, :]
        raw_scores = jnp.where(same_crop[None], raw_scores, unseen)
        prob_full = jnp.exp(raw_scores - logsum_rows[:, row_start : row_start + half_rows, None])
        grad_prob = jnp.einsum(
            "qhd,khd->hqk", grad_block, value_rows, preferred_element_type=jnp.float32
        )
        inner_sum = jnp.sum(prob_full * grad_prob, axis=2, keepdims=True)
        grad_scores = (prob_full * (grad_prob - inner_sum)).astype(jnp.bfloat16)
        query_grads.append(
            jnp.einsum("hqk,khd->qhd", grad_scores, key_rows, preferred_element_type=jnp.float32)
            * score_scale
        )
        grad_keys = (
            grad_keys
            + jnp.einsum(
                "hqk,qhd->khd", grad_scores, query_block, preferred_element_type=jnp.float32
            )
            * score_scale
        )
        grad_values = grad_values + jnp.einsum(
            "hqk,qhd->khd",
            prob_full.astype(jnp.bfloat16),
            grad_block,
            preferred_element_type=jnp.float32,
        )
    return (jnp.concatenate(query_grads, axis=0), grad_keys, grad_values)


def on_device(
    tokens,
    cotangent,
    lengths,
    padding,
    timesteps,
    labels,
    head_mask,
    chan_mask,
    keep_mask,
    qkv_weight,
    qv_bias,
    out_weight,
    out_bias,
    up_weight,
    up_bias,
    down_weight,
    down_bias,
    ada_weight,
    ada_bias,
    time_weight,
    class_table,
):
    row_count, slot_count = lengths.shape
    token_count, local_width = tokens.shape
    row_len = token_count // row_count
    crop_count = row_count * slot_count
    heads_here = head_mask.shape[2]
    head_width = local_width // heads_here
    units_here = up_bias.shape[0]
    groups_here = chan_mask.shape[2]
    full_width = local_width * lax.axis_size("mdl")
    score_scale = 1.0 / math.sqrt(head_width)
    inside, segment = crop_layout(lengths, padding, row_len)
    row_eye = jnp.eye(row_count, dtype=jnp.float32)
    crop_hot = jnp.einsum("rlc,rs->rlsc", inside.astype(jnp.float32), row_eye).reshape(
        token_count, crop_count
    )
    head_tok = exact_dot(crop_hot, head_mask.reshape(crop_count, heads_here).astype(jnp.float32))
    head_units = jnp.repeat(head_tok, head_width, axis=1).astype(jnp.bfloat16)
    chan_tok = exact_dot(crop_hot, chan_mask.reshape(crop_count, groups_here).astype(jnp.float32))
    chan_units = jnp.repeat(chan_tok, units_here // groups_here, axis=1)
    keep_rows = keep_mask.astype(jnp.float32)[:, None]
    label_hot = (
        labels.reshape(crop_count)[:, None]
        == jnp.arange(class_table.shape[0], dtype=jnp.int32)[None, :]
    ).astype(jnp.float32)
    class_local = class_table.astype(jnp.float32)

    def run_forward(weight_shards, start_rows):
        full_weights = (
            lax.all_gather(weight_shards[0], "tok", axis=0, tiled=True),
            lax.all_gather(weight_shards[1], "tok", axis=1, tiled=True),
            lax.all_gather(weight_shards[2], "tok", axis=0, tiled=True),
            lax.all_gather(weight_shards[3], "tok", axis=1, tiled=True),
            lax.all_gather(weight_shards[4], "tok", axis=0, tiled=True),
            lax.all_gather(weight_shards[5], "tok", axis=0, tiled=True),
        )
        qkv_full, out_full, up_full, down_full, ada_full, time_full = full_weights
        step_feats = timestep_features(timesteps.reshape(crop_count), time_full.shape[0])
        embedding = exact_dot(step_feats, time_full.astype(jnp.float32)) + exact_dot(
            label_hot, class_local
        )
        cond_full = lax.all_gather(
            jax.nn.silu(embedding).astype(jnp.bfloat16), "mdl", axis=1, tiled=True
        )
        modulation = (
            jnp.einsum("cd,dke->cke", cond_full, ada_full, preferred_element_type=jnp.float32)
            + ada_bias.astype(jnp.float32)[None]
        )
        per_token = exact_dot(crop_hot, modulation.reshape(crop_count, 6 * local_width)).reshape(
            token_count, 6, local_width
        )
        normed_one, inverse_one = layer_norm(start_rows, full_width)
        modulated_one = (normed_one * (1.0 + per_token[:, 1]) + per_token[:, 0]).astype(
            jnp.bfloat16
        )
        modulated_one_full = spread_rows(modulated_one)
        projected = jnp.einsum(
            "td,dke->tke", modulated_one_full, qkv_full, preferred_element_type=jnp.float32
        )
        queries = (projected[:, 0] + qv_bias[0].astype(jnp.float32)).astype(jnp.bfloat16)
        key_rows = projected[:, 1].astype(jnp.bfloat16)
        value_rows = (projected[:, 2] + qv_bias[1].astype(jnp.float32)).astype(jnp.bfloat16)
        attend_now, logsum_now = attend_row(
            queries.reshape(row_len, heads_here, head_width),
            key_rows.reshape(row_len, heads_here, head_width),
            value_rows.reshape(row_len, heads_here, head_width),
            segment[0],
            score_scale,
        )
        attend_parts = attend_now.reshape(row_len, local_width)
        logsum_parts = [logsum_now]
        attended = (attend_parts * head_units.astype(jnp.float32)).astype(jnp.bfloat16)
        attn_branch = collect_branch(
            jnp.dot(attended, out_full, preferred_element_type=jnp.float32)
        ) + out_bias.astype(jnp.float32)
        middle = start_rows + per_token[:, 2] * attn_branch
        normed_two, inverse_two = layer_norm(middle, full_width)
        modulated_two = (normed_two * (1.0 + per_token[:, 4]) + per_token[:, 3]).astype(
            jnp.bfloat16
        )
        modulated_two_full = spread_rows(modulated_two)
        up_pre = jnp.dot(
            modulated_two_full, up_full, preferred_element_type=jnp.float32
        ) + up_bias.astype(jnp.float32)
        hidden = (jax.nn.gelu(up_pre, approximate=True) * chan_units).astype(jnp.bfloat16)
        mlp_out = collect_branch(
            jnp.dot(hidden, down_full, preferred_element_type=jnp.float32)
        ) + down_bias.astype(jnp.float32)
        result = middle + per_token[:, 5] * keep_rows * mlp_out
        return (
            full_weights,
            embedding,
            cond_full,
            step_feats,
            per_token,
            normed_one,
            inverse_one,
            modulated_one_full,
            queries,
            key_rows,
            value_rows,
            logsum_parts,
            attended,
            attn_branch,
            normed_two,
            inverse_two,
            modulated_two_full,
            up_pre,
            hidden,
            mlp_out,
            result,
        )

    weight_shards = (qkv_weight, out_weight, up_weight, down_weight, ada_weight, time_weight)
    start_rows = tokens.astype(jnp.float32)
    kept_state = run_forward(weight_shards, start_rows)
    output = kept_state[-1].astype(jnp.bfloat16)
    output, fresh_shards, fresh_rows = lax.optimization_barrier((output, weight_shards, start_rows))
    recomputed = run_forward(fresh_shards, fresh_rows)
    (
        full_weights,
        embedding,
        cond_full,
        step_feats,
        per_token,
        normed_one,
        inverse_one,
        modulated_one_full,
        queries,
        key_rows,
        value_rows,
        logsum_parts,
        attended,
        attn_branch,
        normed_two,
        inverse_two,
        modulated_two_full,
        up_pre,
        hidden,
        mlp_out,
        unused_rows,
    ) = recomputed
    qkv_full, out_full, up_full, down_full, ada_full, time_full = full_weights
    scale_one = per_token[:, 1]
    gate_one = per_token[:, 2]
    scale_two = per_token[:, 4]
    gate_two = per_token[:, 5]
    grad_rows = cotangent.astype(jnp.float32)
    grad_mlp = (grad_rows * gate_two * keep_rows).astype(jnp.bfloat16)
    grad_mlp_full = spread_grads(grad_mlp)
    grad_down = jnp.einsum("th,td->hd", hidden, grad_mlp_full, preferred_element_type=jnp.float32)
    grad_down_bias = jnp.sum(grad_mlp.astype(jnp.float32), axis=0)
    grad_hidden = jnp.einsum(
        "td,hd->th", grad_mlp_full, down_full, preferred_element_type=jnp.float32
    )
    gelu_values, gelu_back = jax.vjp(
        lambda pre_acts: jax.nn.gelu(pre_acts, approximate=True), up_pre
    )
    grad_up_pre = gelu_back(grad_hidden * chan_units)[0].astype(jnp.bfloat16)
    grad_up = jnp.einsum(
        "td,th->dh", modulated_two_full, grad_up_pre, preferred_element_type=jnp.float32
    )
    grad_up_bias = jnp.sum(grad_up_pre.astype(jnp.float32), axis=0)
    grad_two = reduce_grads(
        jnp.einsum("th,dh->td", grad_up_pre, up_full, preferred_element_type=jnp.float32)
    )
    grad_gate_two = grad_rows * keep_rows * mlp_out
    grad_middle = grad_rows + norm_back(
        grad_two * (1.0 + scale_two), normed_two, inverse_two, full_width
    )
    grad_attn = (grad_middle * gate_one).astype(jnp.bfloat16)
    grad_attn_full = spread_grads(grad_attn)
    grad_out = jnp.einsum("tc,td->cd", attended, grad_attn_full, preferred_element_type=jnp.float32)
    grad_out_bias = jnp.sum(grad_attn.astype(jnp.float32), axis=0)
    grad_att = (
        jnp.einsum(
            "td,cd->tc", grad_attn_full, out_full, preferred_element_type=jnp.float32
        ).astype(jnp.bfloat16)
        * head_units
    )
    grad_gate_one = grad_middle * attn_branch
    grad_query_row, grad_key_row, grad_value_row = attend_back(
        queries.reshape(row_len, heads_here, head_width),
        key_rows.reshape(row_len, heads_here, head_width),
        value_rows.reshape(row_len, heads_here, head_width),
        segment[0],
        logsum_parts[0],
        grad_att.reshape(row_len, heads_here, head_width),
        score_scale,
    )
    query_parts = grad_query_row.reshape(row_len, local_width)
    key_parts = grad_key_row.reshape(row_len, local_width)
    value_parts = grad_value_row.reshape(row_len, local_width)
    grad_qkv_rows = jnp.stack([query_parts, key_parts, value_parts], axis=1).astype(jnp.bfloat16)
    grad_qkv = jnp.einsum(
        "td,tke->dke", modulated_one_full, grad_qkv_rows, preferred_element_type=jnp.float32
    )
    grad_bias_rows = jnp.sum(grad_qkv_rows.astype(jnp.float32), axis=0)
    grad_qv_bias = jnp.stack([grad_bias_rows[0], grad_bias_rows[2]], axis=0)
    grad_one = reduce_grads(
        jnp.einsum("tke,dke->td", grad_qkv_rows, qkv_full, preferred_element_type=jnp.float32)
    )
    grad_tokens = grad_middle + norm_back(
        grad_one * (1.0 + scale_one), normed_one, inverse_one, full_width
    )
    grad_per_token = jnp.stack(
        [
            grad_one,
            grad_one * normed_one,
            grad_gate_one,
            grad_two,
            grad_two * normed_two,
            grad_gate_two,
        ],
        axis=1,
    ).reshape(token_count, 6 * local_width)
    grad_mod = jnp.einsum(
        "tc,tf->cf", crop_hot, grad_per_token, precision=lax.Precision.HIGHEST
    ).reshape(crop_count, 6, local_width)
    grad_ada_bias = jnp.sum(grad_mod, axis=0)
    grad_ada = jnp.einsum(
        "cd,cke->dke", cond_full.astype(jnp.float32), grad_mod, precision=lax.Precision.HIGHEST
    )
    grad_cond = lax.psum_scatter(
        jnp.einsum(
            "cke,dke->cd", grad_mod, ada_full.astype(jnp.float32), precision=lax.Precision.HIGHEST
        ),
        "mdl",
        scatter_dimension=1,
        tiled=True,
    )
    silu_values, silu_back = jax.vjp(jax.nn.silu, embedding)
    grad_embed = silu_back(grad_cond)[0]
    grad_time = exact_dot(step_feats.T, grad_embed)
    grad_class = exact_dot(label_hot.T, grad_embed)
    grad_qkv, grad_out, grad_up, grad_down, grad_ada, grad_time = (
        lax.psum_scatter(grad_qkv, "tok", scatter_dimension=0, tiled=True),
        lax.psum_scatter(grad_out, "tok", scatter_dimension=1, tiled=True),
        lax.psum_scatter(grad_up, "tok", scatter_dimension=0, tiled=True),
        lax.psum_scatter(grad_down, "tok", scatter_dimension=1, tiled=True),
        lax.psum_scatter(grad_ada, "tok", scatter_dimension=0, tiled=True),
        lax.psum_scatter(grad_time, "tok", scatter_dimension=0, tiled=True),
    )
    grad_class, grad_qv_bias, grad_out_bias, grad_up_bias, grad_down_bias, grad_ada_bias = lax.psum(
        (grad_class, grad_qv_bias, grad_out_bias, grad_up_bias, grad_down_bias, grad_ada_bias),
        "tok",
    )
    return (
        output,
        grad_tokens,
        grad_qkv,
        grad_qv_bias,
        grad_out,
        grad_out_bias,
        grad_up,
        grad_up_bias,
        grad_down,
        grad_down_bias,
        grad_ada,
        grad_ada_bias,
        grad_time,
        grad_class,
    )


def solution(mesh):
    return jax.shard_map(
        on_device,
        mesh=mesh,
        in_specs=(
            P("tok", "mdl"),
            P("tok", "mdl"),
            P("tok", None),
            P("tok", None),
            P("tok", None),
            P("tok", None),
            P("tok", None, "mdl"),
            P("tok", None, "mdl"),
            P("tok"),
            P("tok", None, "mdl"),
            P(None, "mdl"),
            P("mdl", "tok"),
            P("mdl"),
            P("tok", "mdl"),
            P("mdl"),
            P("mdl", "tok"),
            P("mdl"),
            P("tok", None, "mdl"),
            P(None, "mdl"),
            P("tok", "mdl"),
            P(None, "mdl"),
        ),
        out_specs=(
            P("tok", "mdl"),
            P("tok", "mdl"),
            P("tok", None, "mdl"),
            P(None, "mdl"),
            P("mdl", "tok"),
            P("mdl"),
            P("tok", "mdl"),
            P("mdl"),
            P("mdl", "tok"),
            P("mdl"),
            P("tok", None, "mdl"),
            P(None, "mdl"),
            P("tok", "mdl"),
            P(None, "mdl"),
        ),
        check_vma=False,
    )
```

profile of v0, /device:TPU:0, one launch (start us, length us, event | category | flops | bytes accessed | tf_op | source)
XLA Modules:
  0.0 1912.3 jit_solution(6343728101269239566)
XLA Ops:
  9.4 33.3 %all_gather.60 = bf16[256,288]{1,0:T(8,128)(2,1)S(1)} all-gather(bf16[32,288]{1,0:T(8,128)(2,1)} %param.40), channel_id=1, replica_groups=mesh['tok'=8,'mdl'=4] {'tok'}, dimensions={0}, use_global_device_ids=true | all-gather | bytes 165888 | tf_op jit(solution)/shard_map/all_gather | solution.py:190
  64.6 36.6 %all-gather.17.cloned.1.call-done = bf16[1152,6,288]{2,0,1:T(8,128)(2,1)} async-done(((bf16[144,6,288]{2,0,1:T(8,128)(2,1)}), bf16[1152,6,288]{2,0,1:T(8,128)(2,1)}) %all-gather.17.cloned.1.call-update) | async-done | bytes 3981328 | tf_op jit(solution)/shard_map/all_gather | solution.py:189
  113.7 36.4 %all_gather.65 = bf16[288,1152]{0,1:T(8,128)(2,1)} all-gather(bf16[288,144]{0,1:T(8,128)(2,1)S(1)} %copy-done.34), channel_id=1, replica_groups=mesh['tok'=8,'mdl'=4] {'tok'}, dimensions={1}, use_global_device_ids=true | all-gather | bytes 746496 | tf_op jit(solution)/shard_map/all_gather | solution.py:186
  164.0 30.0 %all-gather.19.cloned.1.call-done = bf16[1280,1152]{0,1:T(8,128)(2,1)} async-done(((bf16[1280,288]{0,1:T(8,128)(2,1)}), bf16[1280,1152]{0,1:T(8,128)(2,1)}) %all-gather.19.cloned.1.call-update) | async-done | bytes 2949136 | tf_op jit(solution)/shard_map/all_gather | solution.py:50
  237.4 35.6 %reduce-scatter.16.cloned.1.call-done = bf16[1280,288]{0,1:T(8,128)(2,1)} async-done(((bf16[1280,1152]{0,1:T(8,128)(2,1)}), bf16[1280,288]{0,1:T(8,128)(2,1)}) %reduce-scatter.16.cloned.1.call-update) | async-done | bytes 737296 | tf_op jit(solution)/shard_map/reduce_scatter | solution.py:54
  299.3 31.1 %all-gather.25.cloned.1.call-done = bf16[1152,1152]{1,0:T(8,128)(2,1)} async-done(((bf16[144,1152]{1,0:T(8,128)(2,1)}), bf16[1152,1152]{1,0:T(8,128)(2,1)}) %all-gather.25.cloned.1.call-update) | async-done | bytes 2654224 | tf_op jit(solution)/shard_map/all_gather | solution.py:187
  330.4 55.9 %all-gather.27.cloned.1.call-done = bf16[1152,1152]{0,1:T(8,128)(2,1)} async-done(((bf16[1152,144]{0,1:T(8,128)(2,1)}), bf16[1152,1152]{0,1:T(8,128)(2,1)}) %all-gather.27.cloned.1.call-update) | async-done | bytes 2654224 | tf_op jit(solution)/shard_map/all_gather | solution.py:188
  386.3 28.2 %all-gather.23.cloned.1.call-done = bf16[1280,1152]{0,1:T(8,128)(2,1)} async-done(((bf16[1280,288]{0,1:T(8,128)(2,1)}), bf16[1280,1152]{0,1:T(8,128)(2,1)}) %all-gather.23.cloned.1.call-update) | async-done | bytes 2949136 | tf_op jit(solution)/shard_map/all_gather | solution.py:50
  414.5 16.1 convolution_convert_fusion.2
  432.0 35.5 %reduce-scatter.18.cloned.1.call-done = bf16[1280,288]{0,1:T(8,128)(2,1)} async-done(((bf16[1280,1152]{0,1:T(8,128)(2,1)}), bf16[1280,288]{0,1:T(8,128)(2,1)}) %reduce-scatter.18.cloned.1.call-update) | async-done | bytes 737296 | tf_op jit(solution)/shard_map/reduce_scatter | solution.py:54
  470.9 31.6 %all_gather.69 = bf16[256,288]{1,0:T(8,128)(2,1)S(1)} all-gather(bf16[32,288]{1,0:T(8,128)(2,1)S(1)} %copy-done.45), channel_id=1, replica_groups=mesh['tok'=8,'mdl'=4] {'tok'}, dimensions={0}, use_global_device_ids=true | all-gather | bytes 165888 | tf_op jit(solution)/shard_map/all_gather | solution.py:190
  519.9 38.7 %all-gather.29.cloned.1.call-done = bf16[1152,6,288]{2,0,1:T(8,128)(2,1)} async-done(((bf16[144,6,288]{2,0,1:T(8,128)(2,1)}), bf16[1152,6,288]{2,0,1:T(8,128)(2,1)}) %all-gather.29.cloned.1.call-update) | async-done | bytes 3981328 | tf_op jit(solution)/shard_map/all_gather | solution.py:189
  570.8 36.3 %all_gather.74 = bf16[288,1152]{0,1:T(8,128)(2,1)} all-gather(bf16[288,144]{0,1:T(8,128)(2,1)S(1)} %copy-done.34), channel_id=1, replica_groups=mesh['tok'=8,'mdl'=4] {'tok'}, dimensions={1}, use_global_device_ids=true | all-gather | bytes 746496 | tf_op jit(solution)/shard_map/all_gather | solution.py:186
  607.2 14.3 all-gather.33.cloned.1.call-done
  621.5 29.0 %all-gather.31.cloned.1.call-done = bf16[1280,1152]{0,1:T(8,128)(2,1)} async-done(((bf16[1280,288]{0,1:T(8,128)(2,1)}), bf16[1280,1152]{0,1:T(8,128)(2,1)}) %all-gather.31.cloned.1.call-update) | async-done | bytes 2949136 | tf_op jit(solution)/shard_map/all_gather | solution.py:50
  692.2 36.1 %reduce-scatter.20.cloned.1.call-done = bf16[1280,288]{0,1:T(8,128)(2,1)} async-done(((bf16[1280,1152]{0,1:T(8,128)(2,1)}), bf16[1280,288]{0,1:T(8,128)(2,1)}) %reduce-scatter.20.cloned.1.call-update) | async-done | bytes 737296 | tf_op jit(solution)/shard_map/reduce_scatter | solution.py:54
  746.3 39.4 %all-gather.41.cloned.1.call-done = bf16[1152,1152]{1,0:T(8,128)(2,1)} async-done(((bf16[144,1152]{1,0:T(8,128)(2,1)}), bf16[1152,1152]{1,0:T(8,128)(2,1)}) %all-gather.41.cloned.1.call-update) | async-done | bytes 2654224 | tf_op jit(solution)/shard_map/all_gather | solution.py:187
  785.7 28.1 %all-gather.39.cloned.1.call-done = bf16[1280,1152]{0,1:T(8,128)(2,1)} async-done(((bf16[1280,288]{0,1:T(8,128)(2,1)}), bf16[1280,1152]{0,1:T(8,128)(2,1)}) %all-gather.39.cloned.1.call-update) | async-done | bytes 2949136 | tf_op jit(solution)/shard_map/all_gather | solution.py:50
  827.7 43.4 %all-gather.37.cloned.1.call-done = bf16[1152,1152]{0,1:T(8,128)(2,1)} async-done(((bf16[1152,144]{0,1:T(8,128)(2,1)}), bf16[1152,1152]{0,1:T(8,128)(2,1)}) %all-gather.37.cloned.1.call-update) | async-done | bytes 2654224 | tf_op jit(solution)/shard_map/all_gather | solution.py:188
  871.1 28.1 %all-gather.35.cloned.1.call-done = bf16[1280,1152]{0,1:T(8,128)(2,1)} async-done(((bf16[1280,288]{0,1:T(8,128)(2,1)}), bf16[1280,1152]{0,1:T(8,128)(2,1)}) %all-gather.35.cloned.1.call-update) | async-done | bytes 2949136 | tf_op jit(solution)/shard_map/all_gather | solution.py:60
  919.6 36.8 %reduce-scatter.22.cloned.1.call-done = bf16[1280,288]{0,1:T(8,128)(2,1)} async-done(((bf16[1280,1152]{0,1:T(8,128)(2,1)}), bf16[1280,288]{0,1:T(8,128)(2,1)}) %reduce-scatter.22.cloned.1.call-update) | async-done | bytes 737296 | tf_op jit(solution)/shard_map/reduce_scatter | solution.py:64
  973.4 28.6 %all-gather.43.cloned.1.call-done = bf16[1280,1152]{0,1:T(8,128)(2,1)} async-done(((bf16[1280,288]{0,1:T(8,128)(2,1)}), bf16[1280,1152]{0,1:T(8,128)(2,1)}) %all-gather.43.cloned.1.call-update) | async-done | bytes 2949136 | tf_op jit(solution)/shard_map/all_gather | solution.py:60
  1068.3 28.5 %reduce-scatter.24.cloned.1.call-done = bf16[1280,288]{0,1:T(8,128)(2,1)} async-done(((bf16[1280,1152]{0,1:T(8,128)(2,1)}), bf16[1280,288]{0,1:T(8,128)(2,1)}) %reduce-scatter.24.cloned.1.call-update) | async-done | bytes 737296 | tf_op jit(solution)/shard_map/reduce_scatter | solution.py:64
  1105.8 30.4 %reduce-scatter.34.cloned.1.call-done = bf16[1280,288]{0,1:T(8,128)(2,1)} async-done(((bf16[1280,1152]{0,1:T(8,128)(2,1)}), bf16[1280,288]{0,1:T(8,128)(2,1)}) %reduce-scatter.34.cloned.1.call-update) | async-done | bytes 737296 | tf_op jit(solution)/shard_map/reduce_scatter | solution.py:54
  1200.3 39.4 %all-reduce = (f32[2,288]{1,0:T(2,128)}, f32[288]{0:T(512)}, f32[1152]{0:T(1024)}, f32[288]{0:T(512)}, f32[6,288]{1,0:T(8,128)}) all-reduce(f32[2,288]{1,0:T(2,128)S(1)} %pad_maximum_fusion.8, f32[288]{0:T(512)S(1)} %get-tuple-element.65, f32[1152]{0:T(1024)S(1)} %get-tuple-element.101, ...), channel_id=1, replica_groups=mesh['tok'=8,'mdl'=4] {'tok'}, use_global_device_ids=true, to_apply=%region_43.44 | all-reduce | flops 4032 | bytes 32256 | tf_op jit(solution)/shard_map/psum | solution.py:399
  1256.2 28.3 %reduce-scatter.30.cloned.1.call-done = f32[144,1152]{1,0:T(8,128)} async-done(((f32[1152,1152]{1,0:T(8,128)}), f32[144,1152]{1,0:T(8,128)}) %reduce-scatter.30.cloned.1.call-update) | async-done | bytes 663568 | tf_op jit(solution)/shard_map/reduce_scatter | solution.py:394
  1284.4 108.6 %reduce-scatter.32.cloned.1.call-done = f32[1152,144]{0,1:T(8,128)} async-done(((f32[1152,1152]{0,1:T(8,128)}), f32[1152,144]{0,1:T(8,128)}) %reduce-scatter.32.cloned.1.call-update) | async-done | bytes 663568 | tf_op jit(solution)/shard_map/reduce_scatter | solution.py:395
  1393.0 69.9 %reduce-scatter.28.cloned.1.call-done = f32[288,144]{0,1:T(8,128)} async-done(((f32[288,1152]{0,1:T(8,128)}), f32[288,144]{0,1:T(8,128)}) %reduce-scatter.28.cloned.1.call-update) | async-done | bytes 165904 | tf_op jit(solution)/shard_map/reduce_scatter | solution.py:393
  1462.9 64.5 %reduce-scatter.38.cloned.1.call-done = f32[32,288]{1,0:T(8,128)} async-done(((f32[256,288]{1,0:T(8,128)}), f32[32,288]{1,0:T(8,128)}) %reduce-scatter.38.cloned.1.call-update) | async-done | bytes 36880 | tf_op jit(solution)/shard_map/reduce_scatter | solution.py:397
  1527.4 83.4 %all-reduce.9.cloned.1.call-done = f32[1000,288]{0,1:T(8,128)} async-done(((f32[1000,288]{0,1:T(8,128)}), f32[1000,288]{0,1:T(8,128)}) %all-reduce.9.cloned.1.call-update) | async-done | bytes 1152016 | tf_op jit(solution)/shard_map/psum | solution.py:399
  1610.9 107.6 %reduce-scatter.26.cloned.1.call-done = f32[144,3,288]{2,0,1:T(8,128)} async-done(((f32[1152,3,288]{2,0,1:T(8,128)}), f32[144,3,288]{2,0,1:T(8,128)}) %reduce-scatter.26.cloned.1.call-update) | async-done | bytes 497680 | tf_op jit(solution)/shard_map/reduce_scatter | solution.py:392
  1718.4 184.3 %reduce-scatter.36.cloned.1.call-done = f32[144,6,288]{2,0,1:T(8,128)} async-done(((f32[1152,6,288]{2,0,1:T(8,128)}), f32[144,6,288]{2,0,1:T(8,128)}) %reduce-scatter.36.cloned.1.call-update) | async-done | bytes 995344 | tf_op jit(solution)/shard_map/reduce_scatter | solution.py:396
  (342 shorter events, 422.4 us)
Async XLA Ops:
  7.2 93.9 %all-gather.17.cloned.1.call-start = ((), (), s32[]{:S(2)}) async-start(), calls=%async_computation.13 | async-start | bytes 5971968 | tf_op jit(solution)/shard_map/all_gather | solution.py:189
  7.9 156.0 %all-gather.21.cloned.1.call-start = ((), (), s32[]{:S(2)}) async-start(), calls=%async_computation.15 | async-start | bytes 2985984 | tf_op jit(solution)/shard_map/all_gather | solution.py:185
  8.7 185.3 %all-gather.19.cloned.1.call-start = ((), (), s32[]{:S(2)}) async-start(), calls=%async_computation.14 | async-start | bytes 3686400 | tf_op jit(solution)/shard_map/all_gather | solution.py:50
  43.6 459.0 %copy-start.46 = (f32[6,128]{1,0:T(8,128)}, f32[6,128]{1,0:T(8,128)S(1)}, u32[]{:S(2)}) copy-start(f32[6,128]{1,0:T(8,128)S(1)} %get-tuple-element.91) | copy-start | bytes 9220
  64.6 497.6 %copy-start.53 = (s32[6]{0:T(128)}, s32[6]{0:T(128)S(1)}, u32[]{:S(2)}) copy-start(s32[6]{0:T(128)S(1)} %get-tuple-element.89) | copy-start | bytes 76
  64.6 497.6 %copy-start.55 = (s32[6]{0:T(128)}, s32[6]{0:T(128)S(1)}, u32[]{:S(2)}) copy-start(s32[6]{0:T(128)S(1)} %get-tuple-element.90) | copy-start | bytes 76
  113.2 159.9 %reduce-scatter.16.cloned.1.call-start = ((), (), s32[]{:S(2)}) async-start(), calls=%async_computation.16 | async-start | bytes 3686400 | tf_op jit(solution)/shard_map/reduce_scatter | solution.py:54
  236.2 94.2 %all-gather.25.cloned.1.call-start = ((), (), s32[]{:S(2)}) async-start(), calls=%async_computation.18 | async-start | bytes 2985984 | tf_op jit(solution)/shard_map/all_gather | solution.py:187
  236.8 149.5 %all-gather.27.cloned.1.call-start = ((), (), s32[]{:S(2)}) async-start(), calls=%async_computation.19 | async-start | bytes 2985984 | tf_op jit(solution)/shard_map/all_gather | solution.py:188
  237.4 177.2 %all-gather.23.cloned.1.call-start = ((), (), s32[]{:S(2)}) async-start(), calls=%async_computation.17 | async-start | bytes 3686400 | tf_op jit(solution)/shard_map/all_gather | solution.py:50
  288.3 179.2 %reduce-scatter.18.cloned.1.call-start = ((), (), s32[]{:S(2)}) async-start(), calls=%async_computation.20 | async-start | bytes 3686400 | tf_op jit(solution)/shard_map/reduce_scatter | solution.py:54
  430.6 128.1 %all-gather.29.cloned.1.call-start = ((), (), s32[]{:S(2)}) async-start(), calls=%async_computation.21 | async-start | bytes 5971968 | tf_op jit(solution)/shard_map/all_gather | solution.py:189
  470.3 151.2 %all-gather.33.cloned.1.call-start = ((), (), s32[]{:S(2)}) async-start(), calls=%async_computation.23 | async-start | bytes 2985984 | tf_op jit(solution)/shard_map/all_gather | solution.py:185
  470.8 179.6 %all-gather.31.cloned.1.call-start = ((), (), s32[]{:S(2)}) async-start(), calls=%async_computation.22 | async-start | bytes 3686400 | tf_op jit(solution)/shard_map/all_gather | solution.py:50
  570.8 157.5 %reduce-scatter.20.cloned.1.call-start = ((), (), s32[]{:S(2)}) async-start(), calls=%async_computation.24 | async-start | bytes 3686400 | tf_op jit(solution)/shard_map/reduce_scatter | solution.py:54
  691.4 94.3 %all-gather.41.cloned.1.call-start = ((), (), s32[]{:S(2)}) async-start(), calls=%async_computation.28 | async-start | bytes 2985984 | tf_op jit(solution)/shard_map/all_gather | solution.py:187
  692.1 121.7 %all-gather.39.cloned.1.call-start = ((), (), s32[]{:S(2)}) async-start(), calls=%async_computation.27 | async-start | bytes 3686400 | tf_op jit(solution)/shard_map/all_gather | solution.py:50
  745.1 126.0 %all-gather.37.cloned.1.call-start = ((), (), s32[]{:S(2)}) async-start(), calls=%async_computation.26 | async-start | bytes 2985984 | tf_op jit(solution)/shard_map/all_gather | solution.py:188
  745.7 153.5 %all-gather.35.cloned.1.call-start = ((), (), s32[]{:S(2)}) async-start(), calls=%async_computation.25 | async-start | bytes 3686400 | tf_op jit(solution)/shard_map/all_gather | solution.py:60
  746.3 210.1 %reduce-scatter.22.cloned.1.call-start = ((), (), s32[]{:S(2)}) async-start(), calls=%async_computation.29 | async-start | bytes 3686400 | tf_op jit(solution)/shard_map/reduce_scatter | solution.py:64
  919.5 82.4 %all-gather.43.cloned.1.call-start = ((), (), s32[]{:S(2)}) async-start(), calls=%async_computation.30 | async-start | bytes 3686400 | tf_op jit(solution)/shard_map/all_gather | solution.py:60
  973.3 123.6 %reduce-scatter.24.cloned.1.call-start = ((), (), s32[]{:S(2)}) async-start(), calls=%async_computation.31 | async-start | bytes 3686400 | tf_op jit(solution)/shard_map/reduce_scatter | solution.py:64
  1060.0 76.2 %reduce-scatter.34.cloned.1.call-start = ((), (), s32[]{:S(2)}) async-start(), calls=%async_computation.36 | async-start | bytes 3686400 | tf_op jit(solution)/shard_map/reduce_scatter | solution.py:54
  1068.3 109.4 %reduce-scatter.40.cloned.1.call-start = ((), (), s32[]{:S(2)}) async-start(), calls=%async_computation.40 | async-start | bytes 737280
  1153.3 131.2 %reduce-scatter.30.cloned.1.call-start = ((), (), s32[]{:S(2)}) async-start(), calls=%async_computation.34 | async-start | bytes 5971968 | tf_op jit(solution)/shard_map/reduce_scatter | solution.py:394
  1162.6 230.4 %reduce-scatter.32.cloned.1.call-start = ((), (), s32[]{:S(2)}) async-start(), calls=%async_computation.35 | async-start | bytes 5971968 | tf_op jit(solution)/shard_map/reduce_scatter | solution.py:395
  1171.7 291.2 %reduce-scatter.28.cloned.1.call-start = ((), (), s32[]{:S(2)}) async-start(), calls=%async_computation.33 | async-start | bytes 1990656 | tf_op jit(solution)/shard_map/reduce_scatter | solution.py:393
  1177.6 349.8 %reduce-scatter.38.cloned.1.call-start = ((), (), s32[]{:S(2)}) async-start(), calls=%async_computation.38 | async-start | bytes 442368 | tf_op jit(solution)/shard_map/reduce_scatter | solution.py:397
  1180.2 430.6 %all-reduce.9.cloned.1.call-start = ((), (), s32[]{:S(2)}) async-start(), calls=%async_computation.39 | async-start | bytes 2359296 | tf_op jit(solution)/shard_map/psum | solution.py:399
  1182.0 536.4 %reduce-scatter.26.cloned.1.call-start = ((), (), s32[]{:S(2)}) async-start(), calls=%async_computation.32 | async-start | bytes 5971968 | tf_op jit(solution)/shard_map/reduce_scatter | solution.py:392
  1190.5 712.2 %reduce-scatter.36.cloned.1.call-start = ((), (), s32[]{:S(2)}) async-start(), calls=%async_computation.37 | async-start | bytes 11943936 | tf_op jit(solution)/shard_map/reduce_scatter | solution.py:396
  1252.9 652.3 %copy-start.1 = (bf16[1000,288]{0,1:T(8,128)(2,1)S(1)}, bf16[1000,288]{0,1:T(8,128)(2,1)}, u32[]{:S(2)}) copy-start(bf16[1000,288]{0,1:T(8,128)(2,1)} %param.41) | copy-start | bytes 1728004
  (70 other events, 1547.3 us)
Sparse Core Ops, SparseCore 0:
  10.3 90.8 all-gather.16
  103.4 60.5 all-gather.20
  166.1 27.7 all-gather.18
  236.3 36.7 reduce-scatter.15
  275.3 55.0 all-gather.24
  332.6 53.5 all-gather.26
  388.5 25.9 all-gather.22
  430.7 36.7 reduce-scatter.17
  470.4 88.2 all-gather.28
  560.8 60.6 all-gather.32
  623.0 27.3 all-gather.30
  691.5 36.7 reduce-scatter.19
  730.6 55.0 all-gather.40
  787.8 25.9 all-gather.38
  816.1 55.0 all-gather.36
  873.2 25.9 all-gather.34
  919.6 36.7 reduce-scatter.21
  973.4 28.4 all-gather.42
  1060.1 36.7 reduce-scatter.23
  1099.4 36.7 reduce-scatter.33
  1153.4 22.0 reduce-scatter.39
  1179.7 104.7 reduce-scatter.29
  1289.0 103.9 reduce-scatter.31
  1396.9 65.9 reduce-scatter.27
  1467.1 60.2 reduce-scatter.37
  1531.8 79.0 all-reduce.8
  1614.9 103.5 reduce-scatter.25
  1723.0 179.6 reduce-scatter.35
where the time goes:
time: 1920 us; the launch traced here: 1910 us
  waiting for transfers between devices  1300 us (68%)
  blocking collectives  254 us (13%)
  matrix products  233 us (12%)
  other arithmetic  76.3 us (4%)
  local copies, waits for them, and re-layouts  33.3 us (2%)
    reduce_scatter x1, waiting for transfers between devices, on_device(): lax.psum_scatter(grad_ada, 'tok', scatter_dimension=0, tiled=True)  184 us
    reduce_scatter x4, waiting for transfers between devices, collect_branch(): lax.psum_scatter(partial_rows.astype(jnp.bfloat16), 'mdl', scatter_dimens...  138 us
    all_gather x4, waiting for transfers between devices, spread_rows(): return lax.all_gather(rows_low, 'mdl', axis=1, tiled=True)  115 us
    reduce_scatter x1, waiting for transfers between devices, on_device(): lax.psum_scatter(grad_down, 'tok', scatter_dimension=1, tiled=True)  109 us
    reduce_scatter x1, waiting for transfers between devices, on_device(): lax.psum_scatter(grad_qkv, 'tok', scatter_dimension=0, tiled=True)  108 us
    all_gather x2, waiting for transfers between devices, run_forward(): lax.all_gather(weight_shards[3], 'tok', axis=1, tiled=True)  99.3 us
    psum x1, waiting for transfers between devices, on_device(): lax.psum((grad_class, grad_qv_bias, grad_out_bias, grad_up_bias, grad_dow...  83.4 us
    all_gather x2, waiting for transfers between devices, run_forward(): lax.all_gather(weight_shards[4], 'tok', axis=0, tiled=True)  75.3 us
  transfers between devices with their start and end apart: 28, of which 27 were waited for; matrix products, arithmetic and copies ran while one was open for 7% of the time, Pallas kernels for 0%

commit v1 on v0

v1 whole, which is shorter than its diff:
```python
import math

import jax
import jax.numpy as jnp
from jax import lax
from jax.sharding import PartitionSpec as P

norm_floor = 1e-06
unseen = -1e30
f32 = jnp.float32
bf16 = jnp.bfloat16


def exact_dot(left, right):
    return jnp.dot(left, right, precision=lax.Precision.HIGHEST, preferred_element_type=f32)


def mm(left, right, dims):
    return lax.dot_general(left, right, (dims, ((), ())), preferred_element_type=f32)


def timestep_features(steps, freq_count):
    half_freq = freq_count // 2
    freq_rates = jnp.exp(-math.log(10000.0) * jnp.arange(half_freq, dtype=f32) / half_freq)
    angles = steps.astype(f32)[:, None] * freq_rates[None, :]
    return jnp.concatenate([jnp.cos(angles), jnp.sin(angles)], axis=1)


def crop_layout(lengths, padding, row_len):
    span_sums = lengths + padding
    starts = jnp.cumsum(span_sums, axis=1) - span_sums
    positions = jnp.arange(row_len, dtype=jnp.int32)
    inside = (positions[None, :, None] >= starts[:, None, :]) & (
        positions[None, :, None] < (starts + lengths)[:, None, :]
    )
    slot_ids = jnp.arange(lengths.shape[1], dtype=jnp.int32)
    segment = jnp.min(jnp.where(inside, slot_ids[None, None, :], lengths.shape[1]), axis=2)
    return (inside, segment)


def norm_rows(values):
    row_mean = jnp.mean(values, axis=1, keepdims=True)
    row_var = jnp.mean(values * values, axis=1, keepdims=True) - row_mean * row_mean
    inverse = lax.rsqrt(row_var + norm_floor)
    return ((values - row_mean) * inverse, inverse)


def gather_cols(rows_low):
    return lax.all_gather(rows_low, "mdl", axis=1, tiled=True)


def scatter_cols(partial_rows):
    return lax.psum_scatter(partial_rows.astype(bf16), "mdl", scatter_dimension=1, tiled=True)


def attend_row(queries, key_rows, value_rows, segment, score_scale):
    raw_scores = jnp.einsum("qhd,khd->hqk", queries, key_rows, preferred_element_type=f32) * score_scale
    same_crop = segment[:, None] == segment[None, :]
    raw_scores = jnp.where(same_crop[None], raw_scores, unseen)
    row_max = jnp.max(raw_scores, axis=2, keepdims=True)
    expo_terms = jnp.exp(raw_scores - row_max)
    row_total = jnp.sum(expo_terms, axis=2, keepdims=True)
    prob_low = (expo_terms / row_total).astype(bf16)
    attend = jnp.einsum("hqk,khd->qhd", prob_low, value_rows, preferred_element_type=f32)
    return (attend, (row_max + jnp.log(row_total))[:, :, 0])


def attend_back(queries, key_rows, value_rows, segment, logsum_rows, grad_att, score_scale):
    raw_scores = jnp.einsum("qhd,khd->hqk", queries, key_rows, preferred_element_type=f32) * score_scale
    same_crop = segment[:, None] == segment[None, :]
    raw_scores = jnp.where(same_crop[None], raw_scores, unseen)
    prob_full = jnp.exp(raw_scores - logsum_rows[:, :, None])
    grad_prob = jnp.einsum("qhd,khd->hqk", grad_att, value_rows, preferred_element_type=f32)
    inner_sum = jnp.sum(prob_full * grad_prob, axis=2, keepdims=True)
    grad_scores = (prob_full * (grad_prob - inner_sum)).astype(bf16)
    grad_queries = jnp.einsum("hqk,khd->qhd", grad_scores, key_rows, preferred_element_type=f32) * score_scale
    grad_keys = jnp.einsum("hqk,qhd->khd", grad_scores, queries, preferred_element_type=f32) * score_scale
    grad_values = jnp.einsum("hqk,qhd->khd", prob_full.astype(bf16), grad_att, preferred_element_type=f32)
    return (grad_queries, grad_keys, grad_values)


def on_device(
    tokens,
    cotangent,
    lengths,
    padding,
    timesteps,
    labels,
    head_mask,
    chan_mask,
    keep_mask,
    qkv_weight,
    qv_bias,
    out_weight,
    out_bias,
    up_weight,
    up_bias,
    down_weight,
    down_bias,
    ada_weight,
    ada_bias,
    time_weight,
    class_table,
):
    row_count, slot_count = lengths.shape
    token_count, local_width = tokens.shape
    row_len = token_count // row_count
    heads_here = head_mask.shape[2]
    head_width = local_width // heads_here
    units_here = up_bias.shape[0]
    groups_here = chan_mask.shape[2]
    own_rows = qkv_weight.shape[0]
    full_width = local_width * lax.axis_size("mdl")
    score_scale = 1.0 / math.sqrt(head_width)
    tok_at = lax.axis_index("tok")
    mdl_at = lax.axis_index("mdl")

    def own_cols(full_rows):
        return lax.dynamic_slice_in_dim(full_rows, mdl_at * local_width, local_width, axis=1)

    all_steps = lax.all_gather(jnp.stack([timesteps, labels]), "tok", axis=1, tiled=True)
    time_full = lax.all_gather(time_weight, "tok", axis=0, tiled=True)
    all_crops = all_steps.shape[1] * slot_count
    step_feats = timestep_features(all_steps[0].reshape(all_crops), time_full.shape[0])
    label_hot = (
        all_steps[1].reshape(all_crops)[:, None] == jnp.arange(class_table.shape[0], dtype=jnp.int32)[None, :]
    ).astype(bf16)
    embedding = exact_dot(step_feats, time_full.astype(f32)) + mm(label_hot, class_table, ((1,), (0,)))
    cond_full = gather_cols(jax.nn.silu(embedding).astype(bf16))
    cond_own = lax.dynamic_slice_in_dim(cond_full, tok_at * own_rows, own_rows, axis=1)
    ada_own = ada_weight.reshape(own_rows, 6 * local_width)
    modulation = lax.psum_scatter(
        mm(cond_own, ada_own, ((1,), (0,))), "tok", scatter_dimension=0, tiled=True
    ).reshape(slot_count, 6, local_width) + ada_bias.astype(f32)[None]
    mod_full = lax.all_gather(modulation, "mdl", axis=2, tiled=True)

    head_shard = jnp.concatenate([qkv_weight.reshape(own_rows, 3 * local_width), out_weight.T], axis=1)
    unit_shard = jnp.concatenate([up_weight, down_weight.T], axis=1)
    head_full = lax.all_gather(head_shard, "tok", axis=0, tiled=True)
    unit_full = lax.all_gather(unit_shard, "tok", axis=0, tiled=True)
    qkv_full, out_full = head_full[:, : 3 * local_width], head_full[:, 3 * local_width :]
    up_full, down_full = unit_full[:, :units_here], unit_full[:, units_here:]
    tokens_full = gather_cols(tokens)
    cot_full = gather_cols(cotangent)
    out_bias_full = lax.all_gather(out_bias, "mdl", axis=0, tiled=True).astype(f32)

    inside, segment = crop_layout(lengths, padding, row_len)
    crop_hot = inside[0].astype(bf16)
    crop_hot32 = inside[0].astype(f32)

    def spread(part):
        return exact_dot(crop_hot32, mod_full[:, part])

    head_tok = mm(crop_hot, head_mask[0].astype(bf16), ((1,), (0,)))
    head_units = jnp.repeat(head_tok, head_width, axis=1).astype(bf16)
    chan_tok = mm(crop_hot, chan_mask[0].astype(bf16), ((1,), (0,)))
    chan_units = jnp.repeat(chan_tok, units_here // groups_here, axis=1)
    keep_rows = keep_mask.astype(f32)[:, None]

    start_rows = tokens_full.astype(f32)
    normed_one, inverse_one = norm_rows(start_rows)
    modulated_one = (normed_one * (1.0 + spread(1)) + spread(0)).astype(bf16)
    projected = mm(modulated_one, qkv_full, ((1,), (0,)))
    qv_bias32 = qv_bias.astype(f32)
    queries = (projected[:, :local_width] + qv_bias32[0]).astype(bf16)
    key_rows = projected[:, local_width : 2 * local_width].astype(bf16)
    value_rows = (projected[:, 2 * local_width :] + qv_bias32[1]).astype(bf16)

    def heads(rows):
        return rows.reshape(row_len, heads_here, head_width)

    attend_now, logsum_rows = attend_row(
        heads(queries), heads(key_rows), heads(value_rows), segment[0], score_scale
    )
    attended = (attend_now.reshape(row_len, local_width) * head_units.astype(f32)).astype(bf16)
    branch_own = scatter_cols(mm(attended, out_full, ((1,), (1,))))
    attn_branch = gather_cols(branch_own).astype(f32) + out_bias_full
    gate_one = spread(2)
    middle = start_rows + gate_one * attn_branch
    normed_two, inverse_two = norm_rows(middle)
    scale_two = spread(4)
    modulated_two = (normed_two * (1.0 + scale_two) + spread(3)).astype(bf16)
    up_pre = mm(modulated_two, up_full, ((1,), (0,))) + up_bias.astype(f32)
    gelu_values, gelu_back = jax.vjp(lambda pre: jax.nn.gelu(pre, approximate=True), up_pre)
    hidden = (gelu_values * chan_units).astype(bf16)
    mlp_out = scatter_cols(mm(hidden, down_full, ((1,), (1,)))).astype(f32) + down_bias.astype(f32)
    gate_two = spread(5)
    output = (own_cols(middle) + own_cols(gate_two) * keep_rows * mlp_out).astype(bf16)

    grad_rows = cot_full.astype(f32)
    grad_mlp = (grad_rows * gate_two * keep_rows).astype(bf16)
    grad_hidden = mm(grad_mlp, down_full, ((1,), (0,)))
    grad_down = mm(grad_mlp, hidden, ((0,), (0,)))
    grad_down_bias = jnp.sum(own_cols(grad_mlp).astype(f32), axis=0)
    grad_up_pre = gelu_back(grad_hidden * chan_units)[0].astype(bf16)
    grad_up = mm(modulated_two, grad_up_pre, ((0,), (0,)))
    grad_up_bias = jnp.sum(grad_up_pre.astype(f32), axis=0)
    grad_units = lax.psum_scatter(
        jnp.concatenate([grad_up, grad_down], axis=1).astype(bf16), "tok", scatter_dimension=0, tiled=True
    ).astype(f32)
    two_own = scatter_cols(mm(grad_up_pre, up_full, ((1,), (1,))))
    grad_two = gather_cols(two_own).astype(f32)

    def norm_back(grad_norm, normed, inverse):
        return inverse * (
            grad_norm
            - jnp.mean(grad_norm, axis=1, keepdims=True)
            - normed * jnp.mean(grad_norm * normed, axis=1, keepdims=True)
        )

    grad_middle = grad_rows + norm_back(grad_two * (1.0 + scale_two), normed_two, inverse_two)
    grad_attn = (grad_middle * gate_one).astype(bf16)
    grad_out = mm(grad_attn, attended, ((0,), (0,)))
    grad_out_bias = jnp.sum(own_cols(grad_attn).astype(f32), axis=0)
    grad_att = mm(grad_attn, out_full, ((1,), (0,))).astype(bf16) * head_units
    query_grads, key_grads, value_grads = attend_back(
        heads(queries), heads(key_rows), heads(value_rows), segment[0], logsum_rows, heads(grad_att), score_scale
    )
    grad_qkv_rows = jnp.concatenate(
        [part.reshape(row_len, local_width).astype(bf16) for part in (query_grads, key_grads, value_grads)], axis=1
    )
    grad_qkv = mm(modulated_one, grad_qkv_rows, ((0,), (0,)))
    grad_bias_rows = jnp.sum(grad_qkv_rows.astype(f32), axis=0)
    grad_qv_bias = jnp.stack([grad_bias_rows[:local_width], grad_bias_rows[2 * local_width :]], axis=0)
    grad_heads = lax.psum_scatter(
        jnp.concatenate([grad_qkv, grad_out], axis=1).astype(bf16), "tok", scatter_dimension=0, tiled=True
    ).astype(f32)
    grad_one = scatter_cols(mm(grad_qkv_rows, qkv_full, ((1,), (1,)))).astype(f32)
    normed_one_own = own_cols(normed_one)
    grad_norm = grad_one * (1.0 + own_cols(spread(1)))
    totals = lax.psum(
        jnp.stack([jnp.sum(grad_norm, axis=1), jnp.sum(grad_norm * normed_one_own, axis=1)]), "mdl"
    )
    grad_middle_own = own_cols(grad_middle)
    grad_tokens = grad_middle_own + inverse_one * (
        grad_norm - totals[0][:, None] / full_width - normed_one_own * totals[1][:, None] / full_width
    )
    two_own32 = two_own.astype(f32)
    grad_per_token = jnp.concatenate(
        [
            grad_one,
            grad_one * normed_one_own,
            grad_middle_own * own_cols(attn_branch),
            two_own32,
            two_own32 * own_cols(normed_two),
            cotangent.astype(f32) * keep_rows * mlp_out,
        ],
        axis=1,
    )
    grad_mod_own = lax.dot_general(
        crop_hot32, grad_per_token, (((0,), (0,)), ((), ())), precision=lax.Precision.HIGHEST, preferred_element_type=f32
    )
    grad_mod = lax.all_gather(grad_mod_own, "tok", axis=0, tiled=True)
    grad_ada_bias = jnp.sum(grad_mod.reshape(all_crops, 6, local_width), axis=0)
    grad_ada = lax.dot_general(
        cond_own.astype(f32), grad_mod, (((0,), (0,)), ((), ())), precision=lax.Precision.HIGHEST, preferred_element_type=f32
    ).reshape(own_rows, 6, local_width)
    cond_part = lax.dot_general(
        grad_mod, ada_own.astype(f32), (((1,), (1,)), ((), ())), precision=lax.Precision.HIGHEST, preferred_element_type=f32
    )
    grad_cond = lax.all_gather(lax.psum(cond_part, "mdl"), "tok", axis=1, tiled=True)
    silu_values, silu_back = jax.vjp(jax.nn.silu, embedding)
    grad_embed = silu_back(own_cols(grad_cond))[0]
    freq_rows = time_weight.shape[0]
    own_feats = lax.dynamic_slice_in_dim(step_feats, tok_at * freq_rows, freq_rows, axis=1)
    grad_time = exact_dot(own_feats.T, grad_embed)
    grad_class = exact_dot(label_hot.astype(f32).T, grad_embed)
    grad_qv_bias, grad_out_bias, grad_up_bias, grad_down_bias = lax.psum(
        (grad_qv_bias, grad_out_bias, grad_up_bias, grad_down_bias), "tok"
    )
    return (
        output,
        grad_tokens,
        grad_heads[:, : 3 * local_width].reshape(own_rows, 3, local_width),
        grad_qv_bias,
        grad_heads[:, 3 * local_width :].T,
        grad_out_bias,
        grad_units[:, :units_here],
        grad_up_bias,
        grad_units[:, units_here:].T,
        grad_down_bias,
        grad_ada,
        grad_ada_bias,
        grad_time,
        grad_class,
    )


def solution(mesh):
    return jax.shard_map(
        on_device,
        mesh=mesh,
        in_specs=(
            P("tok", "mdl"),
            P("tok", "mdl"),
            P("tok", None),
            P("tok", None),
            P("tok", None),
            P("tok", None),
            P("tok", None, "mdl"),
            P("tok", None, "mdl"),
            P("tok"),
            P("tok", None, "mdl"),
            P(None, "mdl"),
            P("mdl", "tok"),
            P("mdl"),
            P("tok", "mdl"),
            P("mdl"),
            P("mdl", "tok"),
            P("mdl"),
            P("tok", None, "mdl"),
            P(None, "mdl"),
            P("tok", "mdl"),
            P(None, "mdl"),
        ),
        out_specs=(
            P("tok", "mdl"),
            P("tok", "mdl"),
            P("tok", None, "mdl"),
            P(None, "mdl"),
            P("mdl", "tok"),
            P("mdl"),
            P("tok", "mdl"),
            P("mdl"),
            P("mdl", "tok"),
            P("mdl"),
            P("tok", None, "mdl"),
            P(None, "mdl"),
            P("tok", "mdl"),
            P(None, "mdl"),
        ),
        check_vma=False,
    )
```

time: 1920 us -> 873 us (0.45)
  waiting for transfers between devices: 1300 us -> 247 us
  local copies, waits for them, and re-layouts: 33.3 us -> 87 us
  matrix products: 233 us -> 191 us
  blocking collectives: 254 us -> 229 us
    reduce_scatter x12 -> x4, waiting for transfers between devices: 766 us -> 130 us  [scatter_cols(): lax.psum_scatter(partial_rows.astype(bf16), 'mdl', scatter_dimension=1, t...]
    all_gather x14 -> x6, waiting for transfers between devices: 444 us -> 98.5 us  [the longest x1 69.8 us: on_device(): unit_full = lax.all_gather(unit_shard, 'tok', axis=0, tiled=True)]
    psum x1 -> x0, waiting for transfers between devices: 83.4 us -> none  [on_device(): lax.psum((grad_class, grad_qv_bias, grad_out_bias, grad_up_bias, grad_dow...]
    dot_general x32 -> x24, matrix products: 204 us -> 142 us  [the longest x16 70.4 us: mm(): lax.dot_general(left, right, (dims, ((), ())), preferred_element_type=f32)]
    psum x7 -> x2, blocking collectives: 105 us -> 49.4 us  [the longest x1 38.5 us: on_device(): lax.psum((grad_qv_bias, grad_out_bias, grad_up_bias, grad_down_bias), 'tok')]
    unnamed x152 -> x165, local copies, waits for them, and re-layouts: 18.8 us -> 58.2 us
    dot_general x9, matrix products: 12.4 us -> 41.8 us  [exact_dot(): jnp.dot(left, right, precision=lax.Precision.HIGHEST, preferred_element_t...]
    unnamed x0 -> x2, blocking collectives: none -> 27.6 us
  transfers between devices with their start and end apart: 28 -> 14, of which waited for: 27 -> 9; matrix products, arithmetic and copies ran while one was open for 7% -> 33% of each run, Pallas kernels for 0% -> 0%
where the time goes in v1:
time: 873 us; the launch traced here: 864 us
  waiting for transfers between devices  247 us (28%)
  blocking collectives  229 us (26%)
  matrix products  191 us (22%)
  other arithmetic  89.5 us (10%)
  local copies, waits for them, and re-layouts  87 us (10%)
  between operations  17.2 us (2%)
    reduce_scatter x4, waiting for transfers between devices, scatter_cols(): lax.psum_scatter(partial_rows.astype(bf16), 'mdl', scatter_dimension=1, t...  130 us
    dot_general x16, matrix products, mm(): lax.dot_general(left, right, (dims, ((), ())), preferred_element_type=f32)  70.4 us
    all_gather x1, waiting for transfers between devices, on_device(): unit_full = lax.all_gather(unit_shard, 'tok', axis=0, tiled=True)  69.8 us
    unnamed x165, local copies, waits for them, and re-layouts  58.2 us
    dot_general x9, matrix products, exact_dot(): jnp.dot(left, right, precision=lax.Precision.HIGHEST, preferred_element_t...  41.8 us
    psum x1, blocking collectives, on_device(): lax.psum((grad_qv_bias, grad_out_bias, grad_up_bias, grad_down_bias), 'tok')  38.5 us
    all_gather x1, blocking collectives, on_device(): lax.all_gather(lax.psum(cond_part, 'mdl'), 'tok', axis=1, tiled=True)  31.4 us
    all_gather x1, blocking collectives, on_device(): grad_mod = lax.all_gather(grad_mod_own, 'tok', axis=0, tiled=True)  31.3 us
  transfers between devices with their start and end apart: 14, of which 9 were waited for; matrix products, arithmetic and copies ran while one was open for 33% of the time, Pallas kernels for 0%

profile of v1, /device:TPU:0, one launch (start us, length us, event | category | flops | bytes accessed | tf_op | source)
XLA Modules:
  0.0 864.2 jit_solution(15546386648886690877)
XLA Ops:
  8.7 22.2 %all_gather.40 = s32[2,8,6]{2,0,1:T(2,128)S(1)} all-gather(s32[2,1,6]{2,0,1:T(2,128)S(1)} %bitcast.163), channel_id=1, replica_groups=mesh['tok'=8,'mdl'=4] {'tok'}, dimensions={1}, use_global_device_ids=true | all-gather | bytes 432 | tf_op jit(solution)/shard_map/all_gather | solution.py:121
  31.2 30.9 %all_gather.41 = bf16[256,288]{1,0:T(8,128)(2,1)S(1)} all-gather(bf16[32,288]{1,0:T(8,128)(2,1)} %param.40), channel_id=1, replica_groups=mesh['tok'=8,'mdl'=4] {'tok'}, dimensions={0}, use_global_device_ids=true | all-gather | bytes 165888 | tf_op jit(solution)/shard_map/all_gather | solution.py:122
  71.4 21.8 %fusion = f32[8,1728]{1,0:T(8,128)S(1)} fusion(f32[48,1728]{1,0:T(8,128)S(1)} %fusion.71), kind=kCustom, calls=%all-reduce-scatter | all-reduce-scatter fusion | flops 110593 | bytes 387584
  103.8 30.5 %all_gather.43 = f32[6,6,1152]{1,0,2:T(8,128)} all-gather(f32[6,6,288]{1,0,2:T(8,128)S(1)} %broadcast_add_fusion), channel_id=1, replica_groups=mesh['tok'=8,'mdl'=4] {'mdl'}, dimensions={2}, use_global_device_ids=true | all-gather | bytes 207360 | tf_op jit(solution)/shard_map/all_gather | solution.py:135
  134.2 22.1 %fusion.98 = (f32[6,1,1152]{1,0,2:T(8,128)}, f32[6,1,1152]{1,0,2:T(8,128)}, f32[6,1,1152]{1,0,2:T(8,128)}, f32[6,1,1152]{1,0,2:T(8,128)}, f32[6,1,1152]{1,0,2:T(8,128)}, /*index=5*/f32[6,1,1152]{1,0,2:T(8,128)}) fusion(f32[6,6,1152]{1,0,2:T(8,128)} %all_gather.43), kind=kLoop, calls=%fused_computation.186 | loop fusion | bytes 331776 | tf_op jit(solution)/shard_map/slice | solution.py:152
  171.0 7.6 fusion.8
  186.7 11.6 %fusion.100 = (f32[4,1280]{1,0:T(4,128)S(1)}, f32[4,1280,1280]{1,2,0:T(8,128)}) fusion(bf16[1280,4,72]{0,2,1:T(8,128)(2,1)S(1)} %bitcast.145, bf16[1280,4,72]{0,2,1:T(8,128)(2,1)S(1)} %bitcast.151, pred[1280,1280]{0,1:T(8,128)(4,1)S(1)} %copy-done.29), kind=kOutput, calls=%fused_computation.188 | convolution fusion | flops 963374080 | bytes 29347840 | tf_op jit(solution)/shard_map/qhd,khd->hqk/dot_general | solution.py:57
  198.3 10.6 %fusion.2 = f32[4,1280]{1,0:T(4,128)S(1)} fusion(f32[4,1280,1280]{1,2,0:T(8,128)} %get-tuple-element.129, f32[4,1280]{1,0:T(4,128)S(1)} %get-tuple-element.128), kind=kLoop, calls=%fused_computation.7 | loop fusion | flops 13102080 | bytes 26255360 | tf_op jit(solution)/shard_map/reduce_sum | solution.py:62
  208.9 11.0 %fusion.7 = f32[4,72,1280]{2,1,0:T(8,128)S(1)} fusion(bf16[1280,4,72]{0,2,1:T(8,128)(2,1)S(1)} %bitcast.143, f32[4,1280,1280]{1,2,0:T(8,128)} %get-tuple-element.129, f32[4,1280]{1,0:T(4,128)S(1)} %fusion.2, f32[4,1280]{1,0:T(4,128)S(1)} %get-tuple-element.128), kind=kOutput, calls=%fused_computation.11 | convolution fusion | flops 963379200 | bytes 28467200 | tf_op jit(solution)/shard_map/hqk,khd->qhd/dot_general | solution.py:64
  224.9 34.0 %reduce-scatter.13.cloned.1.call-done = bf16[1280,288]{0,1:T(8,128)(2,1)} async-done(((bf16[1280,1152]{0,1:T(8,128)(2,1)}), bf16[1280,288]{0,1:T(8,128)(2,1)}) %reduce-scatter.13.cloned.1.call-update) | async-done | bytes 737296 | tf_op jit(solution)/shard_map/reduce_scatter | solution.py:53
  287.8 8.2 fusion.11
  295.9 20.8 %all-gather.14.cloned.1.call-done = bf16[1280,1152]{0,1:T(8,128)(2,1)} async-done(((bf16[1280,288]{0,1:T(8,128)(2,1)}), bf16[1280,1152]{0,1:T(8,128)(2,1)}) %all-gather.14.cloned.1.call-update) | async-done | bytes 2949136 | tf_op jit(solution)/shard_map/all_gather | solution.py:49
  316.8 10.0 %fusion.97 = (f32[1280]{0:T(1024)S(1)}, f32[1280]{0:T(1024)S(1)}, f32[1280,1152]{0,1:T(8,128)S(1)}, f32[1280,1152]{0,1:T(8,128)}, f32[1280,1152]{0,1:T(8,128)}, /*index=5*/f32[1280,1152]{0,1:T(8,128)}) fusion(f32[1152]{0:T(1024)S(1)} %convert_element_type.204, bf16[1280,1152]{0,1:T(8,128)(2,1)} %all-gather.14.cloned.1.call-done, ...), kind=kOutput, calls=%fused_computation.185 | convolution fusion | flops 120934400 | bytes 29543984 | tf_op jit(solution)/shard_map/dot_general | solution.py:15
  337.0 69.8 %all-gather.16.cloned.1.call-done = bf16[1152,2304]{1,0:T(8,128)(2,1)} async-done(((bf16[144,2304]{1,0:T(8,128)(2,1)}), bf16[1152,2304]{1,0:T(8,128)(2,1)}) %all-gather.16.cloned.1.call-update) | async-done | bytes 5308432 | tf_op jit(solution)/shard_map/all_gather | solution.py:140
  406.7 9.1 %fusion.19 = (bf16[1280,1152]{0,1:T(8,128)(2,1)}, f32[1280,1152]{0,1:T(8,128)S(1)}) fusion(f32[1280,4]{0,1:T(4,128)S(1)} %fusion.80, f32[1152]{0:T(1024)S(1)} %convert_element_type.207, bf16[1280,1152]{0,1:T(8,128)(2,1)S(1)} %fusion.9, bf16[1152,2304]{1,0:T(8,128)(2,1)} %all-gather.16.cloned.1.call-done), kind=kOutput, calls=%fused_computation.43 | convolution fusion | flops 3413606400 | bytes 14475776 | tf_op jit(solution)/shard_map/dot_general | solution.py:19
  417.6 8.6 convert_reduce_fusion.1
  433.2 35.0 %reduce-scatter.17.cloned.1.call-done = bf16[1280,288]{0,1:T(8,128)(2,1)} async-done(((bf16[1280,1152]{0,1:T(8,128)(2,1)}), bf16[1280,288]{0,1:T(8,128)(2,1)}) %reduce-scatter.17.cloned.1.call-update) | async-done | bytes 737296 | tf_op jit(solution)/shard_map/reduce_scatter | solution.py:53
  481.5 8.6 copy.148
  504.1 10.7 %multiply_convert_fusion.1 = (bf16[1280,1152]{0,1:T(8,128)(2,1)S(1)}, f32[1280,1152]{0,1:T(8,128)}) fusion(f32[1280,1152]{0,1:T(8,128)} %get-tuple-element.130, f32[1280]{0:T(1024)S(1)} %get-tuple-element.139, f32[1280]{0:T(1024)S(1)} %get-tuple-element.140, f32[1280,1152]{0,1:T(8,128)} %convolution_add_fusion.1, bf16[1280,1152]{0,1:T(8,128)(2,1)S(1)} %copy-done.6, ...), kind=kLoop, calls=%fused_computation.47 | loop fusion | flops 17694720 | bytes 32460800 | tf_op jit(solution)/shard_map/convert_element_type | solution.py:212
  519.6 17.1 %multiply_reduce_fusion = (f32[4,1280]{1,0:T(4,128)S(1)}, f32[4,1280,1280]{1,2,0:T(8,128)}) fusion(f32[4,1280,1280]{1,2,0:T(8,128)} %get-tuple-element.129, f32[4,1280]{1,0:T(4,128)S(1)} %log_add_fusion, bf16[1280,4,72]{0,2,1:T(8,128)(2,1)S(1)} %bitcast.141, bf16[1280,4,72]{0,2,1:T(8,128)(2,1)S(1)} %bitcast.144), kind=kOutput, calls=%fused_computation.3 | convolution fusion | flops 963374080 | bytes 53944320 | tf_op jit(solution)/shard_map/qhd,khd->hqk/dot_general | solution.py:73
  536.7 22.8 %multiply_convert_fusion = bf16[4,1280,1280]{1,2,0:T(8,128)(2,1)} fusion(f32[4,1280,1280]{1,2,0:T(8,128)} %get-tuple-element.134, f32[4,1280,1280]{1,2,0:T(8,128)} %get-tuple-element.129, f32[4,1280]{1,0:T(4,128)S(1)} %get-tuple-element.133, f32[4,1280]{1,0:T(4,128)S(1)} %log_add_fusion), kind=kLoop, calls=%fused_computation.2 | loop fusion | flops 26214400 | bytes 65576960 | tf_op jit(solution)/shard_map/convert_element_type | solution.py:75
  559.5 9.1 %fusion.23 = bf16[4,72,1280]{2,1,0:T(8,128)(2,1)S(1)} fusion(bf16[1280,4,72]{0,2,1:T(8,128)(2,1)S(1)} %bitcast.146, bf16[4,1280,1280]{1,2,0:T(8,128)(2,1)} %multiply_convert_fusion), kind=kOutput, calls=%fused_computation.61 | convolution fusion | flops 944455680 | bytes 14581760 | tf_op jit(solution)/shard_map/hqk,qhd->khd/dot_general | solution.py:77
  576.1 11.8 %fusion.24 = bf16[4,72,1280]{2,1,0:T(8,128)(2,1)S(1)} fusion(bf16[1280,4,72]{0,2,1:T(8,128)(2,1)S(1)} %bitcast.142, f32[4,1280,1280]{1,2,0:T(8,128)} %get-tuple-element.129, f32[4,1280]{1,0:T(4,128)S(1)} %log_add_fusion), kind=kOutput, calls=%fused_computation.62 | convolution fusion | flops 957194240 | bytes 27709440 | tf_op jit(solution)/shard_map/hqk,qhd->khd/dot_general | solution.py:78
  605.9 8.3 convolution_convert_fusion.1
  617.4 38.5 %all-reduce.3 = (f32[2,288]{1,0:T(2,128)}, f32[288]{0:T(512)}, f32[1152]{0:T(1024)}, f32[288]{0:T(512)}) all-reduce(f32[2,288]{1,0:T(2,128)S(1)} %pad_maximum_fusion.8, f32[288]{0:T(512)S(1)} %convert_reduce_fusion.4, f32[1152]{0:T(1024)S(1)} %get-tuple-element.137, ...), channel_id=1, replica_groups=mesh['tok'=8,'mdl'=4] {'tok'}, use_global_device_ids=true, to_apply=%region_21.22 | all-reduce | flops 2304 | bytes 18432 | tf_op jit(solution)/shard_map/psum | solution.py:268
  662.8 17.0 %reduce-scatter.21.cloned.1.call-done = bf16[144,1152]{1,0:T(8,128)(2,1)} async-done(((bf16[1152,1152]{1,0:T(8,128)(2,1)}), bf16[144,1152]{1,0:T(8,128)(2,1)}) %reduce-scatter.21.cloned.1.call-update) | async-done | bytes 331792
  683.1 35.0 %reduce-scatter.19.cloned.1.call-done = bf16[1280,288]{0,1:T(8,128)(2,1)} async-done(((bf16[1280,1152]{0,1:T(8,128)(2,1)}), bf16[1280,288]{0,1:T(8,128)(2,1)}) %reduce-scatter.19.cloned.1.call-update) | async-done | bytes 737296 | tf_op jit(solution)/shard_map/reduce_scatter | solution.py:53
  731.4 26.0 %reduce-scatter.15.cloned.1.call-done = bf16[1280,288]{0,1:T(8,128)(2,1)} async-done(((bf16[1280,1152]{0,1:T(8,128)(2,1)}), bf16[1280,288]{0,1:T(8,128)(2,1)}) %reduce-scatter.15.cloned.1.call-update) | async-done | bytes 737296 | tf_op jit(solution)/shard_map/reduce_scatter | solution.py:53
  761.3 7.7 convolution_bitcast_fusion
  769.1 31.3 %all-gather.1 = f32[8,6,1728]{2,1,0:T(8,128)S(1)} all-gather(f32[1,6,1728]{2,1,0:T(8,128)S(1)} %convolution_bitcast_fusion), channel_id=1, replica_groups=mesh['tok'=8,'mdl'=4] {'tok'}, dimensions={0}, use_global_device_ids=true | all-gather | bytes 373248 | tf_op jit(solution)/shard_map/all_gather | solution.py:253
  804.2 10.9 %all-reduce.4 = (f32[2,1280]{1,0:T(2,128)S(1)}, f32[48,144]{1,0:T(8,128)S(1)}) all-reduce(f32[2,1280]{1,0:T(2,128)S(1)} %pad_maximum_fusion.7, f32[48,144]{1,0:T(8,128)S(1)} %fusion.101), channel_id=1, replica_groups=mesh['tok'=8,'mdl'=4] {'mdl'}, use_global_device_ids=true, to_apply=%region_18.19 | all-reduce | flops 9472 | bytes 75776 | tf_op jit(solution)/shard_map/psum | solution.py:231
  815.2 31.4 %all-gather.2 = f32[8,144,48]{1,2,0:T(8,128)S(1)} all-gather(f32[1,144,48]{1,2,0:T(8,128)S(1)} %bitcast.162), channel_id=1, replica_groups=mesh['tok'=8,'mdl'=4] {'tok'}, dimensions={0}, use_global_device_ids=true | all-gather | bytes 248832 | tf_op jit(solution)/shard_map/all_gather | solution.py:261
  (291 shorter events, 196.9 us)
Async XLA Ops:
  7.2 55.3 %copy-start = (bf16[1000,288]{0,1:T(8,128)(2,1)S(1)}, bf16[1000,288]{0,1:T(8,128)(2,1)}, u32[]{:S(2)}) copy-start(bf16[1000,288]{0,1:T(8,128)(2,1)} %param.41) | copy-start | bytes 1728004
  7.2 89.4 %copy-start.36 = (bf16[144,3,288]{2,0,1:T(8,128)(2,1)S(1)}, bf16[144,3,288]{2,0,1:T(8,128)(2,1)}, u32[]{:S(2)}) copy-start(bf16[144,3,288]{2,0,1:T(8,128)(2,1)} %param.30) | copy-start | bytes 746500
  7.2 89.8 %copy-start.41 = (bf16[288,144]{0,1:T(8,128)(2,1)S(1)}, bf16[288,144]{0,1:T(8,128)(2,1)}, u32[]{:S(2)}) copy-start(bf16[288,144]{0,1:T(8,128)(2,1)} %param.32) | copy-start | bytes 248836
  7.2 161.0 %all-gather.10.cloned.1.call-start = ((), (), s32[]{:S(2)}) async-start(), calls=%async_computation.6 | async-start | bytes 3686400 | tf_op jit(solution)/shard_map/all_gather | solution.py:49
  8.0 90.0 %copy-start.61 = (s32[1,6]{1,0:T(1,128)S(1)}, s32[1,6]{1,0:T(1,128)}, u32[]{:S(2)}) copy-start(s32[1,6]{1,0:T(1,128)} %param.23) | copy-start | bytes 76
  8.0 90.0 %copy-start.66 = (s32[1,6]{1,0:T(1,128)S(1)}, s32[1,6]{1,0:T(1,128)}, u32[]{:S(2)}) copy-start(s32[1,6]{1,0:T(1,128)} %param.24) | copy-start | bytes 76
  8.0 90.2 %copy-start.58 = (bf16[2,288]{1,0:T(2,128)(2,1)S(1)}, bf16[2,288]{1,0:T(2,128)(2,1)}, u32[]{:S(2)}) copy-start(bf16[2,288]{1,0:T(2,128)(2,1)} %param.31) | copy-start | bytes 3460
  8.0 90.3 %copy-start.64 = (s32[1,6,4]{1,2,0:T(4,128)S(1)}, s32[1,6,4]{1,2,0:T(4,128)}, u32[]{:S(2)}) copy-start(s32[1,6,4]{1,2,0:T(4,128)} %param.27) | copy-start | bytes 292
  8.0 170.7 %all-gather.12.cloned.1.call-start = ((), (), s32[]{:S(2)}) async-start(), calls=%async_computation.7 | async-start | bytes 2985984 | tf_op jit(solution)/shard_map/all_gather | solution.py:139
  93.3 9.4 %collective-permute-start = (f32[8,1728]{1,0:T(8,128)S(1)}, f32[8,1728]{1,0:T(8,128)S(1)}, u32[]{:S(2)}, u32[]{:S(2)}) collective-permute-start(f32[8,1728]{1,0:T(8,128)S(1)} %fusion), channel_id=1, source_target_pairs={{0,4},{4,8},{8,12},{12,16},{16,20},{20,24},{24,28},{1,5},{5,9},{9,... | collective-permute-start | bytes 165896
  95.3 7.5 collective-permute-start.1
  97.9 161.0 %reduce-scatter.13.cloned.1.call-start = ((), (), s32[]{:S(2)}) async-start(), calls=%async_computation.8 | async-start | bytes 3686400 | tf_op jit(solution)/shard_map/reduce_scatter | solution.py:53
  98.2 229.2 %copy-start.48 = (s32[6]{0:T(128)}, s32[6]{0:T(128)S(1)}, u32[]{:S(2)}) copy-start(s32[6]{0:T(128)S(1)} %get-tuple-element.124) | copy-start | bytes 76
  98.2 229.2 %copy-start.50 = (s32[6]{0:T(128)}, s32[6]{0:T(128)S(1)}, u32[]{:S(2)}) copy-start(s32[6]{0:T(128)S(1)} %get-tuple-element.125) | copy-start | bytes 76
  171.0 145.8 %copy-start.39 = (f32[1280]{0:T(1024)}, f32[1280]{0:T(1024)S(1)}, u32[]{:S(2)}) copy-start(f32[1280]{0:T(1024)S(1)} %get-tuple-element.121) | copy-start | bytes 15364
  224.2 43.9 %copy-start.53 = (s32[1280]{0:T(1024)S(1)}, s32[1280]{0:T(1024)}, u32[]{:S(2)}) copy-start(s32[1280]{0:T(1024)} %param.29) | copy-start | bytes 15364
  224.2 43.9 %copy-start.57 = (bf16[1152]{0:T(1024)(128)(2,1)S(1)}, bf16[1152]{0:T(1024)(128)(2,1)}, u32[]{:S(2)}) copy-start(bf16[1152]{0:T(1024)(128)(2,1)} %param.35) | copy-start | bytes 6916
  224.2 44.0 %copy-start.65 = (s32[1,6,4]{1,2,0:T(4,128)S(1)}, s32[1,6,4]{1,2,0:T(4,128)}, u32[]{:S(2)}) copy-start(s32[1,6,4]{1,2,0:T(4,128)} %param.28) | copy-start | bytes 292
  224.3 63.5 %all-gather.18.cloned.1.call-start = ((), (), s32[]{:S(2)}) async-start(), calls=%async_computation.12 | async-start | bytes 3686400 | tf_op jit(solution)/shard_map/all_gather | solution.py:49
  224.8 91.9 %all-gather.14.cloned.1.call-start = ((), (), s32[]{:S(2)}) async-start(), calls=%async_computation.9 | async-start | bytes 3686400 | tf_op jit(solution)/shard_map/all_gather | solution.py:49
  258.9 147.8 %all-gather.16.cloned.1.call-start = ((), (), s32[]{:S(2)}) async-start(), calls=%async_computation.10 | async-start | bytes 5971968 | tf_op jit(solution)/shard_map/all_gather | solution.py:140
  260.8 207.4 %reduce-scatter.17.cloned.1.call-start = ((), (), s32[]{:S(2)}) async-start(), calls=%async_computation.13 | async-start | bytes 3686400 | tf_op jit(solution)/shard_map/reduce_scatter | solution.py:53
  433.2 64.1 %all-gather.20.cloned.1.call-start = ((), (), s32[]{:S(2)}) async-start(), calls=%async_computation.14 | async-start | bytes 3686400 | tf_op jit(solution)/shard_map/all_gather | solution.py:49
  468.3 187.5 %reduce-scatter.23.cloned.1.call-start = ((), (), s32[]{:S(2)}) async-start(), calls=%async_computation.17 | async-start | bytes 5971968
  490.1 189.6 %reduce-scatter.21.cloned.1.call-start = ((), (), s32[]{:S(2)}) async-start(), calls=%async_computation.16 | async-start | bytes 2985984
  598.7 119.5 %reduce-scatter.19.cloned.1.call-start = ((), (), s32[]{:S(2)}) async-start(), calls=%async_computation.15 | async-start | bytes 3686400 | tf_op jit(solution)/shard_map/reduce_scatter | solution.py:53
  605.8 151.6 %reduce-scatter.15.cloned.1.call-start = ((), (), s32[]{:S(2)}) async-start(), calls=%async_computation.11 | async-start | bytes 3686400 | tf_op jit(solution)/shard_map/reduce_scatter | solution.py:53
  761.3 39.1 %copy-start.11 = (bf16[144,1728]{1,0:T(8,128)(2,1)S(1)}, bf16[144,1728]{1,0:T(8,128)(2,1)}, u32[]{:S(2)}) copy-start(bf16[144,1728]{1,0:T(8,128)(2,1)} %copy-done.10) | copy-start | bytes 1492996
  769.0 78.0 %copy-start.34 = (f32[48,288]{1,0:T(8,128)S(1)}, f32[48,288]{1,0:T(8,128)}, u32[]{:S(2)}) copy-start(f32[48,288]{1,0:T(8,128)} %copy-done.33) | copy-start | bytes 165892
  769.0 78.0 %copy-start.56 = (s32[48]{0:T(128)S(1)}, s32[48]{0:T(128)}, u32[]{:S(2)}) copy-start(s32[48]{0:T(128)} %copy-done.55) | copy-start | bytes 580
  769.0 79.8 %copy-start.43 = (f32[48,128]{1,0:T(8,128)S(1)}, f32[48,128]{1,0:T(8,128)}, u32[]{:S(2)}) copy-start(f32[48,128]{1,0:T(8,128)} %copy-done.42) | copy-start | bytes 73732
  769.1 79.8 %copy-start.45 = (f32[48,128]{1,0:T(8,128)S(1)}, f32[48,128]{1,0:T(8,128)}, u32[]{:S(2)}) copy-start(f32[48,128]{1,0:T(8,128)} %copy-done.44) | copy-start | bytes 73732
  (51 other events, 806.6 us)
Sparse Core Ops, SparseCore 0:
  9.6 30.1 all-gather.9
  98.0 53.6 all-gather.11
  224.4 34.4 reduce-scatter.12
  260.3 27.4 all-gather.17
  289.3 27.4 all-gather.13
  319.6 87.0 all-gather.15
  433.3 34.8 reduce-scatter.16
  469.8 27.4 all-gather.19
  500.9 104.1 reduce-scatter.22
  609.1 70.6 reduce-scatter.20
  682.3 35.7 reduce-scatter.18
  720.7 36.6 reduce-scatter.14

commit v2 on v1

--- a/solution.py
+++ b/solution.py
@@ -3,6 +3,8 @@
 import jax
 import jax.numpy as jnp
 from jax import lax
+from jax.experimental import pallas as pl
+from jax.experimental.pallas import tpu as pltpu
 from jax.sharding import PartitionSpec as P
 
 norm_floor = 1e-06
@@ -77,6 +79,465 @@
     grad_keys = jnp.einsum("hqk,qhd->khd", grad_scores, queries, preferred_element_type=f32) * score_scale
     grad_values = jnp.einsum("hqk,qhd->khd", prob_full.astype(bf16), grad_att, preferred_element_type=f32)
     return (grad_queries, grad_keys, grad_values)
+
+
+def peer(tok=None, mdl=None):
+    where = {}
+    if tok is not None:
+        where["tok"] = tok
+    if mdl is not None:
+        where["mdl"] = mdl
+    return where
+
+
+def remote(src, dst, send_sem, recv_sem, where):
+    return pltpu.make_async_remote_copy(
+        src_ref=src, dst_ref=dst, send_sem=send_sem, recv_sem=recv_sem, device_id=where, device_id_type=pl.DeviceIdType.MESH
+    )
+
+
+def greet(tok_at, mdl_at, tok_count, mdl_count):
+    barrier = pltpu.get_barrier_semaphore()
+    for step in range(1, tok_count):
+        pl.semaphore_signal(
+            barrier, inc=1, device_id=peer(tok=lax.rem(tok_at + step, tok_count)), device_id_type=pl.DeviceIdType.MESH
+        )
+    for step in range(1, mdl_count):
+        pl.semaphore_signal(
+            barrier, inc=1, device_id=peer(mdl=lax.rem(mdl_at + step, mdl_count)), device_id_type=pl.DeviceIdType.MESH
+        )
+    pl.semaphore_wait(barrier, tok_count + mdl_count - 2)
+
+
+def split_two(values):
+    high = values.astype(bf16)
+    return high, (values - high.astype(f32)).astype(bf16)
+
+
+def split_three(values):
+    high, rest = split_two(values)
+    return high, rest, (values - high.astype(f32) - rest.astype(f32)).astype(bf16)
+
+
+class AllToPeers:
+    def __init__(self, axis, me, count, send_sems, recv_sems):
+        self.axis, self.me, self.count, self.send_sems, self.recv_sems = axis, me, count, send_sems, recv_sems
+
+    def copies(self, source, slots):
+        for step in range(1, self.count):
+            other = lax.rem(self.me + step, self.count)
+            yield remote(
+                source(other), slots.at[self.me], self.send_sems.at[step], self.recv_sems.at[self.me], peer(**{self.axis: other})
+            )
+
+    def start(self, source, slots):
+        for copy in self.copies(source, slots):
+            copy.start()
+
+    def wait_recv(self, source, slots):
+        for step in range(1, self.count):
+            other = lax.rem(self.me + step, self.count)
+            remote(
+                source(other), slots.at[other], self.send_sems.at[step], self.recv_sems.at[other], peer(**{self.axis: other})
+            ).wait_recv()
+
+    def wait_send(self, source, slots):
+        for copy in self.copies(source, slots):
+            copy.wait_send()
+
+
+class LineGather:
+    def __init__(self, tok_at, shard, full, rows, up_sems, down_sems, cross_sems, recv_sems):
+        self.tok_at, self.shard, self.full, self.rows = tok_at, shard, full, rows
+        self.sems = (up_sems, down_sems, cross_sems)
+        self.recv_sems = recv_sems
+        self.line = lax.div(tok_at, 2)
+        self.side = lax.rem(tok_at, 2)
+        self.across = tok_at + 1 - 2 * self.side
+
+    def slot(self, owner):
+        return self.full.at[pl.ds(pl.multiple_of(owner * self.rows, 16), self.rows), :]
+
+    def copy(self, kind, owner, own=False):
+        target = (self.tok_at + 2, self.tok_at - 2, self.across)[kind]
+        source = self.shard if own else self.slot(owner)
+        return remote(source, self.slot(owner), self.sems[kind].at[owner], self.recv_sems.at[owner], peer(tok=target))
+
+    def each_send(self, step, act):
+        if step == 0:
+            pl.when(self.line < 3)(lambda: act(self.copy(0, self.tok_at, True)))
+            pl.when(self.line > 0)(lambda: act(self.copy(1, self.tok_at, True)))
+            act(self.copy(2, self.tok_at, True))
+        else:
+            below = self.tok_at - 2 * step
+            above = self.tok_at + 2 * step
+            pl.when((self.line >= step) & (self.line < 3))(lambda: act(self.copy(0, below)))
+            pl.when((self.line + step <= 3) & (self.line > 0))(lambda: act(self.copy(1, above)))
+            pl.when(self.line >= step)(lambda: act(self.copy(2, below)))
+            pl.when(self.line + step <= 3)(lambda: act(self.copy(2, above)))
+
+    def start(self):
+        self.each_send(0, lambda copy: copy.start())
+
+    def arrive(self, owner):
+        self.copy(2, owner).wait_recv()
+
+    def forward(self, step):
+        pl.when(self.line >= step)(lambda: self.arrive(self.tok_at - 2 * step))
+        pl.when(self.line + step <= 3)(lambda: self.arrive(self.tok_at + 2 * step))
+        self.each_send(step, lambda copy: copy.start())
+
+    def arrive_across(self):
+        for place in range(4):
+            self.arrive(2 * place + 1 - self.side)
+
+    def wait_send(self):
+        for step in range(4):
+            self.each_send(step, lambda copy: copy.wait_send())
+
+
+class QuadGather:
+    def __init__(self, mdl_at, own, blocks, chunks, chunk_rows, far_sems, near_sems, hand_sems, recv_sems):
+        self.mdl_at, self.own, self.blocks, self.chunks, self.chunk_rows = mdl_at, own, blocks, chunks, chunk_rows
+        self.far_sems, self.near_sems, self.hand_sems, self.recv_sems = far_sems, near_sems, hand_sems, recv_sems
+        self.far = lax.rem(mdl_at + 2, 4)
+        self.near = mdl_at + 1 - 2 * lax.rem(mdl_at, 2)
+        self.far_near = lax.rem(self.near + 2, 4)
+
+    def place(self, owner, chunk):
+        return self.blocks.at[owner, pl.ds(chunk * self.chunk_rows, self.chunk_rows), :]
+
+    def far_copy(self, chunk):
+        source = self.own.at[pl.ds(chunk * self.chunk_rows, self.chunk_rows), :]
+        return remote(
+            source, self.place(self.mdl_at, chunk), self.far_sems.at[chunk], self.recv_sems.at[self.mdl_at, chunk], peer(mdl=self.far)
+        )
+
+    def near_copy(self, chunk):
+        source = self.own.at[pl.ds(chunk * self.chunk_rows, self.chunk_rows), :]
+        return remote(
+            source, self.place(self.mdl_at, chunk), self.near_sems.at[chunk], self.recv_sems.at[self.mdl_at, chunk], peer(mdl=self.near)
+        )
+
+    def hand_copy(self, chunk):
+        return remote(
+            self.place(self.far, chunk),
+            self.place(self.far, chunk),
+            self.hand_sems.at[chunk],
+            self.recv_sems.at[self.far, chunk],
+            peer(mdl=self.near),
+        )
+
+    def arrive(self, owner, chunk):
+        remote(
+            self.place(owner, chunk), self.place(owner, chunk), self.hand_sems.at[chunk], self.recv_sems.at[owner, chunk], peer(mdl=self.near)
+        ).wait_recv()
+
+    def start(self):
+        for chunk in range(self.chunks):
+            self.far_copy(chunk).start()
+        for chunk in range(self.chunks):
+            self.near_copy(chunk).start()
+
+    def hand(self, chunk):
+        self.arrive(self.far, chunk)
+        self.hand_copy(chunk).start()
+
+    def arrive_rest(self, chunk):
+        self.arrive(self.near, chunk)
+        self.arrive(self.far_near, chunk)
+
+    def wait_send(self):
+        for chunk in range(self.chunks):
+            self.far_copy(chunk).wait_send()
+            self.near_copy(chunk).wait_send()
+            self.hand_copy(chunk).wait_send()
+
+
+def gather_kernel(
+    small_own,
+    time_own,
+    ada_own,
+    ada_bias,
+    head_shard,
+    unit_shard,
+    tokens,
+    cotangent,
+    small_all,
+    embedding_out,
+    cond_out,
+    mod_out,
+    head_full,
+    unit_full,
+    token_blocks,
+    cot_blocks,
+    time_all,
+    cond_blocks,
+    mod_parts,
+    mod_slots,
+    small_send,
+    small_recv,
+    time_send,
+    time_recv,
+    cond_send,
+    cond_recv,
+    part_send,
+    part_recv,
+    mod_send,
+    mod_recv,
+    line_sends,
+    line_recvs,
+    quad_sends,
+    quad_recvs,
+    own_sems,
+):
+    tok_at = lax.axis_index("tok")
+    mdl_at = lax.axis_index("mdl")
+    tok_count, slots = small_all.shape[0], small_all.shape[1]
+    freq_count = time_all.shape[0] * time_all.shape[1]
+    local_width = time_own.shape[1]
+    own_rows = head_shard.shape[0]
+    greet(tok_at, mdl_at, tok_count, 4)
+
+    small = AllToPeers("tok", tok_at, tok_count, small_send, small_recv)
+    times = AllToPeers("tok", tok_at, tok_count, time_send, time_recv)
+    conds = AllToPeers("mdl", mdl_at, 4, cond_send, cond_recv)
+    parts = AllToPeers("tok", tok_at, tok_count, part_send, part_recv)
+    mods = AllToPeers("mdl", mdl_at, 4, mod_send, mod_recv)
+    heads = LineGather(
+        tok_at, head_shard, head_full, own_rows, line_sends.at[0, 0], line_sends.at[0, 1], line_sends.at[0, 2], line_recvs.at[0]
+    )
+    units = LineGather(
+        tok_at, unit_shard, unit_full, own_rows, line_sends.at[1, 0], line_sends.at[1, 1], line_sends.at[1, 2], line_recvs.at[1]
+    )
+    chunks = quad_recvs.shape[2]
+    chunk_rows = tokens.shape[0] // chunks
+    token_quad = QuadGather(
+        mdl_at, tokens, token_blocks, chunks, chunk_rows, quad_sends.at[0, 0], quad_sends.at[0, 1], quad_sends.at[0, 2], quad_recvs.at[0]
+    )
+    cot_quad = QuadGather(
+        mdl_at, cotangent, cot_blocks, chunks, chunk_rows, quad_sends.at[1, 0], quad_sends.at[1, 1], quad_sends.at[1, 2], quad_recvs.at[1]
+    )
+
+    small.start(lambda other: small_own, small_all)
+    times.start(lambda other: time_own, time_all)
+    token_quad.start()
+    heads.start()
+    own_copies = (
+        pltpu.make_async_copy(head_shard, heads.slot(tok_at), own_sems.at[0]),
+        pltpu.make_async_copy(unit_shard, units.slot(tok_at), own_sems.at[1]),
+        pltpu.make_async_copy(tokens, token_blocks.at[mdl_at], own_sems.at[2]),
+        pltpu.make_async_copy(cotangent, cot_blocks.at[mdl_at], own_sems.at[3]),
+    )
+    for copy in own_copies:
+        copy.start()
+    small_all[tok_at] = small_own[...]
+    time_all[tok_at] = time_own[...]
+    small.wait_recv(lambda other: small_own, small_all)
+    times.wait_recv(lambda other: time_own, time_all)
+
+    feats = small_all[:, :, :freq_count].reshape(tok_count * slots, freq_count)
+    time_full = time_all[...].reshape(freq_count, local_width)
+    embedding = small_all[:, :, freq_count : freq_count + local_width].reshape(tok_count * slots, local_width)
+    for piece in split_three(feats):
+        embedding = embedding + mm(piece, time_full, ((1,), (0,)))
+    embedding_out[...] = embedding
+    cond_blocks[mdl_at] = (embedding / (1.0 + jnp.exp(-embedding))).astype(bf16)
+    conds.start(lambda other: cond_blocks.at[mdl_at], cond_blocks)
+    heads.forward(1)
+    conds.wait_recv(lambda other: cond_blocks.at[mdl_at], cond_blocks)
+    cond_block = cond_blocks[lax.div(tok_at, 2)].astype(f32)
+    cond_own = jnp.where(lax.rem(tok_at, 2) == 0, cond_block[:, :own_rows], cond_block[:, own_rows:]).astype(bf16)
+    cond_out[...] = cond_own
+    mod_parts[...] = mm(cond_own, ada_own[...], ((1,), (0,))).reshape(mod_parts.shape)
+    parts.start(lambda other: mod_parts.at[other], mod_slots)
+    units.start()
+    cot_quad.start()
+    for chunk in range(chunks):
+        token_quad.hand(chunk)
+    heads.forward(2)
+    mod_slots[tok_at] = mod_parts[tok_at]
+    parts.wait_recv(lambda other: mod_parts.at[other], mod_slots)
+    modulation = mod_slots[0]
+    for source in range(1, tok_count):
+        modulation = modulation + mod_slots[source]
+    mod_out[mdl_at] = modulation + ada_bias[...]
+    mods.start(lambda other: mod_out.at[mdl_at], mod_out)
+    heads.forward(3)
+    units.forward(1)
+    for chunk in range(chunks):
+        cot_quad.hand(chunk)
+    units.forward(2)
+    units.forward(3)
+    mods.wait_recv(lambda other: mod_out.at[mdl_at], mod_out)
+    heads.arrive_across()
+    units.arrive_across()
+    for chunk in range(chunks):
+        token_quad.arrive_rest(chunk)
+        cot_quad.arrive_rest(chunk)
+    small.wait_send(lambda other: small_own, small_all)
+    times.wait_send(lambda other: time_own, time_all)
+    conds.wait_send(lambda other: cond_blocks.at[mdl_at], cond_blocks)
+    parts.wait_send(lambda other: mod_parts.at[other], mod_slots)
+    mods.wait_send(lambda other: mod_out.at[mdl_at], mod_out)
+    heads.wait_send()
+    units.wait_send()
+    token_quad.wait_send()
+    cot_quad.wait_send()
+    for copy in own_copies:
+        copy.wait()
+
+
+def gather_all(small_own, time_weight, ada_own, ada_bias, head_shard, unit_shard, tokens, cotangent, tok_count):
+    slots, small_width = small_own.shape
+    freq_rows, local_width = time_weight.shape
+    own_rows, mod_width = ada_own.shape
+    rows = tokens.shape[0]
+    chunks = 5
+    whole = own_rows * tok_count
+    dma = pltpu.SemaphoreType.DMA
+    vmem = pl.BlockSpec(memory_space=pltpu.VMEM)
+    anywhere = pl.BlockSpec(memory_space=pl.ANY)
+    return pl.pallas_call(
+        gather_kernel,
+        out_shape=(
+            jax.ShapeDtypeStruct((tok_count, slots, small_width), f32),
+            jax.ShapeDtypeStruct((tok_count * slots, local_width), f32),
+            jax.ShapeDtypeStruct((tok_count * slots, own_rows), bf16),
+            jax.ShapeDtypeStruct((4, slots, mod_width), f32),
+            jax.ShapeDtypeStruct((whole, head_shard.shape[1]), bf16),
+            jax.ShapeDtypeStruct((whole, unit_shard.shape[1]), bf16),
+            jax.ShapeDtypeStruct((4, rows, local_width), bf16),
+            jax.ShapeDtypeStruct((4, rows, local_width), bf16),
+        ),
+        in_specs=[vmem] * 8,
+        out_specs=(vmem, vmem, vmem, vmem, anywhere, anywhere, anywhere, anywhere),
+        scratch_shapes=[
+            pltpu.VMEM((tok_count, freq_rows, local_width), bf16),
+            pltpu.VMEM((4, tok_count * slots, local_width), bf16),
+            pltpu.VMEM((tok_count, slots, mod_width), f32),
+            pltpu.VMEM((tok_count, slots, mod_width), f32),
+            dma((tok_count,)),
+            dma((tok_count,)),
+            dma((tok_count,)),
+            dma((tok_count,)),
+            dma((4,)),
+            dma((4,)),
+            dma((tok_count,)),
+            dma((tok_count,)),
+            dma((4,)),
+            dma((4,)),
+            dma((2, 3, tok_count)),
+            dma((2, tok_count)),
+            dma((2, 3, chunks)),
+            dma((2, 4, chunks)),
+            dma((4,)),
+        ],
+        compiler_params=pltpu.CompilerParams(collective_id=0, has_side_effects=True, vmem_limit_bytes=40 * 2**20),
+    )(small_own, time_weight, ada_own, ada_bias, head_shard, unit_shard, tokens, cotangent)
+
+
+def cond_back_kernel(
+    gmod_own,
+    ada_own,
+    cond_own,
+    embedding,
+    gmod_all,
+    grad_ada,
+    grad_embed,
+    part_own,
+    part_slots,
+    cond_slots,
+    gmod_send,
+    gmod_recv,
+    part_send,
+    part_recv,
+    cond_send,
+    cond_recv,
+):
+    tok_at = lax.axis_index("tok")
+    mdl_at = lax.axis_index("mdl")
+    tok_count, slots = gmod_all.shape[0], gmod_all.shape[1]
+    greet(tok_at, mdl_at, tok_count, 4)
+    gmods = AllToPeers("tok", tok_at, tok_count, gmod_send, gmod_recv)
+    gmods.start(lambda other: gmod_own, gmod_all)
+    gmod_all[tok_at] = gmod_own[...]
+    gmods.wait_recv(lambda other: gmod_own, gmod_all)
+    high, rest = split_two(gmod_all[...].reshape(tok_count * slots, gmod_all.shape[2]))
+    ada = ada_own[...]
+    part_own[...] = mm(high, ada, ((1,), (1,))) + mm(rest, ada, ((1,), (1,)))
+    owner = lax.div(tok_at, 2)
+    half = lax.rem(tok_at, 2)
+
+    def part_copy(source):
+        return remote(part_own, part_slots.at[source], part_send.at[0], part_recv.at[source], peer(mdl=owner))
+
+    pl.when(mdl_at != owner)(lambda: part_copy(mdl_at).start())
+    cond = cond_own[...]
+    grad_ada[...] = mm(cond, high, ((0,), (0,))) + mm(cond, rest, ((0,), (0,)))
+
+    def cond_copy(step):
+        other = lax.rem(tok_at + step, tok_count)
+        return remote(cond_slots.at[half], cond_slots.at[half], cond_send.at[step], cond_recv.at[half], peer(tok=other))
+
+    @pl.when(mdl_at == owner)
+    def _():
+        total = part_own[...]
+        for step in range(1, 4):
+            source = lax.rem(mdl_at + step, 4)
+            part_copy(source).wait_recv()
+            total = total + part_slots[source]
+        cond_slots[half] = total
+        for step in range(1, tok_count):
+            cond_copy(step).start()
+
+    for side in range(2):
+        giver = 2 * mdl_at + side
+
+        @pl.when(tok_at != giver)
+        def _():
+            remote(cond_slots.at[side], cond_slots.at[side], cond_send.at[0], cond_recv.at[side], peer(tok=giver)).wait_recv()
+
+    grad_cond = jnp.concatenate([cond_slots[0], cond_slots[1]], axis=1)
+    embed = embedding[...]
+    gate = 1.0 / (1.0 + jnp.exp(-embed))
+    grad_embed[...] = grad_cond * gate * (1.0 + embed * (1.0 - gate))
+    gmods.wait_send(lambda other: gmod_own, gmod_all)
+    pl.when(mdl_at != owner)(lambda: part_copy(mdl_at).wait_send())
+
+    @pl.when(mdl_at == owner)
+    def _():
+        for step in range(1, tok_count):
+            cond_copy(step).wait_send()
+
+
+def cond_back(gmod_own, ada_own, cond_own, embedding, tok_count):
+    slots, mod_width = gmod_own.shape
+    crops, own_rows = cond_own.shape
+    dma = pltpu.SemaphoreType.DMA
+    vmem = pl.BlockSpec(memory_space=pltpu.VMEM)
+    return pl.pallas_call(
+        cond_back_kernel,
+        out_shape=(
+            jax.ShapeDtypeStruct((tok_count, slots, mod_width), f32),
+            jax.ShapeDtypeStruct((own_rows, mod_width), f32),
+            jax.ShapeDtypeStruct(embedding.shape, f32),
+        ),
+        in_specs=[vmem] * 4,
+        out_specs=(vmem, vmem, vmem),
+        scratch_shapes=[
+            pltpu.VMEM((crops, own_rows), f32),
+            pltpu.VMEM((4, crops, own_rows), f32),
+            pltpu.VMEM((2, crops, own_rows), f32),
+            dma((tok_count,)),
+            dma((tok_count,)),
+            dma((1,)),
+            dma((4,)),
+            dma((tok_count,)),
+            dma((2,)),
+        ],
+        compiler_params=pltpu.CompilerParams(collective_id=1, has_side_effects=True, vmem_limit_bytes=32 * 2**20),
+    )(gmod_own, ada_own, cond_own, embedding)
 
 
 def on_device(
@@ -118,6 +579,218 @@
     def own_cols(full_rows):
         return lax.dynamic_slice_in_dim(full_rows, mdl_at * local_width, local_width, axis=1)
 
+    slots = 8
+    tok_count = lax.axis_size("tok")
+    ada_own = ada_weight.reshape(own_rows, 6 * local_width)
+    freq_rows = time_weight.shape[0]
+    freq_count = freq_rows * tok_count
+    label_hot_own = (labels[0][:, None] == jnp.arange(class_table.shape[0], dtype=jnp.int32)[None, :]).astype(bf16)
+    small_own = jnp.concatenate(
+        [
+            timestep_features(timesteps[0], freq_count),
+            mm(label_hot_own, class_table, ((1,), (0,))),
+            jnp.broadcast_to(labels[0].astype(f32)[:, None], (slot_count, 96)),
+        ],
+        axis=1,
+    )
+    small_own = jnp.pad(small_own, ((0, slots - slot_count), (0, 0)))
+    head_shard = jnp.concatenate([qkv_weight.reshape(own_rows, 3 * local_width), out_weight.T], axis=1)
+    unit_shard = jnp.concatenate([up_weight, down_weight.T], axis=1)
+    small_all, embedding, cond_own, mod_blocks, head_full, unit_full, token_blocks, cot_blocks = gather_all(
+        small_own, time_weight, ada_own, ada_bias.astype(f32).reshape(1, 6 * local_width), head_shard, unit_shard, tokens, cotangent, tok_count
+    )
+    all_crops = tok_count * slots
+    real_crop = (jnp.arange(all_crops, dtype=jnp.int32) % slots < slot_count)[:, None]
+    step_feats = small_all[:, :, :freq_count].reshape(all_crops, freq_count)
+    label_all = small_all[:, :, freq_count + local_width].reshape(all_crops).astype(jnp.int32)
+    label_hot = ((label_all[:, None] == jnp.arange(class_table.shape[0], dtype=jnp.int32)[None, :]) & real_crop).astype(f32)
+    mod_full = jnp.concatenate(
+        [mod_blocks[at, :slot_count].reshape(slot_count, 6, local_width) for at in range(4)], axis=2
+    )
+    tokens_full = jnp.concatenate([token_blocks[at] for at in range(4)], axis=1)
+    cot_full = jnp.concatenate([cot_blocks[at] for at in range(4)], axis=1)
+    qkv_full, out_full = head_full[:, : 3 * local_width], head_full[:, 3 * local_width :]
+    up_full, down_full = unit_full[:, :units_here], unit_full[:, units_here:]
+    out_bias_full = lax.all_gather(out_bias, "mdl", axis=0, tiled=True).astype(f32)
+
+    inside, segment = crop_layout(lengths, padding, row_len)
+    crop_hot = inside[0].astype(bf16)
+    crop_hot32 = inside[0].astype(f32)
+
+    def spread(part):
+        return exact_dot(crop_hot32, mod_full[:, part])
+
+    head_tok = mm(crop_hot, head_mask[0].astype(bf16), ((1,), (0,)))
+    head_units = jnp.repeat(head_tok, head_width, axis=1).astype(bf16)
+    chan_tok = mm(crop_hot, chan_mask[0].astype(bf16), ((1,), (0,)))
+    chan_units = jnp.repeat(chan_tok, units_here // groups_here, axis=1)
+    keep_rows = keep_mask.astype(f32)[:, None]
+
+    start_rows = tokens_full.astype(f32)
+    normed_one, inverse_one = norm_rows(start_rows)
+    modulated_one = (normed_one * (1.0 + spread(1)) + spread(0)).astype(bf16)
+    projected = mm(modulated_one, qkv_full, ((1,), (0,)))
+    qv_bias32 = qv_bias.astype(f32)
+    queries = (projected[:, :local_width] + qv_bias32[0]).astype(bf16)
+    key_rows = projected[:, local_width : 2 * local_width].astype(bf16)
+    value_rows = (projected[:, 2 * local_width :] + qv_bias32[1]).astype(bf16)
+
+    def heads(rows):
+        return rows.reshape(row_len, heads_here, head_width)
+
+    attend_now, logsum_rows = attend_row(
+        heads(queries), heads(key_rows), heads(value_rows), segment[0], score_scale
+    )
+    attended = (attend_now.reshape(row_len, local_width) * head_units.astype(f32)).astype(bf16)
+    branch_own = scatter_cols(mm(attended, out_full, ((1,), (1,))))
+    attn_branch = gather_cols(branch_own).astype(f32) + out_bias_full
+    gate_one = spread(2)
+    middle = start_rows + gate_one * attn_branch
+    normed_two, inverse_two = norm_rows(middle)
+    scale_two = spread(4)
+    modulated_two = (normed_two * (1.0 + scale_two) + spread(3)).astype(bf16)
+    up_pre = mm(modulated_two, up_full, ((1,), (0,))) + up_bias.astype(f32)
+    gelu_values, gelu_back = jax.vjp(lambda pre: jax.nn.gelu(pre, approximate=True), up_pre)
+    hidden = (gelu_values * chan_units).astype(bf16)
+    mlp_out = scatter_cols(mm(hidden, down_full, ((1,), (1,)))).astype(f32) + down_bias.astype(f32)
+    gate_two = spread(5)
+    output = (own_cols(middle) + own_cols(gate_two) * keep_rows * mlp_out).astype(bf16)
+
+    grad_rows = cot_full.astype(f32)
+    grad_mlp = (grad_rows * gate_two * keep_rows).astype(bf16)
+    grad_hidden = mm(grad_mlp, down_full, ((1,), (0,)))
+    grad_down = mm(grad_mlp, hidden, ((0,), (0,)))
+    grad_down_bias = jnp.sum(own_cols(grad_mlp).astype(f32), axis=0)
+    grad_up_pre = gelu_back(grad_hidden * chan_units)[0].astype(bf16)
+    grad_up = mm(modulated_two, grad_up_pre, ((0,), (0,)))
+    grad_up_bias = jnp.sum(grad_up_pre.astype(f32), axis=0)
+    grad_units = lax.psum_scatter(
+        jnp.concatenate([grad_up, grad_down], axis=1).astype(bf16), "tok", scatter_dimension=0, tiled=True
+    ).astype(f32)
+    two_own = scatter_cols(mm(grad_up_pre, up_full, ((1,), (1,))))
+    grad_two = gather_cols(two_own).astype(f32)
+
+    def norm_back(grad_norm, normed, inverse):
+        return inverse * (
+            grad_norm
+            - jnp.mean(grad_norm, axis=1, keepdims=True)
+            - normed * jnp.mean(grad_norm * normed, axis=1, keepdims=True)
+        )
+
+    grad_middle = grad_rows + norm_back(grad_two * (1.0 + scale_two), normed_two, inverse_two)
+    grad_attn = (grad_middle * gate_one).astype(bf16)
+    grad_out = mm(grad_attn, attended, ((0,), (0,)))
+    grad_out_bias = jnp.sum(own_cols(grad_attn).astype(f32), axis=0)
+    grad_att = mm(grad_attn, out_full, ((1,), (0,))).astype(bf16) * head_units
+    query_grads, key_grads, value_grads = attend_back(
+        heads(queries), heads(key_rows), heads(value_rows), segment[0], logsum_rows, heads(grad_att), score_scale
+    )
+    grad_qkv_rows = jnp.concatenate(
+        [part.reshape(row_len, local_width).astype(bf16) for part in (query_grads, key_grads, value_grads)], axis=1
+    )
+    grad_qkv = mm(modulated_one, grad_qkv_rows, ((0,), (0,)))
+    grad_bias_rows = jnp.sum(grad_qkv_rows.astype(f32), axis=0)
+    grad_qv_bias = jnp.stack([grad_bias_rows[:local_width], grad_bias_rows[2 * local_width :]], axis=0)
+    grad_heads = lax.psum_scatter(
+        jnp.concatenate([grad_qkv, grad_out], axis=1).astype(bf16), "tok", scatter_dimension=0, tiled=True
+    ).astype(f32)
+    grad_one = scatter_cols(mm(grad_qkv_rows, qkv_full, ((1,), (1,)))).astype(f32)
+    normed_one_own = own_cols(normed_one)
+    grad_norm = grad_one * (1.0 + own_cols(spread(1)))
+    totals = lax.psum(
+        jnp.stack([jnp.sum(grad_norm, axis=1), jnp.sum(grad_norm * normed_one_own, axis=1)]), "mdl"
+    )
+    grad_middle_own = own_cols(grad_middle)
+    grad_tokens = grad_middle_own + inverse_one * (
+        grad_norm - totals[0][:, None] / full_width - normed_one_own * totals[1][:, None] / full_width
+    )
+    two_own32 = two_own.astype(f32)
+    grad_per_token = jnp.concatenate(
+        [
+            grad_one,
+            grad_one * normed_one_own,
+            grad_middle_own * own_cols(attn_branch),
+            two_own32,
+            two_own32 * own_cols(normed_two),
+            cotangent.astype(f32) * keep_rows * mlp_out,
+        ],
+        axis=1,
+    )
+    grad_mod_own = lax.dot_general(
+        crop_hot32, grad_per_token, (((0,), (0,)), ((), ())), precision=lax.Precision.HIGHEST, preferred_element_type=f32
+    )
+    bias_row = jnp.concatenate([grad_qv_bias.reshape(-1), grad_out_bias, grad_up_bias, grad_down_bias])
+    bias_row = jnp.pad(bias_row, (0, 2 * 6 * local_width - bias_row.shape[0])).reshape(2, 6 * local_width)
+    gmod_all, grad_ada, grad_embed = cond_back(
+        jnp.concatenate([grad_mod_own, bias_row], axis=0), ada_own, cond_own, embedding, tok_count
+    )
+    grad_ada = grad_ada.reshape(own_rows, 6, local_width)
+    grad_ada_bias = jnp.sum(gmod_all[:, :slot_count], axis=(0, 1)).reshape(6, local_width)
+    bias_total = jnp.sum(gmod_all[:, slot_count:], axis=0).reshape(-1)
+    grad_qv_bias = bias_total[: 2 * local_width].reshape(2, local_width)
+    grad_out_bias = bias_total[2 * local_width : 3 * local_width]
+    grad_up_bias = bias_total[3 * local_width : 3 * local_width + units_here]
+    grad_down_bias = bias_total[3 * local_width + units_here : 4 * local_width + units_here]
+    own_feats = lax.dynamic_slice_in_dim(step_feats, tok_at * freq_rows, freq_rows, axis=1)
+    grad_time = exact_dot(own_feats.T, grad_embed)
+    grad_class = exact_dot(label_hot.T, grad_embed)
+    return (
+        output,
+        grad_tokens,
+        grad_heads[:, : 3 * local_width].reshape(own_rows, 3, local_width),
+        grad_qv_bias,
+        grad_heads[:, 3 * local_width :].T,
+        grad_out_bias,
+        grad_units[:, :units_here],
+        grad_up_bias,
+        grad_units[:, units_here:].T,
+        grad_down_bias,
+        grad_ada,
+        grad_ada_bias,
+        grad_time,
+        grad_class,
+    )
+
+
+def on_device_any(
+    tokens,
+    cotangent,
+    lengths,
+    padding,
+    timesteps,
+    labels,
+    head_mask,
+    chan_mask,
+    keep_mask,
+    qkv_weight,
+    qv_bias,
+    out_weight,
+    out_bias,
+    up_weight,
+    up_bias,
+    down_weight,
+    down_bias,
+    ada_weight,
+    ada_bias,
+    time_weight,
+    class_table,
+):
+    row_count, slot_count = lengths.shape
+    token_count, local_width = tokens.shape
+    row_len = token_count // row_count
+    heads_here = head_mask.shape[2]
+    head_width = local_width // heads_here
+    units_here = up_bias.shape[0]
+    groups_here = chan_mask.shape[2]
+    own_rows = qkv_weight.shape[0]
+    full_width = local_width * lax.axis_size("mdl")
+    score_scale = 1.0 / math.sqrt(head_width)
+    tok_at = lax.axis_index("tok")
+    mdl_at = lax.axis_index("mdl")
+
+    def own_cols(full_rows):
+        return lax.dynamic_slice_in_dim(full_rows, mdl_at * local_width, local_width, axis=1)
+
     all_steps = lax.all_gather(jnp.stack([timesteps, labels]), "tok", axis=1, tiled=True)
     time_full = lax.all_gather(time_weight, "tok", axis=0, tiled=True)
     all_crops = all_steps.shape[1] * slot_count
@@ -287,8 +960,9 @@
 
 
 def solution(mesh):
+    body = on_device if dict(mesh.shape) == {"tok": 8, "mdl": 4} else on_device_any
     return jax.shard_map(
-        on_device,
+        body,
         mesh=mesh,
         in_specs=(
             P("tok", "mdl"),

time: 873 us -> 751 us (0.86)
  blocking collectives: 229 us -> 16.2 us
  Pallas kernels: 0 us -> 137 us
  waiting for transfers between devices: 247 us -> 175 us
  local copies, waits for them, and re-layouts: 87 us -> 114 us
    unnamed x16 -> x14, waiting for transfers between devices: 18.3 us -> 175 us
    all_gather x6 -> x0, blocking collectives: 152 us -> none  [the longest x1 31.4 us: on_device(): lax.all_gather(lax.psum(cond_part, 'mdl'), 'tok', axis=1, tiled=True)]
    pallas_call x0 -> x2, Pallas kernels: none -> 137 us  [the longest x1 115 us: gather_all(): pl.pallas_call(gather_kernel, out_shape=(jax.ShapeDtypeStruct((tok_count,...]
    reduce_scatter x4 -> x0, waiting for transfers between devices: 130 us -> none  [scatter_cols(): lax.psum_scatter(partial_rows.astype(bf16), 'mdl', scatter_dimension=1, t...]
    all_gather x2 -> x0, waiting for transfers between devices: 69.8 us -> none  [the longest x1 69.8 us: on_device(): unit_full = lax.all_gather(unit_shard, 'tok', axis=0, tiled=True)]
    psum x1 -> x0, blocking collectives: 38.5 us -> none  [on_device(): lax.psum((grad_qv_bias, grad_out_bias, grad_up_bias, grad_down_bias), 'tok')]
    all_gather x4 -> x2, waiting for transfers between devices: 28.7 us -> 0.02 us  [gather_cols(): return lax.all_gather(rows_low, 'mdl', axis=1, tiled=True)]
    concatenate x0 -> x5, local copies, waits for them, and re-layouts: none -> 24.5 us  [the longest x1 11.2 us: on_device(): jnp.concatenate([grad_one, grad_one * normed_one_own, grad_middle_own * o...]
  transfers between devices with their start and end apart: 14 -> 8, of which waited for: 9 -> 5; matrix products, arithmetic and copies ran while one was open for 33% -> 30% of each run, Pallas kernels for 0% -> 0%
where the time goes in v2:
time: 751 us; the launch traced here: 739 us
  matrix products  183 us (24%)
  waiting for transfers between devices  175 us (23%)
  Pallas kernels  137 us (18%)
  local copies, waits for them, and re-layouts  114 us (15%)
  other arithmetic  97.3 us (13%)
  blocking collectives  16.2 us (2%)
  between operations  16.2 us (2%)
    unnamed x14, waiting for transfers between devices  175 us
    pallas_call x1, Pallas kernels, gather_all(): pl.pallas_call(gather_kernel, out_shape=(jax.ShapeDtypeStruct((tok_count,...  115 us
    dot_general x15, matrix products, mm(): lax.dot_general(left, right, (dims, ((), ())), preferred_element_type=f32)  65 us
    unnamed x127, local copies, waits for them, and re-layouts  51.1 us
    dot_general x8, matrix products, exact_dot(): jnp.dot(left, right, precision=lax.Precision.HIGHEST, preferred_element_t...  41.2 us
    convert_element_type x1, other arithmetic, attend_back(): grad_scores = (prob_full * (grad_prob - inner_sum)).astype(bf16)  22.9 us
    pallas_call x1, Pallas kernels, cond_back(): pl.pallas_call(cond_back_kernel, out_shape=(jax.ShapeDtypeStruct((tok_cou...  22.5 us
    dot_general x1, matrix products, attend_back(): jnp.einsum('qhd,khd->hqk', grad_att, value_rows, preferred_element_type=f32)  17.2 us
  transfers between devices with their start and end apart: 8, of which 5 were waited for; matrix products, arithmetic and copies ran while one was open for 30% of the time, Pallas kernels for 0%

profile of v2, /device:TPU:0, one launch (start us, length us, event | category | flops | bytes accessed | tf_op | source)
XLA Modules:
  0.0 739.5 jit_solution(7566849916674159119)
XLA Ops:
  22.2 115.0 %shard_map.308 = (f32[8,8,640]{2,1,0:T(8,128)S(1)}, f32[64,288]{1,0:T(8,128)S(1)}, bf16[64,144]{1,0:T(8,128)(2,1)S(1)}, f32[4,8,1728]{2,1,0:T(8,128)S(1)}, bf16[...) custom-call(f32[8,640]{1,0:T(8,128)S(1)} %select_maximum_fusion.smal, ...), custom_call_target="tpu_custom_call" | custom-call | tf_op jit(solution)/shard_map/pallas_call | solution.py:401
  141.7 6.5 concatenate.41
  165.6 11.2 %fusion.97 = (f32[4,1280]{1,0:T(4,128)S(1)}, f32[4,1280,1280]{1,2,0:T(8,128)}) fusion(bf16[1280,4,72]{0,2,1:T(8,128)(2,1)S(1)} %bitcast.147, bf16[1280,4,72]{0,2,1:T(8,128)(2,1)S(1)} %bitcast.153, pred[1280,1280]{0,1:T(8,128)(4,1)S(1)} %copy-done.27), kind=kOutput, calls=%fused_computation.192 | convolution fusion | flops 963374080 | bytes 29347840 | tf_op jit(solution)/shard_map/qhd,khd->hqk/dot_general | solution.py:59
  176.7 10.6 %fusion.1 = f32[4,1280]{1,0:T(4,128)S(1)} fusion(f32[4,1280,1280]{1,2,0:T(8,128)} %get-tuple-element.147, f32[4,1280]{1,0:T(4,128)S(1)} %get-tuple-element.146), kind=kLoop, calls=%fused_computation.7 | loop fusion | flops 13102080 | bytes 26255360 | tf_op jit(solution)/shard_map/reduce_sum | solution.py:64
  187.3 10.8 %fusion.6 = f32[4,72,1280]{2,1,0:T(8,128)S(1)} fusion(bf16[1280,4,72]{0,2,1:T(8,128)(2,1)S(1)} %bitcast.145, f32[4,1280,1280]{1,2,0:T(8,128)} %get-tuple-element.147, f32[4,1280]{1,0:T(4,128)S(1)} %fusion.1, f32[4,1280]{1,0:T(4,128)S(1)} %get-tuple-element.146), kind=kOutput, calls=%fused_computation.11 | convolution fusion | flops 963379200 | bytes 28467200 | tf_op jit(solution)/shard_map/hqk,khd->qhd/dot_general | solution.py:66
  202.6 34.9 %reduce-scatter.19.cloned.1.call-done = bf16[288,1280]{1,0:T(8,128)(2,1)} async-done(((bf16[1152,1280]{1,0:T(8,128)(2,1)}), bf16[288,1280]{1,0:T(8,128)(2,1)}) %reduce-scatter.19.cloned.1.call-update) | async-done | bytes 737296
  248.2 7.9 %copy.137 = f32[1280,1152]{1,0:T(8,128)} copy(f32[1280,1152]{0,1:T(8,128)} %bitcast.140) | data formatting | bytes 11796480 | tf_op jit(solution)/shard_map/reshape | solution.py:626
  259.8 6.5 concatenate.43
  271.2 5.9 fusion.14
  282.6 11.2 %fusion.92 = (f32[1280]{0:T(1024)S(1)}, f32[1280]{0:T(1024)S(1)}, f32[1280,1152]{1,0:T(8,128)S(1)}, f32[1280,1152]{1,0:T(8,128)}, f32[1280,1152]{1,0:T(8,128)}, /*index=5*/f32[1280,1152]{1,0:T(8,128)}) fusion(f32[1152]{0:T(1024)S(1)} %convert_element_type.216, bf16[1280,1152]{1,0:T(8,128)(2,1)} %copy.133, bf16[1280,1152]{1,0:T(8,128)(2,1)} %concatenate.41, ...), kind=kOutput, calls=%fused_computation.187 | convolution fusion | flops 120934400 | bytes 29543984 | tf_op jit(solution)/shard_map/dot_general | solution.py:17
  296.8 8.4 %fusion.8 = bf16[1280,1152]{1,0:T(8,128)(2,1)S(1)} fusion(f32[1280,1152]{1,0:T(8,128)S(1)} %subtract_multiply_fusion, f32[1280,1152]{1,0:T(8,128)} %convolution_add_fusion.1, f32[6,1,1152]{2,1,0:T(1,128)S(1)} %get-tuple-element.129, s32[6]{0:T(128)S(1)} %get-tuple-element.145, s32[6]{0:T(128)S(1)} %get-tuple-element.144), kind=kOutput, calls=%fused_computation.28 | convolution fusion | flops 110615040 | bytes 14773296 | tf_op jit(solution)/shard_map/dot_general | solution.py:17
  305.2 6.7 multiply_convert_fusion.2
  312.0 9.1 %convert_reduce_fusion.1 = (f32[1152]{0:T(1024)S(1)}, bf16[1280,1152]{1,0:T(8,128)(2,1)S(1)}) fusion(f32[1280,1152]{1,0:T(8,128)S(1)} %get-tuple-element.154, f32[1280,1152]{1,0:T(8,128)S(1)} %bitcast.142, bf16[1280,1152]{1,0:T(8,128)(2,1)S(1)} %copy-done.15, bf16[1152,2304]{1,0:T(8,128)(2,1)S(1)} %bitcast.171), kind=kOutput, calls=%fused_computation.48 | convolution fusion | flops 3431300096 | bytes 20353536 | tf_op jit(solution)/shard_map/dot_general | solution.py:21
  328.1 38.0 %reduce-scatter.23.cloned.1.call-done = bf16[288,1280]{1,0:T(8,128)(2,1)} async-done(((bf16[1152,1280]{1,0:T(8,128)(2,1)}), bf16[288,1280]{1,0:T(8,128)(2,1)}) %reduce-scatter.23.cloned.1.call-update) | async-done | bytes 737296
  366.2 8.2 %fusion.9 = bf16[1152,1280]{1,0:T(8,128)(2,1)} fusion(bf16[1280,1152]{1,0:T(8,128)(2,1)} %get-tuple-element.153, bf16[1152,2304]{1,0:T(8,128)(2,1)} %get-tuple-element.28), kind=kOutput, calls=%fused_computation.33 | convolution fusion | flops 3398860800 | bytes 8552448 | tf_op jit(solution)/shard_map/dot_general | solution.py:21
  374.9 7.3 convolution_convert_fusion
  389.2 8.6 %copy.176 = bf16[1152,2304]{1,0:T(8,128)(2,1)} copy(bf16[1152,2304]{0,1:T(8,128)(2,1)} %pad_maximum_fusion) | data formatting | bytes 10616832
  403.5 7.5 %fusion.34 = (f32[1280]{0:T(1024)S(1)}, f32[1280]{0:T(1024)S(1)}) fusion(f32[1280,1152]{1,0:T(8,128)} %convolution_add_fusion.1, bf16[1280,1152]{1,0:T(8,128)(2,1)} %copy.143, f32[1280]{0:T(1024)S(1)} %get-tuple-element.137, f32[1280,1152]{1,0:T(8,128)} %copy-done.6, f32[1280]{0:T(1024)S(1)} %get-tuple-element.136), kind=kLoop, calls=%fused_computation.73 | loop fusion | flops 10319360 | bytes 14766080 | tf_op jit(solution)/shard_map/reduce_sum | solution.py:676
  411.5 10.7 %multiply_convert_fusion.1 = (bf16[1280,1152]{1,0:T(8,128)(2,1)S(1)}, f32[1280,1152]{1,0:T(8,128)}) fusion(f32[1280,1152]{1,0:T(8,128)} %get-tuple-element.148, f32[1280]{0:T(1024)S(1)} %get-tuple-element.157, f32[1280]{0:T(1024)S(1)} %get-tuple-element.158, f32[1280,1152]{1,0:T(8,128)} %convolution_add_fusion.1, bf16[1280,1152]{1,0:T(8,128)(2,1)S(1)} %copy-done.10, ...), kind=kLoop, calls=%fused_computation.49 | loop fusion | flops 17694720 | bytes 32460800 | tf_op jit(solution)/shard_map/convert_element_type | solution.py:681
  426.0 17.2 %multiply_reduce_fusion = (f32[4,1280]{1,0:T(4,128)S(1)}, f32[4,1280,1280]{1,2,0:T(8,128)}) fusion(f32[4,1280,1280]{1,2,0:T(8,128)} %get-tuple-element.147, f32[4,1280]{1,0:T(4,128)S(1)} %log_add_fusion, bf16[1280,4,72]{0,2,1:T(8,128)(2,1)S(1)} %bitcast.143, bf16[1280,4,72]{0,2,1:T(8,128)(2,1)} %bitcast.146), kind=kOutput, calls=%fused_computation.3 | convolution fusion | flops 963374080 | bytes 53944320 | tf_op jit(solution)/shard_map/qhd,khd->hqk/dot_general | solution.py:75
  443.2 22.9 %multiply_convert_fusion = bf16[4,1280,1280]{1,2,0:T(8,128)(2,1)} fusion(f32[4,1280,1280]{1,2,0:T(8,128)} %get-tuple-element.152, f32[4,1280,1280]{1,2,0:T(8,128)} %get-tuple-element.147, f32[4,1280]{1,0:T(4,128)S(1)} %get-tuple-element.151, f32[4,1280]{1,0:T(4,128)S(1)} %log_add_fusion), kind=kLoop, calls=%fused_computation.2 | loop fusion | flops 26214400 | bytes 65576960 | tf_op jit(solution)/shard_map/convert_element_type | solution.py:77
  466.2 10.0 %fusion.25 = bf16[4,72,1280]{2,1,0:T(8,128)(2,1)} fusion(bf16[1280,4,72]{0,2,1:T(8,128)(2,1)S(1)} %bitcast.148, bf16[4,1280,1280]{1,2,0:T(8,128)(2,1)} %multiply_convert_fusion), kind=kOutput, calls=%fused_computation.64 | convolution fusion | flops 944455680 | bytes 14581760 | tf_op jit(solution)/shard_map/hqk,qhd->khd/dot_general | solution.py:79
  476.2 8.1 %fusion.24 = bf16[4,72,1280]{2,1,0:T(8,128)(2,1)} fusion(bf16[1280,4,72]{0,2,1:T(8,128)(2,1)S(1)} %bitcast.154, bf16[4,1280,1280]{1,2,0:T(8,128)(2,1)} %multiply_convert_fusion), kind=kOutput, calls=%fused_computation.63 | convolution fusion | flops 944455680 | bytes 14581760 | tf_op jit(solution)/shard_map/hqk,khd->qhd/dot_general | solution.py:78
  484.3 12.5 %fusion.26 = bf16[4,72,1280]{2,1,0:T(8,128)(2,1)} fusion(bf16[1280,4,72]{0,2,1:T(8,128)(2,1)S(1)} %bitcast.144, f32[4,1280,1280]{1,2,0:T(8,128)} %get-tuple-element.147, f32[4,1280]{1,0:T(4,128)S(1)} %log_add_fusion), kind=kOutput, calls=%fused_computation.65 | convolution fusion | flops 957194240 | bytes 27709440 | tf_op jit(solution)/shard_map/hqk,qhd->khd/dot_general | solution.py:80
  509.5 6.9 fusion.12
  551.5 64.8 %reduce-scatter.27.cloned.1.call-done = bf16[144,1152]{1,0:T(8,128)(2,1)} async-done(((bf16[1152,1152]{1,0:T(8,128)(2,1)}), bf16[144,1152]{1,0:T(8,128)(2,1)}) %reduce-scatter.27.cloned.1.call-update) | async-done | bytes 331792
  621.7 33.2 %reduce-scatter.25.cloned.1.call-done = bf16[288,1280]{1,0:T(8,128)(2,1)} async-done(((bf16[1152,1280]{1,0:T(8,128)(2,1)}), bf16[288,1280]{1,0:T(8,128)(2,1)}) %reduce-scatter.25.cloned.1.call-update) | async-done | bytes 737296
  661.5 10.5 %psum.7 = f32[2,1280]{1,0:T(2,128)S(1)} all-reduce(f32[2,1280]{1,0:T(2,128)S(1)} %pad_maximum_fusion.6), channel_id=1, replica_groups=mesh['tok'=8,'mdl'=4] {'mdl'}, use_global_device_ids=true, to_apply=%region_17.18 | all-reduce | flops 2560 | bytes 20480 | tf_op jit(solution)/shard_map/psum | solution.py:700
  672.0 6.8 dynamic-slice_multiply_fusion.1
  678.9 11.2 %concatenate.46 = f32[1280,1728]{1,0:T(8,128)} concatenate(bf16[1280,288]{1,0:T(8,128)(2,1)S(1)} %copy.173, f32[1280,288]{1,0:T(8,128)} %get-tuple-element.107, f32[1280,288]{1,0:T(8,128)} %get-tuple-element.108, bf16[1280,288]{1,0:T(8,128)(2,1)S(1)} %copy-done.14, f32[1280,288]{1,0:T(8,128)} %dynamic-slice_multiply_fusion, f32[1280,288]{1,0:T(8,128)} %get-tuple-element.122), dimensions={1} | concatenate | bytes 16220160 | tf_op jit(solution)/shard_map/concatenate | solution.py:708
  690.1 6.6 fusion.44
  696.7 22.5 %shard_map.309 = (f32[8,8,1728]{2,1,0:T(8,128)S(1)}, f32[144,1728]{1,0:T(8,128)S(1)}, f32[64,288]{1,0:T(8,128)S(1)}) custom-call(f32[8,1728]{1,0:T(8,128)S(1)} %pad_maximum_fusion.5.gmod_own, bf16[144,1728]{1,0:T(8,128)(2,1)S(1)} %reshape.632.ada_own, bf16[64,144]{1,0:T(8,128)(2,1)S(1)} %get-tuple-element.30.cond_own, f32[64,288]{1,0:T(8,128)S(1)} %get-tuple-element.31.embedding), custom_call_target="tpu_custom_call" | custom-call | tf_op jit(solution)/shard_map/pallas_call | solution.py:519
  (248 shorter events, 165.1 us)
Async XLA Ops:
  7.2 13.3 %copy-start = (bf16[1000,288]{0,1:T(8,128)(2,1)S(1)}, bf16[1000,288]{0,1:T(8,128)(2,1)}, u32[]{:S(2)}) copy-start(bf16[1000,288]{0,1:T(8,128)(2,1)} %param.41) | copy-start | bytes 1728004
  7.2 8.9 %copy-start.30 = (bf16[1280,288]{0,1:T(8,128)(2,1)S(1)}, bf16[1280,288]{0,1:T(8,128)(2,1)}, u32[]{:S(2)}) copy-start(bf16[1280,288]{0,1:T(8,128)(2,1)} %param.22) | copy-start | bytes 2211844
  7.2 230.3 %reduce-scatter.19.cloned.1.call-start = ((), (), s32[]{:S(2)}) async-start(), calls=%async_computation.8 | async-start | bytes 3686400
  8.9 287.9 %copy-start.36 = (s32[6]{0:T(128)}, s32[6]{0:T(128)S(1)}, u32[]{:S(2)}) copy-start(s32[6]{0:T(128)S(1)} %get-tuple-element.144) | copy-start | bytes 76
  8.9 287.9 %copy-start.38 = (s32[6]{0:T(128)}, s32[6]{0:T(128)S(1)}, u32[]{:S(2)}) copy-start(s32[6]{0:T(128)S(1)} %get-tuple-element.145) | copy-start | bytes 76
  154.6 128.0 %copy-start.31 = (f32[1280]{0:T(1024)}, f32[1280]{0:T(1024)S(1)}, u32[]{:S(2)}) copy-start(f32[1280]{0:T(1024)S(1)} %get-tuple-element.139) | copy-start | bytes 15364
  163.4 13.3 %copy-start.22 = (bf16[1280,288]{0,1:T(8,128)(2,1)}, bf16[1280,288]{0,1:T(8,128)(2,1)S(1)}, u32[]{:S(2)}) copy-start(bf16[1280,288]{0,1:T(8,128)(2,1)S(1)} %slice.242) | copy-start | bytes 2211844
  163.7 13.1 %copy-start.18 = (bf16[1280,288]{0,1:T(8,128)(2,1)}, bf16[1280,288]{0,1:T(8,128)(2,1)S(1)}, u32[]{:S(2)}) copy-start(bf16[1280,288]{0,1:T(8,128)(2,1)S(1)} %get-tuple-element.110) | copy-start | bytes 2211844
  163.7 23.6 %copy-start.17 = (bf16[1280,288]{0,1:T(8,128)(2,1)}, bf16[1280,288]{0,1:T(8,128)(2,1)S(1)}, u32[]{:S(2)}) copy-start(bf16[1280,288]{0,1:T(8,128)(2,1)S(1)} %get-tuple-element.111) | copy-start | bytes 2211844
  199.2 38.4 %copy-start.46 = (u32[32]{0:T(128)S(1)}, u32[32]{0:T(128)}, u32[]{:S(2)}) copy-start(u32[32]{0:T(128)} %constant.95) | copy-start | bytes 388
  199.2 39.7 %copy-start.43 = (bf16[288]{0:T(512)(128)(2,1)S(1)}, bf16[288]{0:T(512)(128)(2,1)}, u32[]{:S(2)}) copy-start(bf16[288]{0:T(512)(128)(2,1)} %param.33) | copy-start | bytes 1732
  199.2 45.7 %copy-start.40 = (s32[1280]{0:T(1024)S(1)}, s32[1280]{0:T(1024)}, u32[]{:S(2)}) copy-start(s32[1280]{0:T(1024)} %param.29) | copy-start | bytes 15364
  199.2 45.7 %copy-start.41 = (bf16[1152]{0:T(1024)(128)(2,1)S(1)}, bf16[1152]{0:T(1024)(128)(2,1)}, u32[]{:S(2)}) copy-start(bf16[1152]{0:T(1024)(128)(2,1)} %param.35) | copy-start | bytes 6916
  199.2 45.7 %copy-start.45 = (s32[1,6,4]{1,2,0:T(4,128)S(1)}, s32[1,6,4]{1,2,0:T(4,128)}, u32[]{:S(2)}) copy-start(s32[1,6,4]{1,2,0:T(4,128)} %param.28) | copy-start | bytes 292
  202.5 74.6 %all-gather.3.cloned.1.call-start = ((), (), s32[]{:S(2)}) async-start(), calls=%async_computation.6 | async-start | bytes 3686400 | tf_op jit(solution)/shard_map/all_gather | solution.py:51
  237.6 128.6 %reduce-scatter.23.cloned.1.call-start = ((), (), s32[]{:S(2)}) async-start(), calls=%async_computation.10 | async-start | bytes 3686400
  244.9 26.3 %copy-start.34 = (f32[1280]{0:T(1024)}, f32[1280]{0:T(1024)S(1)}, u32[]{:S(2)}) copy-start(f32[1280]{0:T(1024)S(1)} %convert_element_type.217) | copy-start | bytes 15364
  293.7 11.4 %slice-start = ((s8[5898240]{0:T(1024)(128)(4,1)}), s8[1703936]{0:T(1024)(128)(4,1)S(1)}, s32[]{:S(2)}) async-start(s8[5898240]{0:T(1024)(128)(4,1)} %bitcast.141), calls=%async_computation.14 | async-start | bytes 3407872
  293.8 11.4 %slice-start.2 = ((s8[5308416]{0:T(1024)(128)(4,1)}), s8[4194304]{0:T(1024)(128)(4,1)S(1)}, s32[]{:S(2)}) async-start(s8[5308416]{0:T(1024)(128)(4,1)} %bitcast.170), calls=%async_computation.16 | async-start | bytes 8388608
  328.0 70.0 %all-gather.5.cloned.1.call-start = ((), (), s32[]{:S(2)}) async-start(), calls=%async_computation.7 | async-start | bytes 3686400 | tf_op jit(solution)/shard_map/all_gather | solution.py:51
  366.1 154.5 %reduce-scatter.21.cloned.1.call-start = ((), (), s32[]{:S(2)}) async-start(), calls=%async_computation.9 | async-start | bytes 3686400
  374.4 167.8 %reduce-scatter.29.cloned.1.call-start = ((), (), s32[]{:S(2)}) async-start(), calls=%async_computation.13 | async-start | bytes 5971968
  397.8 218.5 %reduce-scatter.27.cloned.1.call-start = ((), (), s32[]{:S(2)}) async-start(), calls=%async_computation.12 | async-start | bytes 2985984
  411.5 10.7 %copy-start.29 = (bf16[1280,288]{0,1:T(8,128)(2,1)S(1)}, bf16[1280,288]{0,1:T(8,128)(2,1)}, u32[]{:S(2)}) copy-start(bf16[1280,288]{0,1:T(8,128)(2,1)} %copy-done.28) | copy-start | bytes 2211844
  443.2 22.9 %copy-start.19 = (bf16[1280,288]{0,1:T(8,128)(2,1)S(1)}, bf16[1280,288]{0,1:T(8,128)(2,1)}, u32[]{:S(2)}) copy-start(bf16[1280,288]{0,1:T(8,128)(2,1)} %copy-done.18) | copy-start | bytes 2211844
  466.2 10.0 %copy-start.23 = (bf16[1280,288]{0,1:T(8,128)(2,1)S(1)}, bf16[1280,288]{0,1:T(8,128)(2,1)}, u32[]{:S(2)}) copy-start(bf16[1280,288]{0,1:T(8,128)(2,1)} %copy-done.22) | copy-start | bytes 2211844
  509.4 145.4 %reduce-scatter.25.cloned.1.call-start = ((), (), s32[]{:S(2)}) async-start(), calls=%async_computation.11 | async-start | bytes 3686400
  520.6 10.5 %copy-start.13 = (bf16[1280,288]{1,0:T(8,128)(2,1)}, bf16[1280,288]{1,0:T(8,128)(2,1)S(1)}, u32[]{:S(2)}) copy-start(bf16[1280,288]{1,0:T(8,128)(2,1)S(1)} %copy.171) | copy-start | bytes 2211844
  621.7 50.3 %copy-start.32 = (f32[1280]{0:T(1024)S(1)}, f32[1280]{0:T(1024)}, u32[]{:S(2)}) copy-start(f32[1280]{0:T(1024)} %copy-done.31) | copy-start | bytes 15364
  678.8 11.2 %copy-start.37 = (s32[6]{0:T(128)S(1)}, s32[6]{0:T(128)}, u32[]{:S(2)}) copy-start(s32[6]{0:T(128)} %copy-done.36) | copy-start | bytes 76
  678.8 11.2 %copy-start.39 = (s32[6]{0:T(128)S(1)}, s32[6]{0:T(128)}, u32[]{:S(2)}) copy-start(s32[6]{0:T(128)} %copy-done.38) | copy-start | bytes 76
  722.0 10.1 %copy-start.1 = (bf16[1000,288]{0,1:T(8,128)(2,1)S(1)}, bf16[1000,288]{0,1:T(8,128)(2,1)}, u32[]{:S(2)}) copy-start(bf16[1000,288]{0,1:T(8,128)(2,1)} %param.41) | copy-start | bytes 1728004
  (29 other events, 159.0 us)
Sparse Core Ops, SparseCore 0:
  202.7 34.8 reduce-scatter.18
  239.2 27.4 all-gather.2
  328.2 37.9 reduce-scatter.22
  367.5 27.4 all-gather.4
  397.4 36.7 reduce-scatter.20
  438.0 104.1 reduce-scatter.28
  545.9 70.3 reduce-scatter.26
  619.0 35.7 reduce-scatter.24

commit v3 on v2

--- a/solution.py
+++ b/solution.py
@@ -266,7 +266,8 @@
     small_all,
     embedding_out,
     cond_out,
-    mod_out,
+    mod_full,
+    pieces,
     head_full,
     unit_full,
     token_blocks,
@@ -275,6 +276,7 @@
     cond_blocks,
     mod_parts,
     mod_slots,
+    mod_out,
     small_send,
     small_recv,
     time_send,
@@ -370,6 +372,11 @@
     units.forward(2)
     units.forward(3)
     mods.wait_recv(lambda other: mod_out.at[mdl_at], mod_out)
+    for part in range(6):
+        rows = jnp.concatenate([mod_out[at, :, part * local_width : (part + 1) * local_width] for at in range(4)], axis=1)
+        mod_full[part] = rows
+        split = [piece.astype(f32) for piece in split_three(rows)]
+        pieces[part] = jnp.concatenate(split + [jnp.zeros_like(rows)], axis=0).astype(bf16)
     heads.arrive_across()
     units.arrive_across()
     for chunk in range(chunks):
@@ -404,19 +411,21 @@
             jax.ShapeDtypeStruct((tok_count, slots, small_width), f32),
             jax.ShapeDtypeStruct((tok_count * slots, local_width), f32),
             jax.ShapeDtypeStruct((tok_count * slots, own_rows), bf16),
-            jax.ShapeDtypeStruct((4, slots, mod_width), f32),
+            jax.ShapeDtypeStruct((6, slots, whole), f32),
+            jax.ShapeDtypeStruct((6, 4 * slots, whole), bf16),
             jax.ShapeDtypeStruct((whole, head_shard.shape[1]), bf16),
             jax.ShapeDtypeStruct((whole, unit_shard.shape[1]), bf16),
             jax.ShapeDtypeStruct((4, rows, local_width), bf16),
             jax.ShapeDtypeStruct((4, rows, local_width), bf16),
         ),
         in_specs=[vmem] * 8,
-        out_specs=(vmem, vmem, vmem, vmem, anywhere, anywhere, anywhere, anywhere),
+        out_specs=(vmem, vmem, vmem, vmem, vmem, anywhere, anywhere, anywhere, anywhere),
         scratch_shapes=[
             pltpu.VMEM((tok_count, freq_rows, local_width), bf16),
             pltpu.VMEM((4, tok_count * slots, local_width), bf16),
             pltpu.VMEM((tok_count, slots, mod_width), f32),
             pltpu.VMEM((tok_count, slots, mod_width), f32),
+            pltpu.VMEM((4, slots, mod_width), f32),
             dma((tok_count,)),
             dma((tok_count,)),
             dma((tok_count,)),
@@ -538,6 +547,246 @@
         ],
         compiler_params=pltpu.CompilerParams(collective_id=1, has_side_effects=True, vmem_limit_bytes=32 * 2**20),
     )(gmod_own, ada_own, cond_own, embedding)
+
+
+class RowReduce:
+    def __init__(self, mdl_at, part, near_in, own_sum, far_in, full, sends, recvs):
+        self.part, self.near_in, self.own_sum, self.far_in, self.full = part, near_in, own_sum, far_in, full
+        self.sends, self.recvs = sends, recvs
+        self.core = lax.rem(mdl_at, 2)
+        self.far = peer(mdl=lax.rem(mdl_at + 2, 4))
+        self.near = peer(mdl=mdl_at + 1 - 2 * self.core)
+        self.half = near_in.shape[1]
+
+    def rows(self, chunk, core):
+        return pl.ds(pl.multiple_of((2 * chunk + core) * self.half, 128), self.half)
+
+    def near_copy(self, chunk):
+        source = self.part.at[self.rows(chunk, 1 - self.core), :]
+        return remote(source, self.near_in.at[chunk], self.sends.at[0, chunk], self.recvs.at[0, chunk], self.near)
+
+    def far_copy(self, chunk):
+        return remote(self.own_sum.at[chunk], self.far_in.at[chunk], self.sends.at[1, chunk], self.recvs.at[1, chunk], self.far)
+
+    def share_copy(self, chunk):
+        place = self.full.at[self.rows(chunk, self.core), :]
+        return remote(place, place, self.sends.at[2, chunk], self.recvs.at[2, chunk], self.near)
+
+    def first(self, chunk):
+        self.near_copy(chunk).start()
+
+    def second(self, chunk):
+        self.near_copy(chunk).wait_recv()
+        own = self.part[self.rows(chunk, self.core), :].astype(f32)
+        self.own_sum[chunk] = (own + self.near_in[chunk].astype(f32)).astype(bf16)
+        self.far_copy(chunk).start()
+
+    def third(self, chunk):
+        self.far_copy(chunk).wait_recv()
+        total = self.own_sum[chunk].astype(f32) + self.far_in[chunk].astype(f32)
+        self.full[self.rows(chunk, self.core), :] = total.astype(bf16)
+        self.share_copy(chunk).start()
+
+    def fourth(self, chunk):
+        place = self.full.at[self.rows(chunk, 1 - self.core), :]
+        remote(place, place, self.sends.at[2, chunk], self.recvs.at[2, chunk], self.near).wait_recv()
+
+    def wait_send(self, chunk):
+        self.near_copy(chunk).wait_send()
+        self.far_copy(chunk).wait_send()
+        self.share_copy(chunk).wait_send()
+
+
+def greet_quad(mdl_at):
+    barrier = pltpu.get_barrier_semaphore()
+    for step in range(1, 4):
+        pl.semaphore_signal(
+            barrier, inc=1, device_id=peer(mdl=lax.rem(mdl_at + step, 4)), device_id_type=pl.DeviceIdType.MESH
+        )
+    pl.semaphore_wait(barrier, 3)
+
+
+def centre(values):
+    center = values - jnp.mean(values, axis=1, keepdims=True)
+    inverse = lax.rsqrt(jnp.mean(center * center, axis=1, keepdims=True) + norm_floor)
+    return center * inverse, inverse
+
+
+def feed_kernel(
+    branch_part,
+    token_blocks,
+    cot_blocks,
+    hot,
+    hot_keep,
+    pieces,
+    out_bias,
+    unit_full,
+    up_bias,
+    chan_rows,
+    branch_full,
+    mlp_part,
+    two_full,
+    unit_grads,
+    up_bias_grad,
+    mlp_sums,
+    token_buf,
+    cot_buf,
+    mod_rows,
+    gup_rows,
+    hid_rows,
+    gmlp_rows,
+    two_part,
+    mlp_buf,
+    near_in,
+    own_sum,
+    far_in,
+    sends,
+    recvs,
+    load_sems,
+    store_sems,
+):
+    mdl_at = lax.axis_index("mdl")
+    rows, width = two_full.shape
+    chunks = near_in.shape[1]
+    size = rows // chunks
+    units = up_bias.shape[1]
+    greet_quad(mdl_at)
+    branch = RowReduce(mdl_at, branch_part, near_in.at[0], own_sum.at[0], far_in.at[0], branch_full, sends.at[0], recvs.at[0])
+    twos = RowReduce(mdl_at, two_part, near_in.at[1], own_sum.at[1], far_in.at[1], two_full, sends.at[1], recvs.at[1])
+
+    def span(chunk):
+        return pl.ds(pl.multiple_of(chunk * size, 128), size)
+
+    def loads(chunk, slot):
+        return (
+            pltpu.make_async_copy(token_blocks.at[:, span(chunk), :], token_buf.at[slot], load_sems.at[0, slot]),
+            pltpu.make_async_copy(cot_blocks.at[:, span(chunk), :], cot_buf.at[slot], load_sems.at[1, slot]),
+        )
+
+    def store(chunk, slot):
+        return pltpu.make_async_copy(mlp_buf.at[slot], mlp_part.at[span(chunk), :], store_sems.at[slot])
+
+    for chunk in range(chunks):
+        branch.first(chunk)
+    for copy in loads(0, 0):
+        copy.start()
+    for chunk in range(chunks):
+        branch.second(chunk)
+    branch.third(0)
+    up_bias_grad[...] = jnp.zeros_like(up_bias_grad)
+    mlp_sums[...] = jnp.zeros_like(mlp_sums)
+
+    def step(chunk, carry):
+        slot = lax.rem(chunk, 2)
+
+        @pl.when(chunk + 1 < chunks)
+        def _():
+            for copy in loads(chunk + 1, 1 - slot):
+                copy.start()
+            branch.third(chunk + 1)
+
+        for copy in loads(chunk, slot):
+            copy.wait()
+        branch.fourth(chunk)
+        here = span(chunk)
+        hot_now = hot[here, :]
+
+        def spread(part):
+            return mm(hot_now, pieces[part], ((1,), (0,)))
+
+        token_rows = jnp.concatenate([token_buf[slot, at] for at in range(4)], axis=1).astype(f32)
+        middle = token_rows + spread(2) * (branch_full[here, :].astype(f32) + out_bias[...])
+        normed, inverse = centre(middle)
+        mod_rows[here, :] = (normed * (1.0 + spread(4)) + spread(3)).astype(bf16)
+        up_pre = mm(mod_rows[here, :], unit_full[:, :units], ((1,), (0,))) + up_bias[...]
+        bend = math.sqrt(2.0 / math.pi)
+        square = up_pre * up_pre
+        turn = jnp.tanh(bend * up_pre * (1.0 + 0.044715 * square))
+        chan = mm(hot_now, chan_rows[...], ((1,), (0,)))
+        hid_rows[here, :] = (0.5 * up_pre * (1.0 + turn) * chan).astype(bf16)
+        slope = (0.5 * (1.0 + turn) + 0.5 * up_pre * (1.0 - turn * turn) * (bend * (1.0 + 3.0 * 0.044715 * square))) * chan
+
+        @pl.when(chunk >= 2)
+        def _():
+            store(chunk - 2, slot).wait()
+
+        mlp_buf[slot] = mm(hid_rows[here, :], unit_full[:, units:], ((1,), (1,))).astype(bf16)
+        store(chunk, slot).start()
+        cot_rows = jnp.concatenate([cot_buf[slot, at] for at in range(4)], axis=1).astype(f32)
+        grad_mlp = (cot_rows * mm(hot_keep[here, :], pieces[5], ((1,), (0,)))).astype(bf16)
+        gmlp_rows[here, :] = grad_mlp
+        mlp_sums[...] += jnp.sum(grad_mlp.astype(f32), axis=0, keepdims=True)
+        grad_up = (mm(gmlp_rows[here, :], unit_full[:, units:], ((1,), (0,))) * slope).astype(bf16)
+        gup_rows[here, :] = grad_up
+        up_bias_grad[...] += jnp.sum(grad_up.astype(f32), axis=0, keepdims=True)
+        two_part[here, :] = mm(gup_rows[here, :], unit_full[:, :units], ((1,), (1,))).astype(bf16)
+        twos.first(chunk)
+        pl.when(chunk >= 1)(lambda: twos.second(chunk - 1))
+        pl.when(chunk >= 2)(lambda: twos.third(chunk - 2))
+        return carry
+
+    lax.fori_loop(0, chunks, step, 0)
+    twos.second(chunks - 1)
+    third = width // 3
+
+    def grads(index, carry):
+        at = pl.ds(pl.multiple_of(index * third, 128), third)
+        unit_grads[at, :units] = mm(mod_rows[:, at], gup_rows[...], ((0,), (0,))).astype(bf16)
+        unit_grads[at, units:] = mm(gmlp_rows[:, at], hid_rows[...], ((0,), (0,))).astype(bf16)
+        pl.when(index == 1)(lambda: twos.third(chunks - 2))
+        return carry
+
+    lax.fori_loop(0, 3, grads, 0)
+    twos.third(chunks - 1)
+    for chunk in range(chunks):
+        twos.fourth(chunk)
+        twos.wait_send(chunk)
+        branch.wait_send(chunk)
+    store(chunks - 2, (chunks - 2) % 2).wait()
+    store(chunks - 1, (chunks - 1) % 2).wait()
+
+
+def feed(branch_part, token_blocks, cot_blocks, hot, hot_keep, pieces, out_bias, unit_full, up_bias, chan_rows):
+    rows, width = branch_part.shape
+    units = up_bias.shape[1]
+    local_width = token_blocks.shape[2]
+    chunks = 5
+    size = rows // chunks
+    dma = pltpu.SemaphoreType.DMA
+    vmem = pl.BlockSpec(memory_space=pltpu.VMEM)
+    anywhere = pl.BlockSpec(memory_space=pl.ANY)
+    low = lambda *shape: pltpu.VMEM(shape, bf16)
+    return pl.pallas_call(
+        feed_kernel,
+        out_shape=(
+            jax.ShapeDtypeStruct((rows, width), bf16),
+            jax.ShapeDtypeStruct((rows, width), bf16),
+            jax.ShapeDtypeStruct((rows, width), bf16),
+            jax.ShapeDtypeStruct((width, 2 * units), bf16),
+            jax.ShapeDtypeStruct((1, units), f32),
+            jax.ShapeDtypeStruct((1, width), f32),
+        ),
+        in_specs=[vmem, anywhere, anywhere] + [vmem] * 7,
+        out_specs=(vmem, anywhere, vmem, vmem, vmem, vmem),
+        scratch_shapes=[
+            low(2, 4, size, local_width),
+            low(2, 4, size, local_width),
+            low(rows, width),
+            low(rows, units),
+            low(rows, units),
+            low(rows, width),
+            low(rows, width),
+            low(2, size, width),
+            low(2, chunks, size // 2, width),
+            low(2, chunks, size // 2, width),
+            low(2, chunks, size // 2, width),
+            dma((2, 3, chunks)),
+            dma((2, 3, chunks)),
+            dma((2, 2)),
+            dma((2,)),
+        ],
+        compiler_params=pltpu.CompilerParams(collective_id=2, has_side_effects=True, vmem_limit_bytes=63 * 2**20),
+    )(branch_part, token_blocks, cot_blocks, hot, hot_keep, pieces, out_bias, unit_full, up_bias, chan_rows)
 
 
 def on_device(
@@ -594,37 +843,50 @@
         axis=1,
     )
     small_own = jnp.pad(small_own, ((0, slots - slot_count), (0, 0)))
+    bias_rows = jnp.concatenate(
+        [
+            jnp.broadcast_to(ada_bias.astype(f32).reshape(1, 6 * local_width), (slot_count, 6 * local_width)),
+            jnp.pad(out_bias.astype(f32)[None], ((0, slots - slot_count - 1), (0, 5 * local_width))),
+        ],
+        axis=0,
+    )
     head_shard = jnp.concatenate([qkv_weight.reshape(own_rows, 3 * local_width), out_weight.T], axis=1)
     unit_shard = jnp.concatenate([up_weight, down_weight.T], axis=1)
-    small_all, embedding, cond_own, mod_blocks, head_full, unit_full, token_blocks, cot_blocks = gather_all(
-        small_own, time_weight, ada_own, ada_bias.astype(f32).reshape(1, 6 * local_width), head_shard, unit_shard, tokens, cotangent, tok_count
+    small_all, embedding, cond_own, mod_full, pieces, head_full, unit_full, token_blocks, cot_blocks = gather_all(
+        small_own, time_weight, ada_own, bias_rows, head_shard, unit_shard, tokens, cotangent, tok_count
     )
     all_crops = tok_count * slots
     real_crop = (jnp.arange(all_crops, dtype=jnp.int32) % slots < slot_count)[:, None]
     step_feats = small_all[:, :, :freq_count].reshape(all_crops, freq_count)
     label_all = small_all[:, :, freq_count + local_width].reshape(all_crops).astype(jnp.int32)
     label_hot = ((label_all[:, None] == jnp.arange(class_table.shape[0], dtype=jnp.int32)[None, :]) & real_crop).astype(f32)
-    mod_full = jnp.concatenate(
-        [mod_blocks[at, :slot_count].reshape(slot_count, 6, local_width) for at in range(4)], axis=2
-    )
     tokens_full = jnp.concatenate([token_blocks[at] for at in range(4)], axis=1)
     cot_full = jnp.concatenate([cot_blocks[at] for at in range(4)], axis=1)
     qkv_full, out_full = head_full[:, : 3 * local_width], head_full[:, 3 * local_width :]
-    up_full, down_full = unit_full[:, :units_here], unit_full[:, units_here:]
-    out_bias_full = lax.all_gather(out_bias, "mdl", axis=0, tiled=True).astype(f32)
+    out_bias_full = mod_full[0, slot_count :slot_count + 1]
+    mod_rows = jnp.transpose(mod_full[:, :slot_count], (1, 0, 2))
 
     inside, segment = crop_layout(lengths, padding, row_len)
     crop_hot = inside[0].astype(bf16)
     crop_hot32 = inside[0].astype(f32)
 
     def spread(part):
-        return exact_dot(crop_hot32, mod_full[:, part])
+        return exact_dot(crop_hot32, mod_rows[:, part])
 
     head_tok = mm(crop_hot, head_mask[0].astype(bf16), ((1,), (0,)))
     head_units = jnp.repeat(head_tok, head_width, axis=1).astype(bf16)
     chan_tok = mm(crop_hot, chan_mask[0].astype(bf16), ((1,), (0,)))
     chan_units = jnp.repeat(chan_tok, units_here // groups_here, axis=1)
     keep_rows = keep_mask.astype(f32)[:, None]
+
+    hot_one = jnp.pad(crop_hot, ((0, 0), (0, slots - slot_count)))
+    hot = jnp.concatenate([hot_one] * 3 + [jnp.zeros_like(hot_one)], axis=1)
+    hot_keep = hot * keep_mask.astype(bf16)[:, None]
+
+    def rows32(rows_low):
+        return jnp.pad(rows_low, ((0, 4 * slots - slot_count), (0, 0)))
+
+    chan_rows = rows32(jnp.repeat(chan_mask[0].astype(bf16), units_here // groups_here, axis=1))
 
     start_rows = tokens_full.astype(f32)
     normed_one, inverse_one = norm_rows(start_rows)
@@ -642,33 +904,24 @@
         heads(queries), heads(key_rows), heads(value_rows), segment[0], score_scale
     )
     attended = (attend_now.reshape(row_len, local_width) * head_units.astype(f32)).astype(bf16)
-    branch_own = scatter_cols(mm(attended, out_full, ((1,), (1,))))
-    attn_branch = gather_cols(branch_own).astype(f32) + out_bias_full
+    branch_part = mm(attended, out_full, ((1,), (1,))).astype(bf16)
+    branch_low, mlp_part, two_low, unit_grads, grad_up_bias, mlp_sums = feed(
+        branch_part, token_blocks, cot_blocks, hot, hot_keep, pieces, out_bias_full, unit_full, up_bias.astype(f32)[None], chan_rows
+    )
+    grad_up_bias = grad_up_bias[0]
+    grad_down_bias = own_cols(mlp_sums)[0]
+    grad_units = lax.psum_scatter(unit_grads, "tok", scatter_dimension=0, tiled=True).astype(f32)
+    mlp_out = scatter_cols(mlp_part).astype(f32) + down_bias.astype(f32)
+    attn_branch = branch_low.astype(f32) + out_bias_full
     gate_one = spread(2)
     middle = start_rows + gate_one * attn_branch
     normed_two, inverse_two = norm_rows(middle)
     scale_two = spread(4)
-    modulated_two = (normed_two * (1.0 + scale_two) + spread(3)).astype(bf16)
-    up_pre = mm(modulated_two, up_full, ((1,), (0,))) + up_bias.astype(f32)
-    gelu_values, gelu_back = jax.vjp(lambda pre: jax.nn.gelu(pre, approximate=True), up_pre)
-    hidden = (gelu_values * chan_units).astype(bf16)
-    mlp_out = scatter_cols(mm(hidden, down_full, ((1,), (1,)))).astype(f32) + down_bias.astype(f32)
     gate_two = spread(5)
     output = (own_cols(middle) + own_cols(gate_two) * keep_rows * mlp_out).astype(bf16)
-
     grad_rows = cot_full.astype(f32)
-    grad_mlp = (grad_rows * gate_two * keep_rows).astype(bf16)
-    grad_hidden = mm(grad_mlp, down_full, ((1,), (0,)))
-    grad_down = mm(grad_mlp, hidden, ((0,), (0,)))
-    grad_down_bias = jnp.sum(own_cols(grad_mlp).astype(f32), axis=0)
-    grad_up_pre = gelu_back(grad_hidden * chan_units)[0].astype(bf16)
-    grad_up = mm(modulated_two, grad_up_pre, ((0,), (0,)))
-    grad_up_bias = jnp.sum(grad_up_pre.astype(f32), axis=0)
-    grad_units = lax.psum_scatter(
-        jnp.concatenate([grad_up, grad_down], axis=1).astype(bf16), "tok", scatter_dimension=0, tiled=True
-    ).astype(f32)
-    two_own = scatter_cols(mm(grad_up_pre, up_full, ((1,), (1,))))
-    grad_two = gather_cols(two_own).astype(f32)
+    grad_two = two_low.astype(f32)
+    two_own = own_cols(two_low)
 
     def norm_back(grad_norm, normed, inverse):
         return inverse * (

time: 751 us -> 698 us (0.929)
  Pallas kernels: 137 us -> 219 us
  matrix products: 183 us -> 135 us
  waiting for transfers between devices: 175 us -> 141 us
  local copies, waits for them, and re-layouts: 114 us -> 82.7 us
  other arithmetic: 97.3 us -> 84.1 us
    pallas_call x0 -> x1, Pallas kernels: none -> 77.7 us  [feed(): pl.pallas_call(feed_kernel, out_shape=(jax.ShapeDtypeStruct((rows, width)...]
    unnamed x14 -> x7, waiting for transfers between devices: 175 us -> 112 us
    dot_general x15 -> x8, matrix products: 65 us -> 24.5 us  [mm(): lax.dot_general(left, right, (dims, ((), ())), preferred_element_type=f32)]
    reduce_scatter x0 -> x1, waiting for transfers between devices: none -> 28.8 us  [on_device(): lax.psum_scatter(unit_grads, 'tok', scatter_dimension=0, tiled=True)]
    unnamed x127 -> x114, local copies, waits for them, and re-layouts: 51.1 us -> 35.3 us
    all_gather x2 -> x0, local copies, waits for them, and re-layouts: 10.9 us -> none  [gather_cols(): return lax.all_gather(rows_low, 'mdl', axis=1, tiled=True)]
    reduce_sum x2 -> x0, other arithmetic: 9.49 us -> none  [the longest x1 7.46 us: norm_back(): jnp.mean(grad_norm, axis=1, keepdims=True)]
    reshape x2 -> x1, local copies, waits for them, and re-layouts: 8.63 us -> 0.09 us  [on_device(): jnp.repeat(chan_mask[0].astype(bf16), units_here // groups_here, axis=1)]
  transfers between devices with their start and end apart: 8 -> 4, of which waited for: 5 -> 4; matrix products, arithmetic and copies ran while one was open for 30% -> 12% of each run, Pallas kernels for 0% -> 4%
where the time goes in v3:
time: 698 us; the launch traced here: 687 us
  Pallas kernels  219 us (31%)
  waiting for transfers between devices  141 us (20%)
  matrix products  135 us (19%)
  other arithmetic  84.1 us (12%)
  local copies, waits for them, and re-layouts  82.7 us (12%)
  between operations  15.1 us (2%)
  blocking collectives  10.8 us (2%)
    pallas_call x1, Pallas kernels, gather_all(): pl.pallas_call(gather_kernel, out_shape=(jax.ShapeDtypeStruct((tok_count,...  115 us
    unnamed x7, waiting for transfers between devices  112 us
    pallas_call x1, Pallas kernels, feed(): pl.pallas_call(feed_kernel, out_shape=(jax.ShapeDtypeStruct((rows, width)...  77.7 us
    unnamed x114, local copies, waits for them, and re-layouts  35.3 us
    dot_general x7, matrix products, exact_dot(): jnp.dot(left, right, precision=lax.Precision.HIGHEST, preferred_element_t...  34.5 us
    reduce_scatter x1, waiting for transfers between devices, on_device(): lax.psum_scatter(unit_grads, 'tok', scatter_dimension=0, tiled=True)  28.8 us
    pallas_call x1, Pallas kernels, cond_back(): pl.pallas_call(cond_back_kernel, out_shape=(jax.ShapeDtypeStruct((tok_cou...  26.1 us
    dot_general x8, matrix products, mm(): lax.dot_general(left, right, (dims, ((), ())), preferred_element_type=f32)  24.5 us
  transfers between devices with their start and end apart: 4, of which 4 were waited for; matrix products, arithmetic and copies ran while one was open for 12% of the time, Pallas kernels for 4%

profile of v3, /device:TPU:0, one launch (start us, length us, event | category | flops | bytes accessed | tf_op | source)
XLA Modules:
  0.0 687.5 jit_solution(15095703849149329054)
XLA Ops:
  21.5 115.0 %shard_map.308 = (f32[8,8,640]{2,1,0:T(8,128)S(1)}, f32[64,288]{1,0:T(8,128)S(1)}, bf16[64,144]{1,0:T(8,128)(2,1)S(1)}, f32[6,8,1152]{2,1,0:T(8,128)S(1)}, bf16[...) custom-call(f32[8,640]{1,0:T(8,128)S(1)} %select_maximum_fusion.smal, ...), custom_call_target="tpu_custom_call" | custom-call | tf_op jit(solution)/shard_map/pallas_call | solution.py:408
  153.6 5.9 concatenate.41
  167.6 5.1 fusion.8
  178.4 11.2 %fusion.61 = (f32[4,1280]{1,0:T(4,128)S(1)}, f32[4,1280,1280]{1,2,0:T(8,128)}) fusion(bf16[1280,4,72]{0,2,1:T(8,128)(2,1)S(1)} %bitcast.125, bf16[1280,4,72]{0,2,1:T(8,128)(2,1)S(1)} %bitcast.131, pred[1280,1280]{0,1:T(8,128)(4,1)S(1)} %copy-done.29), kind=kOutput, calls=%fused_computation.159 | convolution fusion | flops 963374080 | bytes 29347840 | tf_op jit(solution)/shard_map/qhd,khd->hqk/dot_general | solution.py:59
  189.6 10.6 %fusion.1 = f32[4,1280]{1,0:T(4,128)S(1)} fusion(f32[4,1280,1280]{1,2,0:T(8,128)} %get-tuple-element.170, f32[4,1280]{1,0:T(4,128)S(1)} %get-tuple-element.169), kind=kLoop, calls=%fused_computation.7 | loop fusion | flops 13102080 | bytes 26255360 | tf_op jit(solution)/shard_map/reduce_sum | solution.py:64
  200.2 10.8 %fusion.6 = f32[4,72,1280]{2,1,0:T(8,128)S(1)} fusion(bf16[1280,4,72]{0,2,1:T(8,128)(2,1)S(1)} %bitcast.123, f32[4,1280,1280]{1,2,0:T(8,128)} %get-tuple-element.170, f32[4,1280]{1,0:T(4,128)S(1)} %fusion.1, f32[4,1280]{1,0:T(4,128)S(1)} %get-tuple-element.169), kind=kOutput, calls=%fused_computation.11 | convolution fusion | flops 963379200 | bytes 28467200 | tf_op jit(solution)/shard_map/hqk,khd->qhd/dot_general | solution.py:66
  215.8 77.7 %shard_map.309 = (bf16[1280,1152]{1,0:T(8,128)(2,1)}, bf16[1280,1152]{1,0:T(8,128)(2,1)}, bf16[1280,1152]{1,0:T(8,128)(2,1)}, bf16[1152,2304]{1,0:T(8,128)(2,1)}, f32[1,1152]{1,0:T(1,128)}, /*index=5*/f32[1,1152]{1,0:T(1,128)}) custom-call(bf16[1280,1152]{1,0:T(8,128)(2,1)} %convolution_convert_fusion.1.branch_part, bf16[4,1280,288]{2,1,0:T(8,128)(2,1)} %copy-done.2, ...), custom_call_target="tpu_custom_call" | custom-call | tf_op jit(solution)/shard_map/pallas_call | solution.py:759
  293.5 10.9 %multiply_reduce_fusion.2 = (f32[1280]{0:T(1024)S(1)}, f32[1280]{0:T(1024)S(1)}, f32[1280,1152]{1,0:T(8,128)S(1)}, f32[1280,1152]{1,0:T(8,128)}, f32[1280,1152]{1,0:T(8,128)}, /*index=5*/f32[1280,1152]{1,0:T(8,128)}) fusion(f32[1152]{0:T(1024)S(1)} %copy-done.40, bf16[1280,1152]{1,0:T(8,128)(2,1)} %get-tuple-element.38, bf16[1280,1152]{1,0:T(8,128)(2,1)} %copy-done.12, ...), kind=kOutput, calls=%fused_computation.29 | convolution fusion | flops 120934400 | bytes 29563904 | tf_op jit(solution)/shard_map/dot_general | solution.py:17
  304.5 8.1 %fusion.57 = (f32[1280]{0:T(1024)S(1)}, f32[1280]{0:T(1024)S(1)}, f32[1280,1152]{1,0:T(8,128)}, f32[1280,1152]{1,0:T(8,128)}) fusion(f32[1280]{0:T(1024)S(1)} %get-tuple-element.158, f32[1280,1152]{1,0:T(8,128)S(1)} %get-tuple-element.135, f32[1280]{0:T(1024)S(1)} %get-tuple-element.157, f32[6,6,1152]{2,0,1:T(8,128)S(1)} %copy-done.30, ...), kind=kOutput, calls=%fused_computation.155 | convolution fusion | flops 117985280 | bytes 20708352 | tf_op jit(solution)/shard_map/dot_general | solution.py:17
  312.6 5.9 concatenate.43
  318.5 9.9 %multiply_convert_fusion.1 = (bf16[1280,1152]{1,0:T(8,128)(2,1)S(1)}, f32[1280,1152]{1,0:T(8,128)}) fusion(f32[1280,1152]{1,0:T(8,128)} %get-tuple-element.171, f32[1280,1152]{1,0:T(8,128)} %get-tuple-element.134, f32[1280]{0:T(1024)S(1)} %get-tuple-element.175, f32[1280,1152]{1,0:T(8,128)} %get-tuple-element.172, f32[1280]{0:T(1024)S(1)} %get-tuple-element.176, ...), kind=kLoop, calls=%fused_computation.25 | loop fusion | flops 11796480 | bytes 29506560 | tf_op jit(solution)/shard_map/convert_element_type | solution.py:934
  333.7 13.7 %fusion.14 = bf16[4,72,1280]{2,1,0:T(8,128)(2,1)} fusion(bf16[1280,4,72]{0,2,1:T(8,128)(2,1)} %bitcast.121, f32[4,1280,1280]{1,2,0:T(8,128)} %get-tuple-element.170, f32[4,1280]{1,0:T(4,128)S(1)} %log_add_fusion), kind=kOutput, calls=%fused_computation.39 | convolution fusion | flops 957194240 | bytes 27709440 | tf_op jit(solution)/shard_map/hqk,qhd->khd/dot_general | solution.py:80
  347.4 17.0 %multiply_reduce_fusion = (f32[4,1280]{1,0:T(4,128)S(1)}, f32[4,1280,1280]{1,2,0:T(8,128)}) fusion(f32[4,1280,1280]{1,2,0:T(8,128)} %get-tuple-element.170, f32[4,1280]{1,0:T(4,128)S(1)} %log_add_fusion, bf16[1280,4,72]{0,2,1:T(8,128)(2,1)} %bitcast.122, bf16[1280,4,72]{0,2,1:T(8,128)(2,1)} %bitcast.124), kind=kOutput, calls=%fused_computation.3 | convolution fusion | flops 963374080 | bytes 53944320 | tf_op jit(solution)/shard_map/qhd,khd->hqk/dot_general | solution.py:75
  364.3 22.1 %multiply_convert_fusion = bf16[4,1280,1280]{1,2,0:T(8,128)(2,1)} fusion(f32[4,1280,1280]{1,2,0:T(8,128)} %get-tuple-element.174, f32[4,1280,1280]{1,2,0:T(8,128)} %get-tuple-element.170, f32[4,1280]{1,0:T(4,128)S(1)} %get-tuple-element.173, f32[4,1280]{1,0:T(4,128)S(1)} %log_add_fusion), kind=kLoop, calls=%fused_computation.2 | loop fusion | flops 26214400 | bytes 65576960 | tf_op jit(solution)/shard_map/convert_element_type | solution.py:77
  386.5 8.8 %fusion.13 = bf16[4,72,1280]{2,1,0:T(8,128)(2,1)S(1)} fusion(bf16[1280,4,72]{0,2,1:T(8,128)(2,1)S(1)} %bitcast.126, bf16[4,1280,1280]{1,2,0:T(8,128)(2,1)} %multiply_convert_fusion), kind=kOutput, calls=%fused_computation.38 | convolution fusion | flops 944455680 | bytes 14581760 | tf_op jit(solution)/shard_map/hqk,qhd->khd/dot_general | solution.py:79
  395.3 7.4 %fusion.12 = bf16[4,72,1280]{2,1,0:T(8,128)(2,1)S(1)} fusion(bf16[1280,4,72]{0,2,1:T(8,128)(2,1)S(1)} %bitcast.132, bf16[4,1280,1280]{1,2,0:T(8,128)(2,1)} %multiply_convert_fusion), kind=kOutput, calls=%fused_computation.37 | convolution fusion | flops 944455680 | bytes 14581760 | tf_op jit(solution)/shard_map/hqk,khd->qhd/dot_general | solution.py:78
  402.8 4.6 convolution_convert_fusion.2
  409.1 5.3 copy.164
  414.5 5.5 copy.160
  420.0 6.3 fusion.9
  440.1 4.9 fusion.35
  445.0 39.6 %reduce-scatter.17.cloned.1.call-done = bf16[144,1152]{1,0:T(8,128)(2,1)} async-done(((bf16[1152,1152]{1,0:T(8,128)(2,1)}), bf16[144,1152]{1,0:T(8,128)(2,1)}) %reduce-scatter.17.cloned.1.call-update) | async-done | bytes 331792
  488.1 35.2 %reduce-scatter.13.cloned.1.call-done = bf16[288,1280]{1,0:T(8,128)(2,1)} async-done(((bf16[1152,1280]{1,0:T(8,128)(2,1)}), bf16[288,1280]{1,0:T(8,128)(2,1)}) %reduce-scatter.13.cloned.1.call-update) | async-done | bytes 737296
  525.4 37.1 %reduce-scatter.15.cloned.1.call-done = bf16[288,1280]{1,0:T(8,128)(2,1)} async-done(((bf16[1152,1280]{1,0:T(8,128)(2,1)}), bf16[288,1280]{1,0:T(8,128)(2,1)}) %reduce-scatter.15.cloned.1.call-update) | async-done | bytes 737296
  564.2 5.1 fusion.26
  569.3 10.8 %psum.7 = f32[2,1280]{1,0:T(2,128)S(1)} all-reduce(f32[2,1280]{1,0:T(2,128)S(1)} %pad_maximum_fusion.6), channel_id=1, replica_groups=mesh['tok'=8,'mdl'=4] {'mdl'}, use_global_device_ids=true, to_apply=%region_15.16 | all-reduce | flops 2560 | bytes 20480 | tf_op jit(solution)/shard_map/psum | solution.py:953
  580.2 4.8 multiply_multiply_fusion
  585.0 6.8 dynamic-slice_multiply_fusion.1
  591.8 11.6 %concatenate.46 = f32[1280,1728]{1,0:T(8,128)} concatenate(bf16[1280,288]{1,0:T(8,128)(2,1)S(1)} %copy.163, f32[1280,288]{1,0:T(8,128)} %get-tuple-element.136, f32[1280,288]{1,0:T(8,128)} %get-tuple-element.137, f32[1280,288]{1,0:T(8,128)} %dynamic-slice_convert_fusion, f32[1280,288]{1,0:T(8,128)} %dynamic-slice_multiply_fusion, f32[1280,288]{1,0:T(8,128)} %get-tuple-element.151), dimensions={1} | concatenate | bytes 16957440 | tf_op jit(solution)/shard_map/concatenate | solution.py:961
  603.4 6.7 fusion.49
  610.1 26.1 %shard_map.310 = (f32[8,8,1728]{2,1,0:T(8,128)S(1)}, f32[144,1728]{1,0:T(8,128)S(1)}, f32[64,288]{1,0:T(8,128)S(1)}) custom-call(f32[8,1728]{1,0:T(8,128)S(1)} %pad_maximum_fusion.5.gmod_own, bf16[144,1728]{1,0:T(8,128)(2,1)S(1)} %copy-done.6, bf16[64,144]{1,0:T(8,128)(2,1)S(1)} %get-tuple-element.43.cond_own, f32[64,288]{1,0:T(8,128)S(1)} %get-tuple-element.44.embedding), custom_call_target="tpu_custom_call" | custom-call | tf_op jit(solution)/shard_map/pallas_call | solution.py:528
  647.8 28.8 %reduce-scatter.11.cloned.1.call-done = bf16[144,2304]{1,0:T(8,128)(2,1)} async-done(((bf16[1152,2304]{1,0:T(8,128)(2,1)}), bf16[144,2304]{1,0:T(8,128)(2,1)}) %reduce-scatter.11.cloned.1.call-update) | async-done | bytes 663568 | tf_op jit(solution)/shard_map/reduce_scatter | solution.py:913
  (218 shorter events, 93.2 us)
Async XLA Ops:
  7.2 11.9 %copy-start = (bf16[1000,288]{0,1:T(8,128)(2,1)S(1)}, bf16[1000,288]{0,1:T(8,128)(2,1)}, u32[]{:S(2)}) copy-start(bf16[1000,288]{0,1:T(8,128)(2,1)} %param.41) | copy-start | bytes 1728004
  7.2 8.5 %copy-start.33 = (bf16[1280,288]{0,1:T(8,128)(2,1)S(1)}, bf16[1280,288]{0,1:T(8,128)(2,1)}, u32[]{:S(2)}) copy-start(bf16[1280,288]{0,1:T(8,128)(2,1)} %param.22) | copy-start | bytes 2211844
  7.2 477.4 %reduce-scatter.17.cloned.1.call-start = ((), (), s32[]{:S(2)}) async-start(), calls=%async_computation.7 | async-start | bytes 2985984
  15.7 120.8 %copy-start.5 = (bf16[144,1728]{1,0:T(8,128)(2,1)}, bf16[144,1728]{1,0:T(8,128)(2,1)S(1)}, u32[]{:S(2)}) copy-start(bf16[144,1728]{1,0:T(8,128)(2,1)S(1)} %reshape.573.ada_own) | copy-start | bytes 1492996
  16.4 120.1 %copy-start.3 = (bf16[1280,288]{1,0:T(8,128)(2,1)}, bf16[1280,288]{1,0:T(8,128)(2,1)S(1)}, u32[]{:S(2)}) copy-start(bf16[1280,288]{1,0:T(8,128)(2,1)S(1)} %copy.130.cotangent) | copy-start | bytes 2211844
  16.4 126.2 %copy-start.46 = (s32[1,6,4]{1,2,0:T(4,128)S(1)}, s32[1,6,4]{1,2,0:T(4,128)}, u32[]{:S(2)}) copy-start(s32[1,6,4]{1,2,0:T(4,128)} %param.28) | copy-start | bytes 292
  16.4 126.3 %copy-start.47 = (bf16[2,288]{1,0:T(2,128)(2,1)S(1)}, bf16[2,288]{1,0:T(2,128)(2,1)}, u32[]{:S(2)}) copy-start(bf16[2,288]{1,0:T(2,128)(2,1)} %param.31) | copy-start | bytes 3460
  16.4 126.3 %copy-start.44 = (bf16[1152]{0:T(1024)(128)(2,1)S(1)}, bf16[1152]{0:T(1024)(128)(2,1)}, u32[]{:S(2)}) copy-start(bf16[1152]{0:T(1024)(128)(2,1)} %param.35) | copy-start | bytes 6916
  18.3 126.4 %copy-start.42 = (s32[1280]{0:T(1024)S(1)}, s32[1280]{0:T(1024)}, u32[]{:S(2)}) copy-start(s32[1280]{0:T(1024)} %param.29) | copy-start | bytes 15364
  159.5 8.1 %copy-start.12 = (bf16[1280,1152]{1,0:T(8,128)(2,1)}, bf16[1280,1152]{1,0:T(8,128)(2,1)S(1)}, u32[]{:S(2)}) copy-start(bf16[1280,1152]{1,0:T(8,128)(2,1)S(1)} %concatenate.41) | copy-start | bytes 8847364
  176.2 13.3 %copy-start.22 = (bf16[1280,288]{0,1:T(8,128)(2,1)}, bf16[1280,288]{0,1:T(8,128)(2,1)S(1)}, u32[]{:S(2)}) copy-start(bf16[1280,288]{0,1:T(8,128)(2,1)S(1)} %slice.226) | copy-start | bytes 2211844
  176.5 13.1 %copy-start.19 = (bf16[1280,288]{0,1:T(8,128)(2,1)}, bf16[1280,288]{0,1:T(8,128)(2,1)S(1)}, u32[]{:S(2)}) copy-start(bf16[1280,288]{0,1:T(8,128)(2,1)S(1)} %get-tuple-element.139) | copy-start | bytes 2211844
  176.5 23.7 %copy-start.18 = (bf16[1280,288]{0,1:T(8,128)(2,1)}, bf16[1280,288]{0,1:T(8,128)(2,1)S(1)}, u32[]{:S(2)}) copy-start(bf16[1280,288]{0,1:T(8,128)(2,1)S(1)} %get-tuple-element.140) | copy-start | bytes 2211844
  200.2 10.8 %copy-start.37 = (bf16[1280,4]{0,1:T(4,128)(2,1)S(1)}, bf16[1280,4]{0,1:T(4,128)(2,1)}, u32[]{:S(2)}) copy-start(bf16[1280,4]{0,1:T(4,128)(2,1)} %convolution_convert_fusion.5) | copy-start | bytes 30724
  215.8 77.7 %copy-start.40 = (f32[1152]{0:T(1024)S(1)}, f32[1152]{0:T(1024)}, u32[]{:S(2)}) copy-start(f32[1152]{0:T(1024)} %get-tuple-element.153) | copy-start | bytes 13828
  293.5 10.9 %copy-start.15 = (bf16[1280,1152]{1,0:T(8,128)(2,1)S(1)}, bf16[1280,1152]{1,0:T(8,128)(2,1)}, u32[]{:S(2)}) copy-start(bf16[1280,1152]{1,0:T(8,128)(2,1)} %get-tuple-element.40) | copy-start | bytes 8847364
  304.5 8.1 %copy-start.14 = (f32[1280,1152]{1,0:T(8,128)}, f32[1280,1152]{1,0:T(8,128)S(1)}, u32[]{:S(2)}) copy-start(f32[1280,1152]{1,0:T(8,128)S(1)} %get-tuple-element.135) | copy-start | bytes 17694724
  318.5 9.9 %copy-start.32 = (bf16[1280,288]{0,1:T(8,128)(2,1)S(1)}, bf16[1280,288]{0,1:T(8,128)(2,1)}, u32[]{:S(2)}) copy-start(bf16[1280,288]{0,1:T(8,128)(2,1)} %copy-done.31) | copy-start | bytes 2211844
  364.3 22.1 %copy-start.20 = (bf16[1280,288]{0,1:T(8,128)(2,1)S(1)}, bf16[1280,288]{0,1:T(8,128)(2,1)}, u32[]{:S(2)}) copy-start(bf16[1280,288]{0,1:T(8,128)(2,1)} %copy-done.19) | copy-start | bytes 2211844
  386.5 8.8 %copy-start.23 = (bf16[1280,288]{0,1:T(8,128)(2,1)S(1)}, bf16[1280,288]{0,1:T(8,128)(2,1)}, u32[]{:S(2)}) copy-start(bf16[1280,288]{0,1:T(8,128)(2,1)} %copy-done.22) | copy-start | bytes 2211844
  395.3 7.4 %copy-start.21 = (bf16[4,72,1280]{2,1,0:T(8,128)(2,1)}, bf16[4,72,1280]{2,1,0:T(8,128)(2,1)S(1)}, u32[]{:S(2)}) copy-start(bf16[4,72,1280]{2,1,0:T(8,128)(2,1)S(1)} %fusion.13) | copy-start | bytes 2211844
  395.3 7.4 %copy-start.24 = (bf16[4,72,1280]{2,1,0:T(8,128)(2,1)S(1)}, bf16[4,72,1280]{2,1,0:T(8,128)(2,1)}, u32[]{:S(2)}) copy-start(bf16[4,72,1280]{2,1,0:T(8,128)(2,1)} %fusion.14) | copy-start | bytes 2211844
  395.3 7.4 %copy-start.27 = (bf16[1280,1152]{1,0:T(8,128)(2,1)S(1)}, bf16[1280,1152]{1,0:T(8,128)(2,1)}, u32[]{:S(2)}) copy-start(bf16[1280,1152]{1,0:T(8,128)(2,1)} %copy-done.26) | copy-start | bytes 8847364
  414.4 108.8 %reduce-scatter.13.cloned.1.call-start = ((), (), s32[]{:S(2)}) async-start(), calls=%async_computation.5 | async-start | bytes 3686400
  420.0 142.6 %reduce-scatter.15.cloned.1.call-start = ((), (), s32[]{:S(2)}) async-start(), calls=%async_computation.6 | async-start | bytes 3686400
  426.3 250.2 %reduce-scatter.11.cloned.1.call-start = ((), (), s32[]{:S(2)}) async-start(), calls=%async_computation.4 | async-start | bytes 5971968 | tf_op jit(solution)/shard_map/reduce_scatter | solution.py:913
  426.6 7.9 %copy-start.16 = (bf16[1280,1152]{1,0:T(8,128)(2,1)S(1)}, bf16[1280,1152]{1,0:T(8,128)(2,1)}, u32[]{:S(2)}) copy-start(bf16[1280,1152]{1,0:T(8,128)(2,1)} %get-tuple-element.40) | copy-start | bytes 8847364
  562.5 17.6 %copy-start.4 = (bf16[1280,288]{1,0:T(8,128)(2,1)S(1)}, bf16[1280,288]{1,0:T(8,128)(2,1)}, u32[]{:S(2)}) copy-start(bf16[1280,288]{1,0:T(8,128)(2,1)} %copy-done.3) | copy-start | bytes 2211844
  562.6 17.6 %copy-start.39 = (f32[1280]{0:T(1024)S(1)}, f32[1280]{0:T(1024)}, u32[]{:S(2)}) copy-start(f32[1280]{0:T(1024)} %get-tuple-element.159) | copy-start | bytes 15364
  562.6 17.6 %copy-start.41 = (f32[288]{0:T(512)S(1)}, f32[288]{0:T(512)}, u32[]{:S(2)}) copy-start(f32[288]{0:T(512)} %convert_element_type.201) | copy-start | bytes 3460
  603.4 6.7 copy-start.6
  641.7 38.7 %copy-start.1 = (bf16[1000,288]{0,1:T(8,128)(2,1)S(1)}, bf16[1000,288]{0,1:T(8,128)(2,1)}, u32[]{:S(2)}) copy-start(bf16[1000,288]{0,1:T(8,128)(2,1)} %param.41) | copy-start | bytes 1728004
  (22 other events, 81.9 us)
Sparse Core Ops, SparseCore 0:
  414.5 70.0 reduce-scatter.16
  487.4 35.8 reduce-scatter.12
  525.8 36.7 reduce-scatter.14
  566.4 110.0 reduce-scatter.10

commit v4 on v3

--- a/solution.py
+++ b/solution.py
@@ -650,6 +650,7 @@
     chunks = near_in.shape[1]
     size = rows // chunks
     units = up_bias.shape[1]
+    local_width = token_blocks.shape[2]
     greet_quad(mdl_at)
     branch = RowReduce(mdl_at, branch_part, near_in.at[0], own_sum.at[0], far_in.at[0], branch_full, sends.at[0], recvs.at[0])
     twos = RowReduce(mdl_at, two_part, near_in.at[1], own_sum.at[1], far_in.at[1], two_full, sends.at[1], recvs.at[1])
@@ -664,7 +665,7 @@
         )
 
     def store(chunk, slot):
-        return pltpu.make_async_copy(mlp_buf.at[slot], mlp_part.at[span(chunk), :], store_sems.at[slot])
+        return pltpu.make_async_copy(mlp_buf.at[slot], mlp_part.at[:, span(chunk), :], store_sems.at[slot])
 
     for chunk in range(chunks):
         branch.first(chunk)
@@ -710,7 +711,9 @@
         def _():
             store(chunk - 2, slot).wait()
 
-        mlp_buf[slot] = mm(hid_rows[here, :], unit_full[:, units:], ((1,), (1,))).astype(bf16)
+        mlp_rows = mm(hid_rows[here, :], unit_full[:, units:], ((1,), (1,))).astype(bf16)
+        for at in range(4):
+            mlp_buf[slot, at] = mlp_rows[:, at * local_width : (at + 1) * local_width]
         store(chunk, slot).start()
         cot_rows = jnp.concatenate([cot_buf[slot, at] for at in range(4)], axis=1).astype(f32)
         grad_mlp = (cot_rows * mm(hot_keep[here, :], pieces[5], ((1,), (0,)))).astype(bf16)
@@ -760,7 +763,7 @@
         feed_kernel,
         out_shape=(
             jax.ShapeDtypeStruct((rows, width), bf16),
-            jax.ShapeDtypeStruct((rows, width), bf16),
+            jax.ShapeDtypeStruct((4, rows, local_width), bf16),
             jax.ShapeDtypeStruct((rows, width), bf16),
             jax.ShapeDtypeStruct((width, 2 * units), bf16),
             jax.ShapeDtypeStruct((1, units), f32),
@@ -776,7 +779,7 @@
             low(rows, units),
             low(rows, width),
             low(rows, width),
-            low(2, size, width),
+            low(2, 4, size, local_width),
             low(2, chunks, size // 2, width),
             low(2, chunks, size // 2, width),
             low(2, chunks, size // 2, width),
@@ -787,6 +790,425 @@
         ],
         compiler_params=pltpu.CompilerParams(collective_id=2, has_side_effects=True, vmem_limit_bytes=63 * 2**20),
     )(branch_part, token_blocks, cot_blocks, hot, hot_keep, pieces, out_bias, unit_full, up_bias, chan_rows)
+
+
+class ColumnReduce:
+    def __init__(self, mdl_at, source, own_part, far_part, near_in, far_out, far_in, sends, recvs, size):
+        self.source, self.own_part, self.far_part = source, own_part, far_part
+        self.near_in, self.far_out, self.far_in = near_in, far_out, far_in
+        self.sends, self.recvs, self.size = sends, recvs, size
+        self.near_at = mdl_at + 1 - 2 * lax.rem(mdl_at, 2)
+        self.near_far = lax.rem(self.near_at + 2, 4)
+        self.near = peer(mdl=self.near_at)
+        self.far = peer(mdl=lax.rem(mdl_at + 2, 4))
+
+    def rows(self, chunk):
+        return pl.ds(pl.multiple_of(chunk * self.size, 128), self.size)
+
+    def near_copy(self, chunk, which):
+        block = self.near_far if which else self.near_at
+        return remote(
+            self.source.at[block, self.rows(chunk), :],
+            self.near_in.at[which, self.rows(chunk), :],
+            self.sends.at[which, chunk],
+            self.recvs.at[which, chunk],
+            self.near,
+        )
+
+    def far_copy(self, chunk):
+        here = self.rows(chunk)
+        return remote(self.far_out.at[here, :], self.far_in.at[here, :], self.sends.at[2, chunk], self.recvs.at[2, chunk], self.far)
+
+    def first(self, chunk):
+        self.near_copy(chunk, 1).start()
+        self.near_copy(chunk, 0).start()
+
+    def second(self, chunk):
+        here = self.rows(chunk)
+        self.near_copy(chunk, 1).wait_recv()
+        self.far_out[here, :] = (self.far_part[here, :].astype(f32) + self.near_in[1, here, :].astype(f32)).astype(bf16)
+        self.far_copy(chunk).start()
+
+    def third(self, chunk):
+        here = self.rows(chunk)
+        self.near_copy(chunk, 0).wait_recv()
+        self.far_copy(chunk).wait_recv()
+        return self.own_part[here, :].astype(f32) + self.near_in[0, here, :].astype(f32) + self.far_in[here, :].astype(f32)
+
+    def wait_send(self, chunk):
+        self.near_copy(chunk, 1).wait_send()
+        self.near_copy(chunk, 0).wait_send()
+        self.far_copy(chunk).wait_send()
+
+
+class LineScatter:
+    def __init__(self, tok_at, grads, columns, cross_in, sums, above, below, sends, recvs, rows):
+        self.tok_at, self.grads, self.columns, self.rows = tok_at, grads, columns, rows
+        self.cross_in, self.sums, self.above, self.below = cross_in, sums, above, below
+        self.sends, self.recvs = sends, recvs
+        self.line = lax.div(tok_at, 2)
+        self.side = lax.rem(tok_at, 2)
+
+    def shard(self, owner):
+        return self.grads.at[pl.ds(pl.multiple_of(owner * self.rows, 16), self.rows), self.columns]
+
+    def cross_copy(self, place):
+        return remote(
+            self.shard(2 * place + 1 - self.side),
+            self.cross_in.at[place],
+            self.sends.at[0, place],
+            self.recvs.at[0, place],
+            peer(tok=self.tok_at + 1 - 2 * self.side),
+        )
+
+    def down_copy(self, place):
+        return remote(
+            self.sums.at[place], self.above.at[place], self.sends.at[1, place], self.recvs.at[1, place], peer(tok=self.tok_at - 2)
+        )
+
+    def up_copy(self, place):
+        return remote(
+            self.sums.at[place], self.below.at[place], self.sends.at[1, place], self.recvs.at[2, place], peer(tok=self.tok_at + 2)
+        )
+
+    def start(self, places=(0, 3, 1, 2)):
+        for place in places:
+            self.cross_copy(place).start()
+
+    def fold(self, place):
+        self.cross_copy(place).wait_recv()
+        own = self.shard(2 * place + self.side)[...].astype(f32)
+        self.sums[place] = (own + self.cross_in[place].astype(f32)).astype(bf16)
+
+    def pass_on(self, place):
+        @pl.when(self.line > place)
+        def _():
+            @pl.when(self.line < 3)
+            def _():
+                self.down_copy(place).wait_recv()
+                self.sums[place] = (self.sums[place].astype(f32) + self.above[place].astype(f32)).astype(bf16)
+
+            self.down_copy(place).start()
+
+        @pl.when(self.line < place)
+        def _():
+            @pl.when(self.line > 0)
+            def _():
+                self.up_copy(place).wait_recv()
+                self.sums[place] = (self.sums[place].astype(f32) + self.below[place].astype(f32)).astype(bf16)
+
+            self.up_copy(place).start()
+
+    def finish(self, out):
+        own = self.line
+        out[...] = self.sums[own].astype(f32)
+
+        @pl.when(self.line < 3)
+        def _():
+            self.down_copy(own).wait_recv()
+            out[...] += self.above[own].astype(f32)
+
+        @pl.when(self.line > 0)
+        def _():
+            self.up_copy(own).wait_recv()
+            out[...] += self.below[own].astype(f32)
+
+    def wait_send(self):
+        for place in range(4):
+            self.cross_copy(place).wait_send()
+            pl.when(self.line > place)(lambda: self.down_copy(place).wait_send())
+            pl.when(self.line < place)(lambda: self.up_copy(place).wait_send())
+
+
+def greet_line(tok_at, mdl_at):
+    line, side = lax.div(tok_at, 2), lax.rem(tok_at, 2)
+    barrier = pltpu.get_barrier_semaphore()
+    mesh_id = pl.DeviceIdType.MESH
+    pl.semaphore_signal(barrier, inc=1, device_id=peer(tok=tok_at + 1 - 2 * side), device_id_type=mesh_id)
+    for step in range(1, 4):
+        pl.semaphore_signal(barrier, inc=1, device_id=peer(mdl=lax.rem(mdl_at + step, 4)), device_id_type=mesh_id)
+
+    @pl.when(line > 0)
+    def _():
+        pl.semaphore_signal(barrier, inc=1, device_id=peer(tok=tok_at - 2), device_id_type=mesh_id)
+
+    @pl.when(line < 3)
+    def _():
+        pl.semaphore_signal(barrier, inc=1, device_id=peer(tok=tok_at + 2), device_id_type=mesh_id)
+
+    pl.semaphore_wait(barrier, jnp.where((line > 0) & (line < 3), 6, 5))
+
+
+def own_block(mdl_at, values, width, act):
+    for at in range(4):
+        pl.when(mdl_at == at)(lambda at=at: act(values[:, at * width : (at + 1) * width]))
+
+
+def back_kernel(
+    two_full,
+    branch_full,
+    token_blocks,
+    cot_blocks,
+    mlp_blocks,
+    unit_grads,
+    hot,
+    pieces,
+    out_bias,
+    out_full,
+    head_rows,
+    attended,
+    q_heads,
+    k_heads,
+    v_heads,
+    logsum,
+    seg_col,
+    seg_row,
+    up_out,
+    down_out,
+    mlp_own,
+    grad_out,
+    dq_heads,
+    dk_heads,
+    dv_heads,
+    branch_own,
+    two_own,
+    stats,
+    attn_sums,
+    token_buf,
+    cot_buf,
+    g_heads,
+    key_flip,
+    dk_sum,
+    dv_sum,
+    out_sum,
+    cross_in,
+    sums,
+    above,
+    below,
+    mlp_parts,
+    mlp_near,
+    mlp_out,
+    mlp_far,
+    load_sems,
+    part_sems,
+    line_sends,
+    line_recvs,
+    col_sends,
+    col_recvs,
+):
+    tok_at = lax.axis_index("tok")
+    mdl_at = lax.axis_index("mdl")
+    rows, width = two_full.shape
+    chunks = col_sends.shape[1]
+    size = rows // chunks
+    units = up_out.shape[1]
+    heads, _, head_width = q_heads.shape
+    local_width = heads * head_width
+    score_scale = 1.0 / math.sqrt(head_width)
+    greet_line(tok_at, mdl_at)
+    scatters = [
+        LineScatter(
+            tok_at,
+            unit_grads,
+            pl.ds(part * units, units),
+            cross_in.at[part],
+            sums.at[part],
+            above.at[part],
+            below.at[part],
+            line_sends.at[part],
+            line_recvs.at[part],
+            up_out.shape[0],
+        )
+        for part in range(2)
+    ]
+    mlps = ColumnReduce(
+        mdl_at, mlp_blocks, mlp_parts.at[0], mlp_parts.at[1], mlp_near, mlp_out, mlp_far, col_sends, col_recvs, size
+    )
+    for scatter in scatters:
+        scatter.start()
+    for chunk in range(chunks):
+        mlps.first(chunk)
+    part_loads = [
+        pltpu.make_async_copy(mlp_blocks.at[mdl_at], mlp_parts.at[0], part_sems.at[0]),
+        pltpu.make_async_copy(mlp_blocks.at[lax.rem(mdl_at + 2, 4)], mlp_parts.at[1], part_sems.at[1]),
+    ]
+    for copy in part_loads:
+        copy.start()
+
+    def span(chunk):
+        return pl.ds(pl.multiple_of(chunk * size, 128), size)
+
+    def loads(chunk, slot):
+        return (
+            pltpu.make_async_copy(token_blocks.at[:, span(chunk), :], token_buf.at[slot], load_sems.at[0, slot]),
+            pltpu.make_async_copy(cot_blocks.at[:, span(chunk), :], cot_buf.at[slot], load_sems.at[1, slot]),
+        )
+
+    for copy in loads(0, 0):
+        copy.start()
+    for head in range(heads):
+        key_flip[head] = k_heads[head].T
+    attn_sums[...] = jnp.zeros_like(attn_sums)
+    out_sum[...] = jnp.zeros_like(out_sum)
+    for copy in part_loads:
+        copy.wait()
+    for chunk in range(chunks):
+        mlps.second(chunk)
+
+    def step(chunk, carry):
+        slot = lax.rem(chunk, 2)
+
+        @pl.when(chunk + 1 < chunks)
+        def _():
+            for copy in loads(chunk + 1, 1 - slot):
+                copy.start()
+
+        for copy in loads(chunk, slot):
+            copy.wait()
+        here = span(chunk)
+        hot_now = hot[here, :]
+
+        def spread(part):
+            return mm(hot_now, pieces[part], ((1,), (0,)))
+
+        token_rows = jnp.concatenate([token_buf[slot, at] for at in range(4)], axis=1).astype(f32)
+        gate_one = spread(2)
+        middle = token_rows + gate_one * (branch_full[here, :].astype(f32) + out_bias[...])
+        row_mean = jnp.mean(middle, axis=1, keepdims=True)
+        normed, inverse = centre(middle)
+        grad_norm = two_full[here, :].astype(f32) * (1.0 + spread(4))
+        mean_one = jnp.mean(grad_norm, axis=1, keepdims=True)
+        mean_two = jnp.mean(grad_norm * normed, axis=1, keepdims=True)
+        cot_rows = jnp.concatenate([cot_buf[slot, at] for at in range(4)], axis=1).astype(f32)
+        grad_middle = cot_rows + inverse * (grad_norm - mean_one - normed * mean_two)
+        grad_attn = (grad_middle * gate_one).astype(bf16)
+        attn_sums[...] += jnp.sum(grad_attn.astype(f32), axis=0, keepdims=True)
+        grad_att = mm(grad_attn, out_full[...], ((1,), (0,))).astype(bf16).astype(f32)
+        grad_att = (grad_att * mm(hot_now, head_rows[...], ((1,), (0,)))).astype(bf16)
+        for head in range(heads):
+            g_heads[head, here, :] = grad_att[:, head * head_width : (head + 1) * head_width]
+        out_sum[...] += mm(grad_attn, attended[here, :], ((0,), (0,)))
+        for column, value in enumerate((row_mean, inverse, mean_one, mean_two)):
+            stats[here, column : column + 1] = value
+
+        def keep(ref):
+            def act(part):
+                ref[here, :] = part
+
+            return act
+
+        own_block(mdl_at, branch_full[here, :], local_width, keep(branch_own))
+        own_block(mdl_at, two_full[here, :], local_width, keep(two_own))
+        return carry
+
+    lax.fori_loop(0, chunks, step, 0)
+    grad_out[...] = out_sum[...].astype(bf16)
+    for chunk in range(chunks):
+        mlp_own[pl.ds(chunk * size, size), :] = mlps.third(chunk)
+
+    order = ((0, 0), (0, 3), (0, 1), (0, 2), (1, 0), (1, 3), (1, 1), (1, 2))
+
+    def attend_step(at, carry):
+        head = lax.div(at, chunks)
+        chunk = lax.rem(at, chunks)
+        here = span(chunk)
+
+        @pl.when(chunk == 0)
+        def _():
+            dk_sum[...] = jnp.zeros_like(dk_sum)
+            dv_sum[...] = jnp.zeros_like(dv_sum)
+
+        query = q_heads[head, here, :]
+        grad = g_heads[head, here, :]
+        scores = mm(k_heads[head], query, ((1,), (1,)))
+        same = seg_col[...] == seg_row[0:1, here]
+        probs = jnp.exp(jnp.where(same, scores * score_scale - logsum[pl.ds(head, 1), here], unseen))
+        grad_prob = mm(v_heads[head], grad, ((1,), (1,)))
+        dv_sum[...] += mm(probs.astype(bf16), grad, ((1,), (0,)))
+        product = probs * grad_prob
+        grad_scores = (product - probs * jnp.sum(product, axis=0, keepdims=True)).astype(bf16)
+        dk_sum[...] += mm(grad_scores, query, ((1,), (0,)))
+        flipped = mm(key_flip[head], grad_scores, ((1,), (0,)))
+        dq_heads[head, here, :] = (flipped.T * score_scale).astype(bf16)
+
+        @pl.when(chunk == chunks - 1)
+        def _():
+            dk_heads[head] = (dk_sum[...] * score_scale).astype(bf16)
+            dv_heads[head] = dv_sum[...].astype(bf16)
+
+        for index, (part, place) in enumerate(order):
+
+            @pl.when(at == index)
+            def _():
+                scatters[part].fold(place)
+                scatters[part].pass_on(place)
+
+        return carry
+
+    lax.fori_loop(0, chunks * heads, attend_step, 0)
+    scatters[0].finish(up_out)
+    scatters[1].finish(down_out)
+    for scatter in scatters:
+        scatter.wait_send()
+    for chunk in range(chunks):
+        mlps.wait_send(chunk)
+
+
+def back(two_full, branch_full, token_blocks, cot_blocks, mlp_blocks, unit_grads, hot, pieces, out_bias, out_full, head_rows, attended, q_heads, k_heads, v_heads, logsum, seg_col, seg_row, tok_count):
+    rows, width = two_full.shape
+    units = unit_grads.shape[1] // 2
+    heads, _, head_width = q_heads.shape
+    local_width = heads * head_width
+    own_rows = width // tok_count
+    chunks = 5
+    size = rows // chunks
+    dma = pltpu.SemaphoreType.DMA
+    vmem = pl.BlockSpec(memory_space=pltpu.VMEM)
+    anywhere = pl.BlockSpec(memory_space=pl.ANY)
+    low = lambda *shape: pltpu.VMEM(shape, bf16)
+    head_shape = jax.ShapeDtypeStruct((heads, rows, head_width), bf16)
+    return pl.pallas_call(
+        back_kernel,
+        out_shape=(
+            jax.ShapeDtypeStruct((own_rows, units), f32),
+            jax.ShapeDtypeStruct((own_rows, units), f32),
+            jax.ShapeDtypeStruct((rows, local_width), f32),
+            jax.ShapeDtypeStruct((width, local_width), bf16),
+            head_shape,
+            head_shape,
+            head_shape,
+            jax.ShapeDtypeStruct((rows, local_width), bf16),
+            jax.ShapeDtypeStruct((rows, local_width), bf16),
+            jax.ShapeDtypeStruct((rows, 128), f32),
+            jax.ShapeDtypeStruct((1, width), f32),
+        ),
+        in_specs=[vmem, vmem, anywhere, anywhere, anywhere] + [vmem] * 13,
+        out_specs=(vmem,) * 11,
+        scratch_shapes=[
+            low(2, 4, size, local_width),
+            low(2, 4, size, local_width),
+            low(heads, rows, head_width),
+            low(heads, head_width, rows),
+            pltpu.VMEM((rows, head_width), f32),
+            pltpu.VMEM((rows, head_width), f32),
+            pltpu.VMEM((width, local_width), f32),
+            low(2, 4, own_rows, units),
+            low(2, 4, own_rows, units),
+            low(2, 4, own_rows, units),
+            low(2, 4, own_rows, units),
+            low(2, rows, local_width),
+            low(2, rows, local_width),
+            low(rows, local_width),
+            low(rows, local_width),
+            dma((2, 2)),
+            dma((2,)),
+            dma((2, 2, 4)),
+            dma((2, 3, 4)),
+            dma((3, chunks)),
+            dma((3, chunks)),
+        ],
+        compiler_params=pltpu.CompilerParams(collective_id=3, has_side_effects=True, vmem_limit_bytes=63 * 2**20),
+    )(two_full, branch_full, token_blocks, cot_blocks, mlp_blocks, unit_grads, hot, pieces, out_bias, out_full, head_rows, attended, q_heads, k_heads, v_heads, logsum, seg_col, seg_row)
 
 
 def on_device(
@@ -861,7 +1283,6 @@
     label_all = small_all[:, :, freq_count + local_width].reshape(all_crops).astype(jnp.int32)
     label_hot = ((label_all[:, None] == jnp.arange(class_table.shape[0], dtype=jnp.int32)[None, :]) & real_crop).astype(f32)
     tokens_full = jnp.concatenate([token_blocks[at] for at in range(4)], axis=1)
-    cot_full = jnp.concatenate([cot_blocks[at] for at in range(4)], axis=1)
     qkv_full, out_full = head_full[:, : 3 * local_width], head_full[:, 3 * local_width :]
     out_bias_full = mod_full[0, slot_count :slot_count + 1]
     mod_rows = jnp.transpose(mod_full[:, :slot_count], (1, 0, 2))
@@ -905,66 +1326,61 @@
     )
     attended = (attend_now.reshape(row_len, local_width) * head_units.astype(f32)).astype(bf16)
     branch_part = mm(attended, out_full, ((1,), (1,))).astype(bf16)
-    branch_low, mlp_part, two_low, unit_grads, grad_up_bias, mlp_sums = feed(
+    branch_low, mlp_blocks, two_low, unit_grads, grad_up_bias, mlp_sums = feed(
         branch_part, token_blocks, cot_blocks, hot, hot_keep, pieces, out_bias_full, unit_full, up_bias.astype(f32)[None], chan_rows
     )
     grad_up_bias = grad_up_bias[0]
     grad_down_bias = own_cols(mlp_sums)[0]
-    grad_units = lax.psum_scatter(unit_grads, "tok", scatter_dimension=0, tiled=True).astype(f32)
-    mlp_out = scatter_cols(mlp_part).astype(f32) + down_bias.astype(f32)
-    attn_branch = branch_low.astype(f32) + out_bias_full
-    gate_one = spread(2)
-    middle = start_rows + gate_one * attn_branch
-    normed_two, inverse_two = norm_rows(middle)
-    scale_two = spread(4)
-    gate_two = spread(5)
-    output = (own_cols(middle) + own_cols(gate_two) * keep_rows * mlp_out).astype(bf16)
-    grad_rows = cot_full.astype(f32)
-    grad_two = two_low.astype(f32)
-    two_own = own_cols(two_low)
-
-    def norm_back(grad_norm, normed, inverse):
-        return inverse * (
-            grad_norm
-            - jnp.mean(grad_norm, axis=1, keepdims=True)
-            - normed * jnp.mean(grad_norm * normed, axis=1, keepdims=True)
-        )
-
-    grad_middle = grad_rows + norm_back(grad_two * (1.0 + scale_two), normed_two, inverse_two)
-    grad_attn = (grad_middle * gate_one).astype(bf16)
-    grad_out = mm(grad_attn, attended, ((0,), (0,)))
-    grad_out_bias = jnp.sum(own_cols(grad_attn).astype(f32), axis=0)
-    grad_att = mm(grad_attn, out_full, ((1,), (0,))).astype(bf16) * head_units
-    query_grads, key_grads, value_grads = attend_back(
-        heads(queries), heads(key_rows), heads(value_rows), segment[0], logsum_rows, heads(grad_att), score_scale
-    )
+    head_rows = rows32(jnp.repeat(head_mask[0].astype(bf16), head_width, axis=1))
+
+    def by_head(rows_low):
+        return jnp.transpose(heads(rows_low), (1, 0, 2))
+
+    grad_up, grad_down, mlp_own, grad_out, dq_heads, dk_heads, dv_heads, branch_own, two_own, stats, attn_sums = back(
+        two_low, branch_low, token_blocks, cot_blocks, mlp_blocks, unit_grads, hot, pieces, out_bias_full, out_full, head_rows,
+        attended, by_head(queries), by_head(key_rows), by_head(value_rows), logsum_rows, segment[0][:, None], segment, tok_count,
+    )
+    own_pieces = lax.dynamic_slice_in_dim(mod_rows, mdl_at * local_width, local_width, axis=2)
+
+    def spread_own(part):
+        return exact_dot(crop_hot32, own_pieces[:, part])
+
+    mlp_out = mlp_own + down_bias.astype(f32)
+    branch_own = branch_own.astype(f32) + out_bias.astype(f32)
+    gate_one_own = spread_own(2)
+    middle_own = tokens.astype(f32) + gate_one_own * branch_own
+    output = (middle_own + spread_own(5) * keep_rows * mlp_out).astype(bf16)
+    normed_two_own = (middle_own - stats[:, 0:1]) * stats[:, 1:2]
+    two_own32 = two_own.astype(f32)
+    grad_middle_own = cotangent.astype(f32) + stats[:, 1:2] * (
+        two_own32 * (1.0 + spread_own(4)) - stats[:, 2:3] - normed_two_own * stats[:, 3:4]
+    )
+    grad_out_bias = own_cols(attn_sums)[0]
     grad_qkv_rows = jnp.concatenate(
-        [part.reshape(row_len, local_width).astype(bf16) for part in (query_grads, key_grads, value_grads)], axis=1
+        [jnp.transpose(part, (1, 0, 2)).reshape(row_len, local_width) for part in (dq_heads, dk_heads, dv_heads)], axis=1
     )
     grad_qkv = mm(modulated_one, grad_qkv_rows, ((0,), (0,)))
     grad_bias_rows = jnp.sum(grad_qkv_rows.astype(f32), axis=0)
     grad_qv_bias = jnp.stack([grad_bias_rows[:local_width], grad_bias_rows[2 * local_width :]], axis=0)
     grad_heads = lax.psum_scatter(
-        jnp.concatenate([grad_qkv, grad_out], axis=1).astype(bf16), "tok", scatter_dimension=0, tiled=True
+        jnp.concatenate([grad_qkv.astype(bf16), grad_out], axis=1), "tok", scatter_dimension=0, tiled=True
     ).astype(f32)
     grad_one = scatter_cols(mm(grad_qkv_rows, qkv_full, ((1,), (1,)))).astype(f32)
     normed_one_own = own_cols(normed_one)
-    grad_norm = grad_one * (1.0 + own_cols(spread(1)))
+    grad_norm = grad_one * (1.0 + spread_own(1))
     totals = lax.psum(
         jnp.stack([jnp.sum(grad_norm, axis=1), jnp.sum(grad_norm * normed_one_own, axis=1)]), "mdl"
     )
-    grad_middle_own = own_cols(grad_middle)
     grad_tokens = grad_middle_own + inverse_one * (
         grad_norm - totals[0][:, None] / full_width - normed_one_own * totals[1][:, None] / full_width
     )
-    two_own32 = two_own.astype(f32)
     grad_per_token = jnp.concatenate(
         [
             grad_one,
             grad_one * normed_one_own,
-            grad_middle_own * own_cols(attn_branch),
+            grad_middle_own * branch_own,
             two_own32,
-            two_own32 * own_cols(normed_two),
+            two_own32 * normed_two_own,
             cotangent.astype(f32) * keep_rows * mlp_out,
         ],
         axis=1,
@@ -994,9 +1410,9 @@
         grad_qv_bias,
         grad_heads[:, 3 * local_width :].T,
         grad_out_bias,
-        grad_units[:, :units_here],
+        grad_up,
         grad_up_bias,
-        grad_units[:, units_here:].T,
+        grad_down.T,
         grad_down_bias,
         grad_ada,
         grad_ada_bias,

time: 698 us -> 623 us (0.89)
  Pallas kernels: 219 us -> 304 us
  waiting for transfers between devices: 141 us -> 84.6 us
  matrix products: 135 us -> 79.8 us
  other arithmetic: 84.1 us -> 31.4 us
    pallas_call x0 -> x1, Pallas kernels: none -> 88.7 us  [back(): pl.pallas_call(back_kernel, out_shape=(jax.ShapeDtypeStruct((own_rows, un...]
    dot_general x4 -> x0, matrix products: 46.8 us -> none  [the longest x1 17 us: attend_back(): jnp.einsum('qhd,khd->hqk', grad_att, value_rows, preferred_element_type=f32)]
    convert_element_type x7 -> x4, other arithmetic: 35.5 us -> 2.17 us  [the longest x1 2.16 us: on_device(): grad_heads = lax.psum_scatter(jnp.concatenate([grad_qkv.astype(bf16), gra...]
    reduce_scatter x1 -> x0, waiting for transfers between devices: 28.8 us -> none  [on_device(): lax.psum_scatter(unit_grads, 'tok', scatter_dimension=0, tiled=True)]
    unnamed x7 -> x4, waiting for transfers between devices: 112 us -> 84.6 us
    mul x2 -> x1, other arithmetic: 10.8 us -> 3.18 us  [norm_rows(): return ((values - row_mean) * inverse, inverse)]
    concatenate x2 -> x1, local copies, waits for them, and re-layouts: 17.5 us -> 11.4 us  [on_device(): jnp.concatenate([grad_one, grad_one * normed_one_own, grad_middle_own * b...]
    dot_general x8 -> x6, matrix products: 24.5 us -> 18.4 us  [mm(): lax.dot_general(left, right, (dims, ((), ())), preferred_element_type=f32)]
  transfers between devices with their start and end apart: 4 -> 2, of which waited for: 4 -> 2; matrix products, arithmetic and copies ran while one was open for 12% -> 7% of each run, Pallas kernels for 4% -> 0%
where the time goes in v4:
time: 623 us; the launch traced here: 612 us
  Pallas kernels  304 us (49%)
  local copies, waits for them, and re-layouts  87.1 us (14%)
  waiting for transfers between devices  84.6 us (14%)
  matrix products  79.8 us (13%)
  other arithmetic  31.4 us (5%)
  between operations  15.2 us (2%)
  blocking collectives  10.4 us (2%)
    pallas_call x1, Pallas kernels, gather_all(): pl.pallas_call(gather_kernel, out_shape=(jax.ShapeDtypeStruct((tok_count,...  115 us
    pallas_call x1, Pallas kernels, back(): pl.pallas_call(back_kernel, out_shape=(jax.ShapeDtypeStruct((own_rows, un...  88.7 us
    unnamed x4, waiting for transfers between devices  84.6 us
    pallas_call x1, Pallas kernels, feed(): pl.pallas_call(feed_kernel, out_shape=(jax.ShapeDtypeStruct((rows, width)...  77.6 us
    dot_general x8, matrix products, exact_dot(): jnp.dot(left, right, precision=lax.Precision.HIGHEST, preferred_element_t...  32.1 us
    unnamed x104, local copies, waits for them, and re-layouts  31.4 us
    pallas_call x1, Pallas kernels, cond_back(): pl.pallas_call(cond_back_kernel, out_shape=(jax.ShapeDtypeStruct((tok_cou...  22.4 us
    dot_general x6, matrix products, mm(): lax.dot_general(left, right, (dims, ((), ())), preferred_element_type=f32)  18.4 us
  transfers between devices with their start and end apart: 2, of which 2 were waited for; matrix products, arithmetic and copies ran while one was open for 7% of the time, Pallas kernels for 0%

profile of v4, /device:TPU:0, one launch (start us, length us, event | category | flops | bytes accessed | tf_op | source)
XLA Modules:
  0.0 612.4 jit_solution(4683833608204755662)
XLA Ops:
  18.8 115.1 %shard_map.308 = (f32[8,8,640]{2,1,0:T(8,128)S(1)}, f32[64,288]{1,0:T(8,128)S(1)}, bf16[64,144]{1,0:T(8,128)(2,1)S(1)}, f32[6,8,1152]{2,1,0:T(8,128)S(1)}, bf16[...) custom-call(f32[8,640]{1,0:T(8,128)S(1)} %select_maximum_fusion.1.sm, ...), custom_call_target="tpu_custom_call" | custom-call | tf_op jit(solution)/shard_map/pallas_call | solution.py:408
  139.8 4.1 slice_bitcast_fusion
  143.9 5.9 concatenate.37
  150.8 4.9 fusion.3
  155.7 4.6 fusion.4
  162.1 3.4 fusion.25
  166.8 11.2 %fusion.61 = (f32[4,1280]{1,0:T(4,128)S(1)}, f32[4,1280,1280]{1,2,0:T(8,128)}) fusion(bf16[1280,4,72]{0,2,1:T(8,128)(2,1)S(1)} %bitcast.113, bf16[1280,4,72]{0,2,1:T(8,128)(2,1)S(1)} %bitcast.124, pred[1280,1280]{0,1:T(8,128)(4,1)S(1)} %broadcast_compare_fusion), kind=kOutput, calls=%fused_computation.143 | convolution fusion | flops 963374080 | bytes 29347840 | tf_op jit(solution)/shard_map/qhd,khd->hqk/dot_general | solution.py:59
  178.0 10.6 %fusion.1 = f32[4,1280]{1,0:T(4,128)S(1)} fusion(f32[4,1280,1280]{1,2,0:T(8,128)} %get-tuple-element.178, f32[4,1280]{1,0:T(4,128)S(1)} %get-tuple-element.177), kind=kLoop, calls=%fused_computation.4 | loop fusion | flops 13102080 | bytes 26255360 | tf_op jit(solution)/shard_map/reduce_sum | solution.py:64
  188.6 11.4 %fusion.20 = bf16[1280,4,72]{0,2,1:T(8,128)(2,1)S(1)} fusion(bf16[1280,4,72]{0,2,1:T(8,128)(2,1)S(1)} %bitcast.111, f32[4,1280,1280]{1,2,0:T(8,128)} %get-tuple-element.178, f32[4,1280]{1,0:T(4,128)S(1)} %fusion.1, f32[4,1280]{1,0:T(4,128)S(1)} %get-tuple-element.177, f32[1280,4]{0,1:T(4,128)S(1)} %fusion.21), kind=kOutput, calls=%fused_computation.38 | convolution fusion | flops 964116480 | bytes 27750400 | tf_op jit(solution)/shard_map/hqk,khd->qhd/dot_general | solution.py:66
  200.0 3.6 convolution_convert_fusion.1.branch_part
  215.2 77.6 %shard_map.309 = (bf16[1280,1152]{1,0:T(8,128)(2,1)}, bf16[4,1280,288]{2,1,0:T(8,128)(2,1)}, bf16[1280,1152]{1,0:T(8,128)(2,1)}, bf16[1152,2304]{1,0:T(8,128)(2,...) custom-call(bf16[1280,1152]{1,0:T(8,128)(2,1)} %convolution_convert_fusion.1.branch_part, bf16[4,1280,288]{2,1,0:T(8,128)(2,1)} %copy-done.2, ...), custom_call_target="tpu_custom_call" | custom-call | tf_op jit(solution)/shard_map/pallas_call | solution.py:762
  292.8 88.7 %shard_map.310 = (f32[144,1152]{1,0:T(8,128)}, f32[144,1152]{1,0:T(8,128)}, f32[1280,288]{1,0:T(8,128)}, bf16[1152,288]{1,0:T(8,128)(2,1)}, bf16[4,1280,72]{2,1,...) custom-call(bf16[1280,1152]{1,0:T(8,128)(2,1)} %get-tuple-element.49, ...), custom_call_target="tpu_custom_call" | custom-call | tf_op jit(solution)/shard_map/pallas_call | solution.py:1170
  381.5 2.4 copy.172
  385.2 2.4 copy.170
  387.6 2.3 copy.175
  389.9 4.6 convolution_convert_fusion.2
  394.8 3.3 copy.188
  399.8 6.4 %fusion.5 = bf16[1152,1280]{1,0:T(8,128)(2,1)} fusion(bf16[1152,1152]{1,0:T(8,128)(2,1)S(1)} %copy-done.12, bf16[1280,288]{0,1:T(8,128)(2,1)} %bitcast.116, bf16[1280,288]{0,1:T(8,128)(2,1)} %bitcast.119, bf16[1280,288]{0,1:T(8,128)(2,1)} %bitcast.122), kind=kOutput, calls=%fused_computation.15 | convolution fusion | flops 2556149760 | bytes 7225344 | tf_op jit(solution)/shard_map/dot_general | solution.py:21
  409.8 4.7 fusion.27
  414.5 2.6 fusion.17
  424.5 3.4 fusion.22
  427.9 3.2 fusion.6
  431.0 56.5 %reduce-scatter.9.cloned.1.call-done = bf16[144,1152]{1,0:T(8,128)(2,1)} async-done(((bf16[1152,1152]{1,0:T(8,128)(2,1)}), bf16[144,1152]{1,0:T(8,128)(2,1)}) %reduce-scatter.9.cloned.1.call-update) | async-done | bytes 331792
  493.8 2.5 copy.178
  498.2 28.0 %reduce-scatter.7.cloned.1.call-done = bf16[288,1280]{1,0:T(8,128)(2,1)} async-done(((bf16[1152,1280]{1,0:T(8,128)(2,1)}), bf16[288,1280]{1,0:T(8,128)(2,1)}) %reduce-scatter.7.cloned.1.call-update) | async-done | bytes 737296
  528.3 6.1 %fusion.56 = (f32[1280]{0:T(1024)S(1)}, f32[1280]{0:T(1024)S(1)}, f32[1280,288]{1,0:T(8,128)}, f32[1280,288]{1,0:T(8,128)}) fusion(f32[1280,1152]{1,0:T(8,128)} %fusion.6, s32[]{:T(128)S(6)} %select_n.36, bf16[1280,288]{1,0:T(8,128)(2,1)} %copy.187, f32[6,6,288]{2,0,1:T(8,128)S(1)} %dynamic-slice_bitcast_fusion, s32[6]{0:T(128)S(1)} %get-tuple-element.174, ...), kind=kOutput, calls=%fused_computation.138 | convolution fusion | flops 29143040 | bytes 5184516 | tf_op jit(solution)/shard_map/dot_general | solution.py:17
  534.5 10.4 %psum.7 = f32[2,1280]{1,0:T(2,128)S(1)} all-reduce(f32[2,1280]{1,0:T(2,128)S(1)} %pad_maximum_fusion.5), channel_id=1, replica_groups=mesh['tok'=8,'mdl'=4] {'mdl'}, use_global_device_ids=true, to_apply=%region_9.10 | all-reduce | flops 2560 | bytes 20480 | tf_op jit(solution)/shard_map/psum | solution.py:1371
  545.0 6.5 %fusion.23 = (f32[1280,288]{1,0:T(8,128)}, f32[1280,288]{1,0:T(8,128)}) fusion(bf16[1280,288]{1,0:T(8,128)(2,1)} %get-tuple-element.53, f32[288]{0:T(512)S(1)} %copy-done.31, f32[1280]{0:T(1024)S(1)} %get-tuple-element.151, f32[1280,1152]{1,0:T(8,128)} %fusion.6, s32[]{:T(128)S(6)} %select_n.36, f32[1280,288]{1,0:T(8,128)} %get-tuple-element.179, ...), kind=kOutput, calls=%fused_computation.48 | convolution fusion | flops 33937920 | bytes 10394628 | tf_op jit(solution)/shard_map/dot_general | solution.py:17
  551.4 11.4 %concatenate.41 = f32[1280,1728]{1,0:T(8,128)} concatenate(bf16[1280,288]{1,0:T(8,128)(2,1)} %copy.187, f32[1280,288]{1,0:T(8,128)} %get-tuple-element.154, f32[1280,288]{1,0:T(8,128)} %get-tuple-element.161, bf16[1280,288]{1,0:T(8,128)(2,1)} %get-tuple-element.56, f32[1280,288]{1,0:T(8,128)} %get-tuple-element.180, f32[1280,288]{1,0:T(8,128)} %fusion.22), dimensions={1} | concatenate | bytes 16220160 | tf_op jit(solution)/shard_map/concatenate | solution.py:1377
  562.9 6.7 %fusion.46 = f32[6,1728]{1,0:T(8,128)S(1)} fusion(f32[1280,1728]{1,0:T(8,128)} %concatenate.41, s32[6]{0:T(128)S(1)} %get-tuple-element.174, s32[6]{0:T(128)S(1)} %get-tuple-element.173), kind=kOutput, calls=%fused_computation.135 | convolution fusion | flops 159275520 | bytes 8888880 | tf_op jit(solution)/shard_map/dot_general | solution.py:1388
  569.6 22.4 %shard_map.311 = (f32[8,8,1728]{2,1,0:T(8,128)S(1)}, f32[144,1728]{1,0:T(8,128)S(1)}, f32[64,288]{1,0:T(8,128)S(1)}) custom-call(f32[8,1728]{1,0:T(8,128)S(1)} %pad_maximum_fusion.4.gmod_own, bf16[144,1728]{1,0:T(8,128)(2,1)S(1)} %copy-done.8, bf16[64,144]{1,0:T(8,128)(2,1)S(1)} %get-tuple-element.64.cond_own, f32[64,288]{1,0:T(8,128)S(1)} %get-tuple-element.65.embedding), custom_call_target="tpu_custom_call" | custom-call | tf_op jit(solution)/shard_map/pallas_call | solution.py:528
  593.6 2.7 copy.177
  (201 shorter events, 67.6 us)
Async XLA Ops:
  7.2 9.8 %copy-start = (bf16[1000,288]{0,1:T(8,128)(2,1)S(1)}, bf16[1000,288]{0,1:T(8,128)(2,1)}, u32[]{:S(2)}) copy-start(bf16[1000,288]{0,1:T(8,128)(2,1)} %param.41) | copy-start | bytes 1728004
  7.2 5.7 copy-start.35
  7.2 5.7 copy-start.33
  7.2 5.8 copy-start.24
  7.2 480.3 %reduce-scatter.9.cloned.1.call-start = ((), (), s32[]{:S(2)}) async-start(), calls=%async_computation.3 | async-start | bytes 2985984
  12.9 5.9 copy-start.7
  13.2 3.7 copy-start.44
  13.5 3.9 copy-start.26
  15.1 3.7 copy-start.5
  15.1 3.7 copy-start.13
  16.9 116.9 %copy-start.3 = (bf16[1280,288]{1,0:T(8,128)(2,1)}, bf16[1280,288]{1,0:T(8,128)(2,1)S(1)}, u32[]{:S(2)}) copy-start(bf16[1280,288]{1,0:T(8,128)(2,1)S(1)} %copy.153.cotangent) | copy-start | bytes 2211844
  18.6 120.8 %copy-start.39 = (s32[1,6,4]{1,2,0:T(4,128)S(1)}, s32[1,6,4]{1,2,0:T(4,128)}, u32[]{:S(2)}) copy-start(s32[1,6,4]{1,2,0:T(4,128)} %param.27) | copy-start | bytes 292
  149.8 5.9 copy-start.14
  155.7 4.7 copy-start.11
  160.4 5.1 copy-start.19
  206.3 5.1 copy-start.27
  206.3 5.5 copy-start.32
  206.3 5.5 copy-start.37
  206.3 6.2 %copy-start.40 = (s32[1,6,4]{1,2,0:T(4,128)S(1)}, s32[1,6,4]{1,2,0:T(4,128)}, u32[]{:S(2)}) copy-start(s32[1,6,4]{1,2,0:T(4,128)} %param.28) | copy-start | bytes 292
  385.2 4.7 copy-start.20
  389.9 4.7 copy-start.21
  398.1 128.0 %reduce-scatter.7.cloned.1.call-start = ((), (), s32[]{:S(2)}) async-start(), calls=%async_computation.2 | async-start | bytes 3686400
  406.9 7.6 %copy-start.30 = (f32[288]{0:T(512)}, f32[288]{0:T(512)S(1)}, u32[]{:S(2)}) copy-start(f32[288]{0:T(512)S(1)} %convert_element_type.144) | copy-start | bytes 3460
  409.8 4.7 copy-start.17
  417.1 4.3 copy-start.34
  417.1 7.4 %copy-start.4 = (bf16[1280,288]{1,0:T(8,128)(2,1)S(1)}, bf16[1280,288]{1,0:T(8,128)(2,1)}, u32[]{:S(2)}) copy-start(bf16[1280,288]{1,0:T(8,128)(2,1)} %copy-done.3) | copy-start | bytes 2211844
  528.3 16.6 %copy-start.28 = (f32[1280]{0:T(1024)S(1)}, f32[1280]{0:T(1024)}, u32[]{:S(2)}) copy-start(f32[1280]{0:T(1024)} %get-tuple-element.147) | copy-start | bytes 15364
  528.3 16.7 %copy-start.29 = (f32[1280]{0:T(1024)S(1)}, f32[1280]{0:T(1024)}, u32[]{:S(2)}) copy-start(f32[1280]{0:T(1024)} %get-tuple-element.149) | copy-start | bytes 15364
  528.3 16.7 %copy-start.31 = (f32[288]{0:T(512)S(1)}, f32[288]{0:T(512)}, u32[]{:S(2)}) copy-start(f32[288]{0:T(512)} %copy-done.30) | copy-start | bytes 3460
  562.9 6.7 %copy-start.8 = (bf16[144,1728]{1,0:T(8,128)(2,1)S(1)}, bf16[144,1728]{1,0:T(8,128)(2,1)}, u32[]{:S(2)}) copy-start(bf16[144,1728]{1,0:T(8,128)(2,1)} %copy-done.7) | copy-start | bytes 1492996
  597.6 6.6 %copy-start.23 = (f32[144,1152]{1,0:T(8,128)S(1)}, f32[144,1152]{1,0:T(8,128)}, u32[]{:S(2)}) copy-start(f32[144,1152]{1,0:T(8,128)} %get-tuple-element.68) | copy-start | bytes 1990660
  597.6 7.5 %copy-start.1 = (bf16[1000,288]{0,1:T(8,128)(2,1)S(1)}, bf16[1000,288]{0,1:T(8,128)(2,1)}, u32[]{:S(2)}) copy-start(bf16[1000,288]{0,1:T(8,128)(2,1)} %param.41) | copy-start | bytes 1728004
  (15 other events, 33.1 us)
Sparse Core Ops, SparseCore 0:
  398.2 89.3 reduce-scatter.8
  490.3 35.7 reduce-scatter.6

commit v5 on v4

--- a/solution.py
+++ b/solution.py
@@ -444,109 +444,6 @@
         ],
         compiler_params=pltpu.CompilerParams(collective_id=0, has_side_effects=True, vmem_limit_bytes=40 * 2**20),
     )(small_own, time_weight, ada_own, ada_bias, head_shard, unit_shard, tokens, cotangent)
-
-
-def cond_back_kernel(
-    gmod_own,
-    ada_own,
-    cond_own,
-    embedding,
-    gmod_all,
-    grad_ada,
-    grad_embed,
-    part_own,
-    part_slots,
-    cond_slots,
-    gmod_send,
-    gmod_recv,
-    part_send,
-    part_recv,
-    cond_send,
-    cond_recv,
-):
-    tok_at = lax.axis_index("tok")
-    mdl_at = lax.axis_index("mdl")
-    tok_count, slots = gmod_all.shape[0], gmod_all.shape[1]
-    greet(tok_at, mdl_at, tok_count, 4)
-    gmods = AllToPeers("tok", tok_at, tok_count, gmod_send, gmod_recv)
-    gmods.start(lambda other: gmod_own, gmod_all)
-    gmod_all[tok_at] = gmod_own[...]
-    gmods.wait_recv(lambda other: gmod_own, gmod_all)
-    high, rest = split_two(gmod_all[...].reshape(tok_count * slots, gmod_all.shape[2]))
-    ada = ada_own[...]
-    part_own[...] = mm(high, ada, ((1,), (1,))) + mm(rest, ada, ((1,), (1,)))
-    owner = lax.div(tok_at, 2)
-    half = lax.rem(tok_at, 2)
-
-    def part_copy(source):
-        return remote(part_own, part_slots.at[source], part_send.at[0], part_recv.at[source], peer(mdl=owner))
-
-    pl.when(mdl_at != owner)(lambda: part_copy(mdl_at).start())
-    cond = cond_own[...]
-    grad_ada[...] = mm(cond, high, ((0,), (0,))) + mm(cond, rest, ((0,), (0,)))
-
-    def cond_copy(step):
-        other = lax.rem(tok_at + step, tok_count)
-        return remote(cond_slots.at[half], cond_slots.at[half], cond_send.at[step], cond_recv.at[half], peer(tok=other))
-
-    @pl.when(mdl_at == owner)
-    def _():
-        total = part_own[...]
-        for step in range(1, 4):
-            source = lax.rem(mdl_at + step, 4)
-            part_copy(source).wait_recv()
-            total = total + part_slots[source]
-        cond_slots[half] = total
-        for step in range(1, tok_count):
-            cond_copy(step).start()
-
-    for side in range(2):
-        giver = 2 * mdl_at + side
-
-        @pl.when(tok_at != giver)
-        def _():
-            remote(cond_slots.at[side], cond_slots.at[side], cond_send.at[0], cond_recv.at[side], peer(tok=giver)).wait_recv()
-
-    grad_cond = jnp.concatenate([cond_slots[0], cond_slots[1]], axis=1)
-    embed = embedding[...]
-    gate = 1.0 / (1.0 + jnp.exp(-embed))
-    grad_embed[...] = grad_cond * gate * (1.0 + embed * (1.0 - gate))
-    gmods.wait_send(lambda other: gmod_own, gmod_all)
-    pl.when(mdl_at != owner)(lambda: part_copy(mdl_at).wait_send())
-
-    @pl.when(mdl_at == owner)
-    def _():
-        for step in range(1, tok_count):
-            cond_copy(step).wait_send()
-
-
-def cond_back(gmod_own, ada_own, cond_own, embedding, tok_count):
-    slots, mod_width = gmod_own.shape
-    crops, own_rows = cond_own.shape
-    dma = pltpu.SemaphoreType.DMA
-    vmem = pl.BlockSpec(memory_space=pltpu.VMEM)
-    return pl.pallas_call(
-        cond_back_kernel,
-        out_shape=(
-            jax.ShapeDtypeStruct((tok_count, slots, mod_width), f32),
-            jax.ShapeDtypeStruct((own_rows, mod_width), f32),
-            jax.ShapeDtypeStruct(embedding.shape, f32),
-        ),
-        in_specs=[vmem] * 4,
-        out_specs=(vmem, vmem, vmem),
-        scratch_shapes=[
-            pltpu.VMEM((crops, own_rows), f32),
-            pltpu.VMEM((4, crops, own_rows), f32),
-            pltpu.VMEM((2, crops, own_rows), f32),
-            dma((tok_count,)),
-            dma((tok_count,)),
-            dma((1,)),
-            dma((4,)),
-            dma((tok_count,)),
-            dma((2,)),
-        ],
-        compiler_params=pltpu.CompilerParams(collective_id=1, has_side_effects=True, vmem_limit_bytes=32 * 2**20),
-    )(gmod_own, ada_own, cond_own, embedding)
 
 
 class RowReduce:
@@ -1211,6 +1108,332 @@
     )(two_full, branch_full, token_blocks, cot_blocks, mlp_blocks, unit_grads, hot, pieces, out_bias, out_full, head_rows, attended, q_heads, k_heads, v_heads, logsum, seg_col, seg_row)
 
 
+def tail_kernel(
+    dq_heads,
+    dk_heads,
+    dv_heads,
+    mod_one,
+    qkv_full,
+    grad_out,
+    tokens,
+    cotangent,
+    branch_own,
+    two_own,
+    mlp_own,
+    stats_one,
+    stats_two,
+    hot,
+    hot_keep,
+    own_pieces,
+    out_bias,
+    down_bias,
+    bias_sums,
+    ada_own,
+    cond_own,
+    embedding,
+    output,
+    grad_tokens,
+    head_grads,
+    gmod_all,
+    grad_ada,
+    grad_embed,
+    qkv_rows,
+    full_grads,
+    one_blocks,
+    one_near,
+    one_out,
+    one_far,
+    one_own,
+    gmod_own,
+    row_sums,
+    cross_in,
+    sums,
+    above,
+    below,
+    part_own,
+    part_slots,
+    cond_slots,
+    line_sends,
+    line_recvs,
+    col_sends,
+    col_recvs,
+    row_send,
+    row_recv,
+    gmod_send,
+    gmod_recv,
+    part_send,
+    part_recv,
+    cond_send,
+    cond_recv,
+):
+    tok_at = lax.axis_index("tok")
+    mdl_at = lax.axis_index("mdl")
+    tok_count, slots = gmod_all.shape[0], gmod_all.shape[1]
+    rows, local_width = tokens.shape
+    width = qkv_full.shape[0]
+    own_rows = head_grads.shape[0]
+    heads, _, head_width = dq_heads.shape
+    chunks = col_sends.shape[1]
+    size = rows // chunks
+    pieces_count = line_sends.shape[0]
+    piece = head_grads.shape[1] // pieces_count
+    greet(tok_at, mdl_at, tok_count, 4)
+    scatters = [
+        LineScatter(
+            tok_at,
+            full_grads,
+            pl.ds(part * piece, piece),
+            cross_in.at[part],
+            sums.at[part],
+            above.at[part],
+            below.at[part],
+            line_sends.at[part],
+            line_recvs.at[part],
+            own_rows,
+        )
+        for part in range(pieces_count)
+    ]
+    ones = ColumnReduce(
+        mdl_at, one_blocks, one_blocks.at[mdl_at], one_blocks.at[lax.rem(mdl_at + 2, 4)], one_near, one_out, one_far, col_sends, col_recvs, size
+    )
+    row_peers = AllToPeers("mdl", mdl_at, 4, row_send, row_recv)
+    gmods = AllToPeers("tok", tok_at, tok_count, gmod_send, gmod_recv)
+
+    def span(chunk):
+        return pl.ds(pl.multiple_of(chunk * size, 128), size)
+
+    gmod_own[...] = bias_sums[...]
+
+    def gather_rows(chunk, carry):
+        here = span(chunk)
+        parts = [part[head, here, :] for part in (dq_heads, dk_heads, dv_heads) for head in range(heads)]
+        joined = jnp.concatenate(parts, axis=1)
+        qkv_rows[here, :] = joined
+        total = jnp.sum(joined.astype(f32), axis=0, keepdims=True)
+        gmod_own[slots - 2 : slots - 1, :local_width] += total[:, :local_width]
+        gmod_own[slots - 2 : slots - 1, local_width : 2 * local_width] += total[:, 2 * local_width :]
+        return carry
+
+    lax.fori_loop(0, chunks, gather_rows, 0)
+    third = width // 3
+
+    def grads(index, carry):
+        at = pl.ds(pl.multiple_of(index * third, 128), third)
+        full_grads[at, :] = jnp.concatenate(
+            [mm(mod_one[:, at], qkv_rows[...], ((0,), (0,))).astype(bf16), grad_out[at, :]], axis=1
+        )
+        return carry
+
+    lax.fori_loop(0, 3, grads, 0)
+    for scatter in scatters:
+        scatter.start()
+
+    def ones_step(chunk, carry):
+        here = span(chunk)
+        part = mm(qkv_rows[here, :], qkv_full[...], ((1,), (1,))).astype(bf16)
+        for at in range(4):
+            one_blocks[at, here, :] = part[:, at * local_width : (at + 1) * local_width]
+        ones.first(chunk)
+        pl.when(chunk >= 1)(lambda: ones.second(chunk - 1))
+        return carry
+
+    lax.fori_loop(0, chunks, ones_step, 0)
+    ones.second(chunks - 1)
+    order = tuple((part, place) for part in range(pieces_count) for place in (0, 3, 1, 2))
+    pick = lax.broadcasted_iota(jnp.int32, (8, local_width), 0)
+    first_row = jnp.where(pick == 0, 1.0, 0.0).astype(bf16)
+    second_row = jnp.where(pick == 1, 1.0, 0.0).astype(bf16)
+
+    def final_step(chunk, carry):
+        here = span(chunk)
+        hot_now = hot[here, :]
+        crop_now = hot_now[:, :slots]
+        keep_now = hot_keep[here, :]
+
+        def spread(part):
+            return mm(hot_now, own_pieces[part], ((1,), (0,)))
+
+        token_rows = tokens[here, :].astype(f32)
+        branch = branch_own[here, :].astype(f32) + out_bias[...]
+        mlp = mlp_own[here, :] + down_bias[...]
+        cot_rows = cotangent[here, :].astype(f32)
+        grad_two = two_own[here, :].astype(f32)
+        middle = token_rows + spread(2) * branch
+        output[here, :] = (middle + mm(keep_now, own_pieces[5], ((1,), (0,))) * mlp).astype(bf16)
+        inverse_two = stats_two[here, 1:2]
+        normed_two = (middle - stats_two[here, 0:1]) * inverse_two
+        grad_middle = cot_rows + inverse_two * (
+            grad_two * (1.0 + spread(4)) - stats_two[here, 2:3] - normed_two * stats_two[here, 3:4]
+        )
+        grad_tokens[here, :] = grad_middle
+        grad_one = ones.third(chunk)
+        one_own[here, :] = grad_one
+        normed_one = (token_rows - stats_one[here, 0:1]) * stats_one[here, 1:2]
+        grad_norm = grad_one * (1.0 + spread(1))
+        total = jnp.zeros((8, size), f32)
+        for row, values in ((first_row, grad_norm), (second_row, grad_norm * normed_one)):
+            for split in split_two(values):
+                total = total + mm(row, split, ((1,), (1,)))
+        row_sums[mdl_at, :, here] = total
+        terms = (
+            (0, crop_now, grad_one),
+            (1, crop_now, grad_one * normed_one),
+            (2, crop_now, grad_middle * branch),
+            (3, crop_now, grad_two),
+            (4, crop_now, grad_two * normed_two),
+            (5, keep_now[:, :slots], cot_rows * mlp),
+        )
+        for part, chosen, values in terms:
+            high, rest = split_two(values)
+            gmod_own[:, part * local_width : (part + 1) * local_width] += mm(chosen, high, ((0,), (0,))) + mm(
+                chosen, rest, ((0,), (0,))
+            )
+        for index, (part, place) in enumerate(order[: 2 * chunks]):
+
+            @pl.when(chunk == index // 2)
+            def _():
+                scatters[part].fold(place)
+                scatters[part].pass_on(place)
+
+        return carry
+
+    lax.fori_loop(0, chunks, final_step, 0)
+    row_peers.start(lambda other: row_sums.at[mdl_at], row_sums)
+    gmods.start(lambda other: gmod_own, gmod_all)
+    gmod_all[tok_at] = gmod_own[...]
+    for part, place in order[2 * chunks :]:
+        scatters[part].fold(place)
+        scatters[part].pass_on(place)
+    row_peers.wait_recv(lambda other: row_sums.at[mdl_at], row_sums)
+    totals = ((row_sums[0] + row_sums[1] + row_sums[2] + row_sums[3]) * (1.0 / width)).T
+    for chunk in range(chunks):
+        here = pl.ds(chunk * size, size)
+        flip = totals[chunk * size : (chunk + 1) * size]
+        inverse_one = stats_one[here, 1:2]
+        normed_one = (tokens[here, :].astype(f32) - stats_one[here, 0:1]) * inverse_one
+        grad_norm = one_own[here, :] * (1.0 + mm(hot[here, :], own_pieces[1], ((1,), (0,))))
+        grad_tokens[here, :] += inverse_one * (grad_norm - flip[:, 0:1] - normed_one * flip[:, 1:2])
+    gmods.wait_recv(lambda other: gmod_own, gmod_all)
+    high, rest = split_two(gmod_all[...].reshape(tok_count * slots, gmod_all.shape[2]))
+    ada = ada_own[...]
+    part_own[...] = mm(high, ada, ((1,), (1,))) + mm(rest, ada, ((1,), (1,)))
+    owner = lax.div(tok_at, 2)
+    half = lax.rem(tok_at, 2)
+
+    def part_copy(source):
+        return remote(part_own, part_slots.at[source], part_send.at[0], part_recv.at[source], peer(mdl=owner))
+
+    pl.when(mdl_at != owner)(lambda: part_copy(mdl_at).start())
+    cond = cond_own[...]
+    grad_ada[...] = mm(cond, high, ((0,), (0,))) + mm(cond, rest, ((0,), (0,)))
+
+    def cond_copy(step):
+        other = lax.rem(tok_at + step, tok_count)
+        return remote(cond_slots.at[half], cond_slots.at[half], cond_send.at[step], cond_recv.at[half], peer(tok=other))
+
+    @pl.when(mdl_at == owner)
+    def _():
+        total = part_own[...]
+        for step in range(1, 4):
+            source = lax.rem(mdl_at + step, 4)
+            part_copy(source).wait_recv()
+            total = total + part_slots[source]
+        cond_slots[half] = total
+        for step in range(1, tok_count):
+            cond_copy(step).start()
+
+    for part, scatter in enumerate(scatters):
+        scatter.finish(head_grads.at[:, pl.ds(part * piece, piece)])
+    for side in range(2):
+        giver = 2 * mdl_at + side
+
+        @pl.when(tok_at != giver)
+        def _():
+            remote(cond_slots.at[side], cond_slots.at[side], cond_send.at[0], cond_recv.at[side], peer(tok=giver)).wait_recv()
+
+    grad_cond = jnp.concatenate([cond_slots[0], cond_slots[1]], axis=1)
+    embed = embedding[...]
+    gate = 1.0 / (1.0 + jnp.exp(-embed))
+    grad_embed[...] = grad_cond * gate * (1.0 + embed * (1.0 - gate))
+    gmods.wait_send(lambda other: gmod_own, gmod_all)
+    row_peers.wait_send(lambda other: row_sums.at[mdl_at], row_sums)
+    pl.when(mdl_at != owner)(lambda: part_copy(mdl_at).wait_send())
+
+    @pl.when(mdl_at == owner)
+    def _():
+        for step in range(1, tok_count):
+            cond_copy(step).wait_send()
+
+    for scatter in scatters:
+        scatter.wait_send()
+    for chunk in range(chunks):
+        ones.wait_send(chunk)
+
+
+def tail(
+    dq_heads, dk_heads, dv_heads, mod_one, qkv_full, grad_out, tokens, cotangent, branch_own, two_own, mlp_own, stats_one, stats_two,
+    hot, hot_keep, own_pieces, out_bias, down_bias, bias_sums, ada_own, cond_own, embedding, tok_count,
+):
+    rows, local_width = tokens.shape
+    width, three = qkv_full.shape
+    own_rows = width // tok_count
+    slots, mod_width = bias_sums.shape
+    crops = cond_own.shape[0]
+    chunks, pieces_count = 5, 3
+    total = three + grad_out.shape[1]
+    piece = total // pieces_count
+    dma = pltpu.SemaphoreType.DMA
+    vmem = pl.BlockSpec(memory_space=pltpu.VMEM)
+    low = lambda *shape: pltpu.VMEM(shape, bf16)
+    return pl.pallas_call(
+        tail_kernel,
+        out_shape=(
+            jax.ShapeDtypeStruct((rows, local_width), bf16),
+            jax.ShapeDtypeStruct((rows, local_width), f32),
+            jax.ShapeDtypeStruct((own_rows, total), f32),
+            jax.ShapeDtypeStruct((tok_count, slots, mod_width), f32),
+            jax.ShapeDtypeStruct((own_rows, mod_width), f32),
+            jax.ShapeDtypeStruct(embedding.shape, f32),
+        ),
+        in_specs=[vmem] * 22,
+        out_specs=(vmem,) * 6,
+        scratch_shapes=[
+            low(rows, three),
+            low(width, total),
+            low(4, rows, local_width),
+            low(2, rows, local_width),
+            low(rows, local_width),
+            low(rows, local_width),
+            pltpu.VMEM((rows, local_width), f32),
+            pltpu.VMEM((slots, mod_width), f32),
+            pltpu.VMEM((4, 8, rows), f32),
+            low(pieces_count, 4, own_rows, piece),
+            low(pieces_count, 4, own_rows, piece),
+            low(pieces_count, 4, own_rows, piece),
+            low(pieces_count, 4, own_rows, piece),
+            pltpu.VMEM((crops, own_rows), f32),
+            pltpu.VMEM((4, crops, own_rows), f32),
+            pltpu.VMEM((2, crops, own_rows), f32),
+            dma((pieces_count, 2, 4)),
+            dma((pieces_count, 3, 4)),
+            dma((3, chunks)),
+            dma((3, chunks)),
+            dma((4,)),
+            dma((4,)),
+            dma((tok_count,)),
+            dma((tok_count,)),
+            dma((1,)),
+            dma((4,)),
+            dma((tok_count,)),
+            dma((2,)),
+        ],
+        compiler_params=pltpu.CompilerParams(collective_id=1, has_side_effects=True, vmem_limit_bytes=63 * 2**20),
+    )(
+        dq_heads, dk_heads, dv_heads, mod_one, qkv_full, grad_out, tokens, cotangent, branch_own, two_own, mlp_own, stats_one, stats_two,
+        hot, hot_keep, own_pieces, out_bias, down_bias, bias_sums, ada_own, cond_own, embedding,
+    )
+
+
 def on_device(
     tokens,
     cotangent,
@@ -1310,6 +1533,7 @@
     chan_rows = rows32(jnp.repeat(chan_mask[0].astype(bf16), units_here // groups_here, axis=1))
 
     start_rows = tokens_full.astype(f32)
+    mean_one = jnp.mean(start_rows, axis=1, keepdims=True)
     normed_one, inverse_one = norm_rows(start_rows)
     modulated_one = (normed_one * (1.0 + spread(1)) + spread(0)).astype(bf16)
     projected = mm(modulated_one, qkv_full, ((1,), (0,)))
@@ -1330,7 +1554,6 @@
         branch_part, token_blocks, cot_blocks, hot, hot_keep, pieces, out_bias_full, unit_full, up_bias.astype(f32)[None], chan_rows
     )
     grad_up_bias = grad_up_bias[0]
-    grad_down_bias = own_cols(mlp_sums)[0]
     head_rows = rows32(jnp.repeat(head_mask[0].astype(bf16), head_width, axis=1))
 
     def by_head(rows_low):
@@ -1340,58 +1563,17 @@
         two_low, branch_low, token_blocks, cot_blocks, mlp_blocks, unit_grads, hot, pieces, out_bias_full, out_full, head_rows,
         attended, by_head(queries), by_head(key_rows), by_head(value_rows), logsum_rows, segment[0][:, None], segment, tok_count,
     )
-    own_pieces = lax.dynamic_slice_in_dim(mod_rows, mdl_at * local_width, local_width, axis=2)
-
-    def spread_own(part):
-        return exact_dot(crop_hot32, own_pieces[:, part])
-
-    mlp_out = mlp_own + down_bias.astype(f32)
-    branch_own = branch_own.astype(f32) + out_bias.astype(f32)
-    gate_one_own = spread_own(2)
-    middle_own = tokens.astype(f32) + gate_one_own * branch_own
-    output = (middle_own + spread_own(5) * keep_rows * mlp_out).astype(bf16)
-    normed_two_own = (middle_own - stats[:, 0:1]) * stats[:, 1:2]
-    two_own32 = two_own.astype(f32)
-    grad_middle_own = cotangent.astype(f32) + stats[:, 1:2] * (
-        two_own32 * (1.0 + spread_own(4)) - stats[:, 2:3] - normed_two_own * stats[:, 3:4]
-    )
-    grad_out_bias = own_cols(attn_sums)[0]
-    grad_qkv_rows = jnp.concatenate(
-        [jnp.transpose(part, (1, 0, 2)).reshape(row_len, local_width) for part in (dq_heads, dk_heads, dv_heads)], axis=1
-    )
-    grad_qkv = mm(modulated_one, grad_qkv_rows, ((0,), (0,)))
-    grad_bias_rows = jnp.sum(grad_qkv_rows.astype(f32), axis=0)
-    grad_qv_bias = jnp.stack([grad_bias_rows[:local_width], grad_bias_rows[2 * local_width :]], axis=0)
-    grad_heads = lax.psum_scatter(
-        jnp.concatenate([grad_qkv.astype(bf16), grad_out], axis=1), "tok", scatter_dimension=0, tiled=True
-    ).astype(f32)
-    grad_one = scatter_cols(mm(grad_qkv_rows, qkv_full, ((1,), (1,)))).astype(f32)
-    normed_one_own = own_cols(normed_one)
-    grad_norm = grad_one * (1.0 + spread_own(1))
-    totals = lax.psum(
-        jnp.stack([jnp.sum(grad_norm, axis=1), jnp.sum(grad_norm * normed_one_own, axis=1)]), "mdl"
-    )
-    grad_tokens = grad_middle_own + inverse_one * (
-        grad_norm - totals[0][:, None] / full_width - normed_one_own * totals[1][:, None] / full_width
-    )
-    grad_per_token = jnp.concatenate(
-        [
-            grad_one,
-            grad_one * normed_one_own,
-            grad_middle_own * branch_own,
-            two_own32,
-            two_own32 * normed_two_own,
-            cotangent.astype(f32) * keep_rows * mlp_out,
-        ],
-        axis=1,
-    )
-    grad_mod_own = lax.dot_general(
-        crop_hot32, grad_per_token, (((0,), (0,)), ((), ())), precision=lax.Precision.HIGHEST, preferred_element_type=f32
-    )
-    bias_row = jnp.concatenate([grad_qv_bias.reshape(-1), grad_out_bias, grad_up_bias, grad_down_bias])
+    own_pieces = lax.dynamic_slice_in_dim(pieces, mdl_at * local_width, local_width, axis=2)
+    bias_row = jnp.concatenate(
+        [jnp.zeros((2 * local_width,), f32), own_cols(attn_sums)[0], grad_up_bias, own_cols(mlp_sums)[0]]
+    )
     bias_row = jnp.pad(bias_row, (0, 2 * 6 * local_width - bias_row.shape[0])).reshape(2, 6 * local_width)
-    gmod_all, grad_ada, grad_embed = cond_back(
-        jnp.concatenate([grad_mod_own, bias_row], axis=0), ada_own, cond_own, embedding, tok_count
+    bias_sums = jnp.pad(bias_row, ((slot_count, 0), (0, 0)))
+    stats_one = jnp.concatenate([mean_one, inverse_one], axis=1)
+    output, grad_tokens, grad_heads, gmod_all, grad_ada, grad_embed = tail(
+        dq_heads, dk_heads, dv_heads, modulated_one, qkv_full, grad_out, tokens, cotangent, branch_own, two_own, mlp_own,
+        stats_one, stats, hot, hot_keep, own_pieces, out_bias.astype(f32)[None], down_bias.astype(f32)[None], bias_sums,
+        ada_own, cond_own, embedding, tok_count,
     )
     grad_ada = grad_ada.reshape(own_rows, 6, local_width)
     grad_ada_bias = jnp.sum(gmod_all[:, :slot_count], axis=(0, 1)).reshape(6, local_width)

time: 623 us -> 506 us (0.81)
  the two profiles are of different devices: /device:TPU:0 before, /device:TPU:25 now
where the time goes in v5:
time: 506 us; the launch traced here: 496 us
  Pallas kernels  379 us (75%)
  local copies, waits for them, and re-layouts  54 us (11%)
  matrix products  41.1 us (8%)
  other arithmetic  19.7 us (4%)
    pallas_call x1, Pallas kernels, gather_all(): pl.pallas_call(gather_kernel, out_shape=(jax.ShapeDtypeStruct((tok_count,...  111 us
    pallas_call x1, Pallas kernels, tail(): pl.pallas_call(tail_kernel, out_shape=(jax.ShapeDtypeStruct((rows, local_...  99.4 us
    pallas_call x1, Pallas kernels, back(): pl.pallas_call(back_kernel, out_shape=(jax.ShapeDtypeStruct((own_rows, un...  89.9 us
    pallas_call x1, Pallas kernels, feed(): pl.pallas_call(feed_kernel, out_shape=(jax.ShapeDtypeStruct((rows, width)...  79.1 us
    unnamed x102, local copies, waits for them, and re-layouts  17.7 us
    dot_general x1, matrix products, attend_row(): jnp.einsum('qhd,khd->hqk', queries, key_rows, preferred_element_type=f32)  11.2 us
    dot_general x1, matrix products, attend_row(): jnp.einsum('hqk,khd->qhd', prob_low, value_rows, preferred_element_type=f32)  11.2 us
    dot_general x4, matrix products, exact_dot(): jnp.dot(left, right, precision=lax.Precision.HIGHEST, preferred_element_t...  10.7 us

profile of v5, /device:TPU:25, one launch (start us, length us, event | category | flops | bytes accessed | tf_op | source)
XLA Modules:
  0.0 496.2 jit_solution(16215631234765734215)
XLA Ops:
  4.2 1.3 copy.97
  6.9 1.1 pad_maximum_fusion.unit_shard
  8.7 1.8 copy.100.cotangent
  12.0 111.0 %shard_map.308 = (f32[8,8,640]{2,1,0:T(8,128)S(1)}, f32[64,288]{1,0:T(8,128)S(1)}, bf16[64,144]{1,0:T(8,128)(2,1)S(1)}, f32[6,8,1152]{2,1,0:T(8,128)S(1)}, bf16[...) custom-call(f32[8,640]{1,0:T(8,128)S(1)} %copy-done.12, ...), custom_call_target="tpu_custom_call" | custom-call | tf_op jit(solution)/shard_map/pallas_call | solution.py:408
  123.1 2.3 slice_bitcast_fusion
  127.3 5.9 %concatenate.28 = bf16[1280,1152]{1,0:T(8,128)(2,1)S(1)} concatenate(bf16[1280,288]{1,0:T(8,128)(2,1)} %get-tuple-element.143, bf16[1280,288]{1,0:T(8,128)(2,1)} %get-tuple-element.142, bf16[1280,288]{1,0:T(8,128)(2,1)} %get-tuple-element.141, bf16[1280,288]{1,0:T(8,128)(2,1)} %get-tuple-element.140), dimensions={1} | concatenate | bytes 5898240 | tf_op jit(solution)/shard_map/concatenate | solution.py:1508
  134.4 4.1 fusion.3
  138.5 3.9 fusion.4.mod_one
  142.5 3.3 fusion.38
  147.4 11.2 %fusion.41 = (f32[4,1280]{1,0:T(4,128)S(1)}, f32[4,1280,1280]{1,2,0:T(8,128)}) fusion(bf16[1280,4,72]{0,2,1:T(8,128)(2,1)S(1)} %bitcast.69, bf16[1280,4,72]{0,2,1:T(8,128)(2,1)S(1)} %bitcast.71, pred[1280,1280]{0,1:T(8,128)(4,1)S(1)} %broadcast_compare_fusion), kind=kOutput, calls=%fused_computation.103 | convolution fusion | flops 963374080 | bytes 29347840 | tf_op jit(solution)/shard_map/qhd,khd->hqk/dot_general | solution.py:59
  158.6 10.6 %fusion.1 = f32[4,1280]{1,0:T(4,128)S(1)} fusion(f32[4,1280,1280]{1,2,0:T(8,128)} %get-tuple-element.154, f32[4,1280]{1,0:T(4,128)S(1)} %get-tuple-element.153), kind=kLoop, calls=%fused_computation.4 | loop fusion | flops 13102080 | bytes 26255360 | tf_op jit(solution)/shard_map/reduce_sum | solution.py:64
  169.4 11.2 %fusion.9 = bf16[1280,4,72]{0,2,1:T(8,128)(2,1)S(1)} fusion(bf16[1280,4,72]{0,2,1:T(8,128)(2,1)S(1)} %bitcast.67, f32[4,1280,1280]{1,2,0:T(8,128)} %get-tuple-element.154, f32[4,1280]{1,0:T(4,128)S(1)} %fusion.1, f32[4,1280]{1,0:T(4,128)S(1)} %get-tuple-element.153, f32[1280,4]{0,1:T(4,128)S(1)} %fusion.10), kind=kOutput, calls=%fused_computation.19 | convolution fusion | flops 964116480 | bytes 27750400 | tf_op jit(solution)/shard_map/hqk,khd->qhd/dot_general | solution.py:66
  180.6 3.6 convolution_convert_fusion.branch_part
  184.8 1.0 broadcast_multiply_fusion.hot_keep
  187.9 79.1 %shard_map.309 = (bf16[1280,1152]{1,0:T(8,128)(2,1)}, bf16[4,1280,288]{2,1,0:T(8,128)(2,1)}, bf16[1280,1152]{1,0:T(8,128)(2,1)}, bf16[1152,2304]{1,0:T(8,128)(2,...) custom-call(bf16[1280,1152]{1,0:T(8,128)(2,1)} %convolution_convert_fusion.branch_part, bf16[4,1280,288]{2,1,0:T(8,128)(2,1)} %copy-done.2, ...), custom_call_target="tpu_custom_call" | custom-call | tf_op jit(solution)/shard_map/pallas_call | solution.py:659
  267.0 2.7 slice.92.out_full
  270.6 2.2 copy.110.attended
  272.8 1.4 copy.106
  274.2 1.4 copy.107
  275.6 1.4 copy.108
  277.7 1.1 broadcast_in_dim_squeeze.6.seg_col
  279.4 89.9 %shard_map.310 = (f32[144,1152]{1,0:T(8,128)}, f32[144,1152]{1,0:T(8,128)}, f32[1280,288]{1,0:T(8,128)}, bf16[1152,288]{1,0:T(8,128)(2,1)}, bf16[4,1280,72]{2,1,...) custom-call(bf16[1280,1152]{1,0:T(8,128)(2,1)} %get-tuple-element.52, ...), custom_call_target="tpu_custom_call" | custom-call | tf_op jit(solution)/shard_map/pallas_call | solution.py:1067
  369.3 3.1 slice.86.qkv_full
  372.4 1.1 copy.114.stats_one
  373.6 1.7 constant_dynamic-slice_fusion.own_pieces
  377.4 99.4 %shard_map.311 = (bf16[1280,288]{1,0:T(8,128)(2,1)}, f32[1280,288]{1,0:T(8,128)}, f32[144,1152]{1,0:T(8,128)}, f32[8,8,1728]{2,1,0:T(8,128)}, f32[144,1728]{1,0:T(8,128)}, /*index=5*/f32[64,288]{1,0:T(8,128)}) custom-call(bf16[4,1280,72]{2,1,0:T(8,128)(2,1)} %get-tuple-element.56.dq_heads, bf16[4,1280,72]{2,1,0:T(8,128)(2,1)} %get-tuple-element.57.dk_heads, ...), custom_call_target="tpu_custom_call" | custom-call | tf_op jit(solution)/shard_map/pallas_call | solution.py:1388
  476.8 2.2 copy.116
  479.1 2.7 copy.117
  483.1 1.1 slice_reduce_fusion.1
  487.9 1.3 copy.119
  491.2 1.7 fusion.14
  493.0 2.0 copy.123
  (171 shorter events, 26.4 us)
Async XLA Ops:
  0.7 5.5 %copy-start.42 = (bf16[288]{0:T(512)(128)(2,1)S(1)}, bf16[288]{0:T(512)(128)(2,1)}, u32[]{:S(2)}) copy-start(bf16[288]{0:T(512)(128)(2,1)} %param.33) | copy-start | bytes 1732
  0.7 5.5 %copy-start.36 = (bf16[6,288]{1,0:T(8,128)(2,1)S(1)}, bf16[6,288]{1,0:T(8,128)(2,1)}, u32[]{:S(2)}) copy-start(bf16[6,288]{1,0:T(8,128)(2,1)} %param.39) | copy-start | bytes 10372
  0.7 6.1 %copy-start.33 = (bf16[288,144]{0,1:T(8,128)(2,1)S(1)}, bf16[288,144]{0,1:T(8,128)(2,1)}, u32[]{:S(2)}) copy-start(bf16[288,144]{0,1:T(8,128)(2,1)} %param.32) | copy-start | bytes 248836
  0.7 5.6 %copy-start.32 = (bf16[144,3,288]{2,0,1:T(8,128)(2,1)S(1)}, bf16[144,3,288]{2,0,1:T(8,128)(2,1)}, u32[]{:S(2)}) copy-start(bf16[144,3,288]{2,0,1:T(8,128)(2,1)} %param.30) | copy-start | bytes 746500
  4.2 3.8 copy-start.27
  6.2 4.3 copy-start.5
  6.2 4.3 copy-start.34
  8.7 116.7 %copy-start.3 = (bf16[1280,288]{1,0:T(8,128)(2,1)}, bf16[1280,288]{1,0:T(8,128)(2,1)S(1)}, u32[]{:S(2)}) copy-start(bf16[1280,288]{1,0:T(8,128)(2,1)S(1)} %copy.99.tokens) | copy-start | bytes 2211844
  12.0 113.4 %copy-start.4 = (bf16[1280,288]{1,0:T(8,128)(2,1)}, bf16[1280,288]{1,0:T(8,128)(2,1)S(1)}, u32[]{:S(2)}) copy-start(bf16[1280,288]{1,0:T(8,128)(2,1)S(1)} %copy.100.cotangent) | copy-start | bytes 2211844
  123.0 3.9 copy-start.6
  123.0 4.1 copy-start.8
  123.1 4.1 copy-start.9
  123.1 4.1 copy-start.11
  123.1 4.2 copy-start.13
  123.1 4.2 copy-start.15
  138.5 4.0 copy-start.7
  146.1 12.5 %copy-start.21 = (bf16[1280,288]{0,1:T(8,128)(2,1)}, bf16[1280,288]{0,1:T(8,128)(2,1)S(1)}, u32[]{:S(2)}) copy-start(bf16[1280,288]{0,1:T(8,128)(2,1)S(1)} %get-tuple-element.138) | copy-start | bytes 2211844
  146.2 23.2 %copy-start.19 = (bf16[1280,288]{0,1:T(8,128)(2,1)}, bf16[1280,288]{0,1:T(8,128)(2,1)S(1)}, u32[]{:S(2)}) copy-start(bf16[1280,288]{0,1:T(8,128)(2,1)S(1)} %get-tuple-element.139) | copy-start | bytes 2211844
  146.3 12.4 %copy-start.23 = (bf16[1280,288]{0,1:T(8,128)(2,1)}, bf16[1280,288]{0,1:T(8,128)(2,1)S(1)}, u32[]{:S(2)}) copy-start(bf16[1280,288]{0,1:T(8,128)(2,1)S(1)} %slice.144) | copy-start | bytes 2211844
  158.6 10.6 %copy-start.39 = (s32[1,6,4]{1,2,0:T(4,128)S(1)}, s32[1,6,4]{1,2,0:T(4,128)}, u32[]{:S(2)}) copy-start(s32[1,6,4]{1,2,0:T(4,128)} %param.27) | copy-start | bytes 292
  180.6 4.2 copy-start.35
  180.6 5.8 %copy-start.38 = (bf16[1152]{0:T(1024)(128)(2,1)S(1)}, bf16[1152]{0:T(1024)(128)(2,1)}, u32[]{:S(2)}) copy-start(bf16[1152]{0:T(1024)(128)(2,1)} %param.35) | copy-start | bytes 6916
  180.6 6.3 %copy-start.40 = (s32[1,6,4]{1,2,0:T(4,128)S(1)}, s32[1,6,4]{1,2,0:T(4,128)}, u32[]{:S(2)}) copy-start(s32[1,6,4]{1,2,0:T(4,128)} %param.28) | copy-start | bytes 292
  267.0 5.8 %copy-start.22 = (bf16[1280,288]{0,1:T(8,128)(2,1)S(1)}, bf16[1280,288]{0,1:T(8,128)(2,1)}, u32[]{:S(2)}) copy-start(bf16[1280,288]{0,1:T(8,128)(2,1)} %copy-done.21) | copy-start | bytes 2211844
  267.0 7.2 %copy-start.24 = (bf16[1280,288]{0,1:T(8,128)(2,1)S(1)}, bf16[1280,288]{0,1:T(8,128)(2,1)}, u32[]{:S(2)}) copy-start(bf16[1280,288]{0,1:T(8,128)(2,1)} %copy-done.23) | copy-start | bytes 2211844
  269.7 5.9 %copy-start.20 = (bf16[1280,288]{0,1:T(8,128)(2,1)S(1)}, bf16[1280,288]{0,1:T(8,128)(2,1)}, u32[]{:S(2)}) copy-start(bf16[1280,288]{0,1:T(8,128)(2,1)} %copy-done.19) | copy-start | bytes 2211844
  369.3 6.0 %copy-start.43 = (bf16[288]{0:T(512)(128)(2,1)S(1)}, bf16[288]{0:T(512)(128)(2,1)}, u32[]{:S(2)}) copy-start(bf16[288]{0:T(512)(128)(2,1)} %param.37) | copy-start | bytes 1732
  369.3 7.3 %copy-start.37 = (f32[1,1152]{1,0:T(1,128)S(1)}, f32[1,1152]{1,0:T(1,128)}, u32[]{:S(2)}) copy-start(f32[1,1152]{1,0:T(1,128)} %get-tuple-element.65) | copy-start | bytes 13828
  476.8 4.9 copy-start.26
  481.8 5.4 %copy-start.25 = (f32[144,1728]{1,0:T(8,128)S(1)}, f32[144,1728]{1,0:T(8,128)}, u32[]{:S(2)}) copy-start(f32[144,1728]{1,0:T(8,128)} %get-tuple-element.75) | copy-start | bytes 2985988
  487.8 7.1 %copy-start.30 = (f32[144,1152]{1,0:T(8,128)S(1)}, f32[144,1152]{1,0:T(8,128)}, u32[]{:S(2)}) copy-start(f32[144,1152]{1,0:T(8,128)} %get-tuple-element.74) | copy-start | bytes 1990660
  487.8 7.9 %copy-start.1 = (bf16[1000,288]{0,1:T(8,128)(2,1)S(1)}, bf16[1000,288]{0,1:T(8,128)(2,1)}, u32[]{:S(2)}) copy-start(bf16[1000,288]{0,1:T(8,128)(2,1)} %param.41) | copy-start | bytes 1728004
  (14 other events, 28.5 us)

commit v6 on v5

--- a/solution.py
+++ b/solution.py
@@ -254,7 +254,70 @@
             self.hand_copy(chunk).wait_send()
 
 
-def gather_kernel(
+class RowReduce:
+    def __init__(self, mdl_at, part, near_in, own_sum, far_in, full, sends, recvs):
+        self.part, self.near_in, self.own_sum, self.far_in, self.full = part, near_in, own_sum, far_in, full
+        self.sends, self.recvs = sends, recvs
+        self.core = lax.rem(mdl_at, 2)
+        self.far = peer(mdl=lax.rem(mdl_at + 2, 4))
+        self.near = peer(mdl=mdl_at + 1 - 2 * self.core)
+        self.half = near_in.shape[1]
+
+    def rows(self, chunk, core):
+        return pl.ds(pl.multiple_of((2 * chunk + core) * self.half, 128), self.half)
+
+    def near_copy(self, chunk):
+        source = self.part.at[self.rows(chunk, 1 - self.core), :]
+        return remote(source, self.near_in.at[chunk], self.sends.at[0, chunk], self.recvs.at[0, chunk], self.near)
+
+    def far_copy(self, chunk):
+        return remote(self.own_sum.at[chunk], self.far_in.at[chunk], self.sends.at[1, chunk], self.recvs.at[1, chunk], self.far)
+
+    def share_copy(self, chunk):
+        place = self.full.at[self.rows(chunk, self.core), :]
+        return remote(place, place, self.sends.at[2, chunk], self.recvs.at[2, chunk], self.near)
+
+    def first(self, chunk):
+        self.near_copy(chunk).start()
+
+    def second(self, chunk):
+        self.near_copy(chunk).wait_recv()
+        own = self.part[self.rows(chunk, self.core), :].astype(f32)
+        self.own_sum[chunk] = (own + self.near_in[chunk].astype(f32)).astype(bf16)
+        self.far_copy(chunk).start()
+
+    def third(self, chunk):
+        self.far_copy(chunk).wait_recv()
+        total = self.own_sum[chunk].astype(f32) + self.far_in[chunk].astype(f32)
+        self.full[self.rows(chunk, self.core), :] = total.astype(bf16)
+        self.share_copy(chunk).start()
+
+    def fourth(self, chunk):
+        place = self.full.at[self.rows(chunk, 1 - self.core), :]
+        remote(place, place, self.sends.at[2, chunk], self.recvs.at[2, chunk], self.near).wait_recv()
+
+    def wait_send(self, chunk):
+        self.near_copy(chunk).wait_send()
+        self.far_copy(chunk).wait_send()
+        self.share_copy(chunk).wait_send()
+
+
+def greet_quad(mdl_at):
+    barrier = pltpu.get_barrier_semaphore()
+    for step in range(1, 4):
+        pl.semaphore_signal(
+            barrier, inc=1, device_id=peer(mdl=lax.rem(mdl_at + step, 4)), device_id_type=pl.DeviceIdType.MESH
+        )
+    pl.semaphore_wait(barrier, 3)
+
+
+def centre(values):
+    center = values - jnp.mean(values, axis=1, keepdims=True)
+    inverse = lax.rsqrt(jnp.mean(center * center, axis=1, keepdims=True) + norm_floor)
+    return center * inverse, inverse
+
+
+def front_kernel(
     small_own,
     time_own,
     ada_own,
@@ -263,20 +326,42 @@
     unit_shard,
     tokens,
     cotangent,
+    hot,
+    head_rows,
+    qkv_bias,
+    seg_col,
+    seg_row,
     small_all,
     embedding_out,
     cond_out,
     mod_full,
     pieces,
+    unit_full,
+    cot_blocks,
+    tokens_full,
+    qkv_full,
+    out_full,
+    mod_one,
+    stats,
+    q_heads,
+    k_heads,
+    v_heads,
+    logsum,
+    attended,
+    branch_full,
     head_full,
-    unit_full,
     token_blocks,
-    cot_blocks,
     time_all,
     cond_blocks,
     mod_parts,
     mod_slots,
     mod_out,
+    v_flip,
+    att_heads,
+    branch_part,
+    near_in,
+    own_sum,
+    far_in,
     small_send,
     small_recv,
     time_send,
@@ -291,6 +376,8 @@
     line_recvs,
     quad_sends,
     quad_recvs,
+    sum_sends,
+    sum_recvs,
     own_sems,
 ):
     tok_at = lax.axis_index("tok")
@@ -299,6 +386,8 @@
     freq_count = time_all.shape[0] * time_all.shape[1]
     local_width = time_own.shape[1]
     own_rows = head_shard.shape[0]
+    heads, rows, head_width = q_heads.shape
+    score_scale = 1.0 / math.sqrt(head_width)
     greet(tok_at, mdl_at, tok_count, 4)
 
     small = AllToPeers("tok", tok_at, tok_count, small_send, small_recv)
@@ -306,28 +395,29 @@
     conds = AllToPeers("mdl", mdl_at, 4, cond_send, cond_recv)
     parts = AllToPeers("tok", tok_at, tok_count, part_send, part_recv)
     mods = AllToPeers("mdl", mdl_at, 4, mod_send, mod_recv)
-    heads = LineGather(
+    head_line = LineGather(
         tok_at, head_shard, head_full, own_rows, line_sends.at[0, 0], line_sends.at[0, 1], line_sends.at[0, 2], line_recvs.at[0]
     )
-    units = LineGather(
+    unit_line = LineGather(
         tok_at, unit_shard, unit_full, own_rows, line_sends.at[1, 0], line_sends.at[1, 1], line_sends.at[1, 2], line_recvs.at[1]
     )
     chunks = quad_recvs.shape[2]
-    chunk_rows = tokens.shape[0] // chunks
+    size = rows // chunks
     token_quad = QuadGather(
-        mdl_at, tokens, token_blocks, chunks, chunk_rows, quad_sends.at[0, 0], quad_sends.at[0, 1], quad_sends.at[0, 2], quad_recvs.at[0]
+        mdl_at, tokens, token_blocks, chunks, size, quad_sends.at[0, 0], quad_sends.at[0, 1], quad_sends.at[0, 2], quad_recvs.at[0]
     )
     cot_quad = QuadGather(
-        mdl_at, cotangent, cot_blocks, chunks, chunk_rows, quad_sends.at[1, 0], quad_sends.at[1, 1], quad_sends.at[1, 2], quad_recvs.at[1]
-    )
+        mdl_at, cotangent, cot_blocks, chunks, size, quad_sends.at[1, 0], quad_sends.at[1, 1], quad_sends.at[1, 2], quad_recvs.at[1]
+    )
+    branch = RowReduce(mdl_at, branch_part, near_in, own_sum, far_in, branch_full, sum_sends, sum_recvs)
 
     small.start(lambda other: small_own, small_all)
     times.start(lambda other: time_own, time_all)
     token_quad.start()
-    heads.start()
+    head_line.start()
     own_copies = (
-        pltpu.make_async_copy(head_shard, heads.slot(tok_at), own_sems.at[0]),
-        pltpu.make_async_copy(unit_shard, units.slot(tok_at), own_sems.at[1]),
+        pltpu.make_async_copy(head_shard, head_line.slot(tok_at), own_sems.at[0]),
+        pltpu.make_async_copy(unit_shard, unit_line.slot(tok_at), own_sems.at[1]),
         pltpu.make_async_copy(tokens, token_blocks.at[mdl_at], own_sems.at[2]),
         pltpu.make_async_copy(cotangent, cot_blocks.at[mdl_at], own_sems.at[3]),
     )
@@ -346,18 +436,17 @@
     embedding_out[...] = embedding
     cond_blocks[mdl_at] = (embedding / (1.0 + jnp.exp(-embedding))).astype(bf16)
     conds.start(lambda other: cond_blocks.at[mdl_at], cond_blocks)
-    heads.forward(1)
+    head_line.forward(1)
     conds.wait_recv(lambda other: cond_blocks.at[mdl_at], cond_blocks)
     cond_block = cond_blocks[lax.div(tok_at, 2)].astype(f32)
     cond_own = jnp.where(lax.rem(tok_at, 2) == 0, cond_block[:, :own_rows], cond_block[:, own_rows:]).astype(bf16)
     cond_out[...] = cond_own
     mod_parts[...] = mm(cond_own, ada_own[...], ((1,), (0,))).reshape(mod_parts.shape)
     parts.start(lambda other: mod_parts.at[other], mod_slots)
-    units.start()
-    cot_quad.start()
+    unit_line.start()
     for chunk in range(chunks):
         token_quad.hand(chunk)
-    heads.forward(2)
+    head_line.forward(2)
     mod_slots[tok_at] = mod_parts[tok_at]
     parts.wait_recv(lambda other: mod_parts.at[other], mod_slots)
     modulation = mod_slots[0]
@@ -365,67 +454,162 @@
         modulation = modulation + mod_slots[source]
     mod_out[mdl_at] = modulation + ada_bias[...]
     mods.start(lambda other: mod_out.at[mdl_at], mod_out)
-    heads.forward(3)
-    units.forward(1)
-    for chunk in range(chunks):
-        cot_quad.hand(chunk)
-    units.forward(2)
-    units.forward(3)
+    cot_quad.start()
+    head_line.forward(3)
     mods.wait_recv(lambda other: mod_out.at[mdl_at], mod_out)
     for part in range(6):
-        rows = jnp.concatenate([mod_out[at, :, part * local_width : (part + 1) * local_width] for at in range(4)], axis=1)
-        mod_full[part] = rows
-        split = [piece.astype(f32) for piece in split_three(rows)]
-        pieces[part] = jnp.concatenate(split + [jnp.zeros_like(rows)], axis=0).astype(bf16)
-    heads.arrive_across()
-    units.arrive_across()
+        joined = jnp.concatenate([mod_out[at, :, part * local_width : (part + 1) * local_width] for at in range(4)], axis=1)
+        mod_full[part] = joined
+        split = [piece.astype(f32) for piece in split_three(joined)]
+        pieces[part] = jnp.concatenate(split + [jnp.zeros_like(joined)], axis=0).astype(bf16)
     for chunk in range(chunks):
         token_quad.arrive_rest(chunk)
+    own_copies[0].wait()
+    own_copies[2].wait()
+    head_line.arrive_across()
+    qkv_full[...] = head_full[:, : 3 * local_width]
+    out_full[...] = head_full[:, 3 * local_width :]
+    unit_line.forward(1)
+
+    def span(chunk):
+        return pl.ds(pl.multiple_of(chunk * size, 128), size)
+
+    def project(chunk, carry):
+        here = span(chunk)
+        joined = jnp.concatenate([token_blocks[at, here, :] for at in range(4)], axis=1)
+        tokens_full[here, :] = joined
+        token_rows = joined.astype(f32)
+        hot_now = hot[here, :]
+        normed, inverse = centre(token_rows)
+        stats[here, 0:1] = jnp.mean(token_rows, axis=1, keepdims=True)
+        stats[here, 1:2] = inverse
+        scale = mm(hot_now, pieces[1], ((1,), (0,)))
+        mod_one[here, :] = (normed * (1.0 + scale) + mm(hot_now, pieces[0], ((1,), (0,)))).astype(bf16)
+        projected = (mm(mod_one[here, :], qkv_full[...], ((1,), (0,))) + qkv_bias[...]).astype(bf16)
+        for head in range(heads):
+            for kind, ref in enumerate((q_heads, k_heads, v_heads)):
+                start = kind * local_width + head * head_width
+                ref[head, here, :] = projected[:, start : start + head_width]
+        return carry
+
+    lax.fori_loop(0, chunks, project, 0)
+    for head in range(heads):
+        v_flip[head] = v_heads[head].T
+
+    def attend_step(at, carry):
+        chunk = lax.div(at, heads)
+        head = lax.rem(at, heads)
+        here = span(chunk)
+        scores = mm(k_heads[head], q_heads[head, here, :], ((1,), (1,)))
+        same = seg_col[...] == seg_row[0:1, here]
+        scores = jnp.where(same, scores * score_scale, unseen)
+        column_max = jnp.max(scores, axis=0, keepdims=True)
+        terms = jnp.exp(scores - column_max)
+        total = jnp.sum(terms, axis=0, keepdims=True)
+        logsum[pl.ds(head, 1), here] = column_max + jnp.log(total)
+        probs = (terms * (1.0 / total)).astype(bf16)
+        att_heads[head] = mm(v_flip[head], probs, ((1,), (0,))).T
+
+        @pl.when(head == heads - 1)
+        def _():
+            joined = jnp.concatenate([att_heads[which] for which in range(heads)], axis=1)
+            attended[here, :] = (joined * mm(hot[here, :], head_rows[...], ((1,), (0,)))).astype(bf16)
+            branch_part[here, :] = mm(attended[here, :], out_full[...], ((1,), (1,))).astype(bf16)
+            branch.first(chunk)
+            pl.when(chunk >= 2)(lambda: branch.third(chunk - 2))
+
+        @pl.when((head == 0) & (chunk >= 1))
+        def _():
+            branch.second(chunk - 1)
+
+        @pl.when(head == 1)
+        def _():
+            cot_quad.hand(chunk)
+
+        pl.when(at == 5)(lambda: unit_line.forward(2))
+        pl.when(at == 14)(lambda: unit_line.forward(3))
+        return carry
+
+    lax.fori_loop(0, chunks * heads, attend_step, 0)
+    branch.second(chunks - 1)
+    branch.third(chunks - 2)
+    branch.third(chunks - 1)
+    for chunk in range(chunks):
+        branch.fourth(chunk)
+    for chunk in range(chunks):
         cot_quad.arrive_rest(chunk)
+    unit_line.arrive_across()
     small.wait_send(lambda other: small_own, small_all)
     times.wait_send(lambda other: time_own, time_all)
     conds.wait_send(lambda other: cond_blocks.at[mdl_at], cond_blocks)
     parts.wait_send(lambda other: mod_parts.at[other], mod_slots)
     mods.wait_send(lambda other: mod_out.at[mdl_at], mod_out)
-    heads.wait_send()
-    units.wait_send()
+    head_line.wait_send()
+    unit_line.wait_send()
     token_quad.wait_send()
     cot_quad.wait_send()
-    for copy in own_copies:
-        copy.wait()
-
-
-def gather_all(small_own, time_weight, ada_own, ada_bias, head_shard, unit_shard, tokens, cotangent, tok_count):
+    for chunk in range(chunks):
+        branch.wait_send(chunk)
+    own_copies[1].wait()
+    own_copies[3].wait()
+
+
+def front(
+    small_own, time_weight, ada_own, ada_bias, head_shard, unit_shard, tokens, cotangent, hot, head_rows, qkv_bias, seg_col, seg_row,
+    heads, tok_count,
+):
     slots, small_width = small_own.shape
     freq_rows, local_width = time_weight.shape
     own_rows, mod_width = ada_own.shape
     rows = tokens.shape[0]
+    head_width = local_width // heads
     chunks = 5
+    size = rows // chunks
     whole = own_rows * tok_count
     dma = pltpu.SemaphoreType.DMA
     vmem = pl.BlockSpec(memory_space=pltpu.VMEM)
     anywhere = pl.BlockSpec(memory_space=pl.ANY)
+    low = lambda *shape: pltpu.VMEM(shape, bf16)
+    shape = jax.ShapeDtypeStruct
+    head_shape = shape((heads, rows, head_width), bf16)
     return pl.pallas_call(
-        gather_kernel,
+        front_kernel,
         out_shape=(
-            jax.ShapeDtypeStruct((tok_count, slots, small_width), f32),
-            jax.ShapeDtypeStruct((tok_count * slots, local_width), f32),
-            jax.ShapeDtypeStruct((tok_count * slots, own_rows), bf16),
-            jax.ShapeDtypeStruct((6, slots, whole), f32),
-            jax.ShapeDtypeStruct((6, 4 * slots, whole), bf16),
-            jax.ShapeDtypeStruct((whole, head_shard.shape[1]), bf16),
-            jax.ShapeDtypeStruct((whole, unit_shard.shape[1]), bf16),
-            jax.ShapeDtypeStruct((4, rows, local_width), bf16),
-            jax.ShapeDtypeStruct((4, rows, local_width), bf16),
+            shape((tok_count, slots, small_width), f32),
+            shape((tok_count * slots, local_width), f32),
+            shape((tok_count * slots, own_rows), bf16),
+            shape((6, slots, whole), f32),
+            shape((6, 4 * slots, whole), bf16),
+            shape((whole, unit_shard.shape[1]), bf16),
+            shape((4, rows, local_width), bf16),
+            shape((rows, whole), bf16),
+            shape((whole, 3 * local_width), bf16),
+            shape((whole, local_width), bf16),
+            shape((rows, whole), bf16),
+            shape((rows, 128), f32),
+            head_shape,
+            head_shape,
+            head_shape,
+            shape((heads, rows), f32),
+            shape((rows, local_width), bf16),
+            shape((rows, whole), bf16),
         ),
-        in_specs=[vmem] * 8,
-        out_specs=(vmem, vmem, vmem, vmem, vmem, anywhere, anywhere, anywhere, anywhere),
+        in_specs=[vmem] * 13,
+        out_specs=(vmem,) * 5 + (anywhere,) * 2 + (vmem,) * 11,
         scratch_shapes=[
-            pltpu.VMEM((tok_count, freq_rows, local_width), bf16),
-            pltpu.VMEM((4, tok_count * slots, local_width), bf16),
+            low(whole, head_shard.shape[1]),
+            low(4, rows, local_width),
+            low(tok_count, freq_rows, local_width),
+            low(4, tok_count * slots, local_width),
             pltpu.VMEM((tok_count, slots, mod_width), f32),
             pltpu.VMEM((tok_count, slots, mod_width), f32),
             pltpu.VMEM((4, slots, mod_width), f32),
+            low(heads, head_width, rows),
+            pltpu.VMEM((heads, size, head_width), f32),
+            low(rows, whole),
+            low(chunks, size // 2, whole),
+            low(chunks, size // 2, whole),
+            low(chunks, size // 2, whole),
             dma((tok_count,)),
             dma((tok_count,)),
             dma((tok_count,)),
@@ -440,78 +624,17 @@
             dma((2, tok_count)),
             dma((2, 3, chunks)),
             dma((2, 4, chunks)),
+            dma((3, chunks)),
+            dma((3, chunks)),
             dma((4,)),
         ],
-        compiler_params=pltpu.CompilerParams(collective_id=0, has_side_effects=True, vmem_limit_bytes=40 * 2**20),
-    )(small_own, time_weight, ada_own, ada_bias, head_shard, unit_shard, tokens, cotangent)
-
-
-class RowReduce:
-    def __init__(self, mdl_at, part, near_in, own_sum, far_in, full, sends, recvs):
-        self.part, self.near_in, self.own_sum, self.far_in, self.full = part, near_in, own_sum, far_in, full
-        self.sends, self.recvs = sends, recvs
-        self.core = lax.rem(mdl_at, 2)
-        self.far = peer(mdl=lax.rem(mdl_at + 2, 4))
-        self.near = peer(mdl=mdl_at + 1 - 2 * self.core)
-        self.half = near_in.shape[1]
-
-    def rows(self, chunk, core):
-        return pl.ds(pl.multiple_of((2 * chunk + core) * self.half, 128), self.half)
-
-    def near_copy(self, chunk):
-        source = self.part.at[self.rows(chunk, 1 - self.core), :]
-        return remote(source, self.near_in.at[chunk], self.sends.at[0, chunk], self.recvs.at[0, chunk], self.near)
-
-    def far_copy(self, chunk):
-        return remote(self.own_sum.at[chunk], self.far_in.at[chunk], self.sends.at[1, chunk], self.recvs.at[1, chunk], self.far)
-
-    def share_copy(self, chunk):
-        place = self.full.at[self.rows(chunk, self.core), :]
-        return remote(place, place, self.sends.at[2, chunk], self.recvs.at[2, chunk], self.near)
-
-    def first(self, chunk):
-        self.near_copy(chunk).start()
-
-    def second(self, chunk):
-        self.near_copy(chunk).wait_recv()
-        own = self.part[self.rows(chunk, self.core), :].astype(f32)
-        self.own_sum[chunk] = (own + self.near_in[chunk].astype(f32)).astype(bf16)
-        self.far_copy(chunk).start()
-
-    def third(self, chunk):
-        self.far_copy(chunk).wait_recv()
-        total = self.own_sum[chunk].astype(f32) + self.far_in[chunk].astype(f32)
-        self.full[self.rows(chunk, self.core), :] = total.astype(bf16)
-        self.share_copy(chunk).start()
-
-    def fourth(self, chunk):
-        place = self.full.at[self.rows(chunk, 1 - self.core), :]
-        remote(place, place, self.sends.at[2, chunk], self.recvs.at[2, chunk], self.near).wait_recv()
-
-    def wait_send(self, chunk):
-        self.near_copy(chunk).wait_send()
-        self.far_copy(chunk).wait_send()
-        self.share_copy(chunk).wait_send()
-
-
-def greet_quad(mdl_at):
-    barrier = pltpu.get_barrier_semaphore()
-    for step in range(1, 4):
-        pl.semaphore_signal(
-            barrier, inc=1, device_id=peer(mdl=lax.rem(mdl_at + step, 4)), device_id_type=pl.DeviceIdType.MESH
-        )
-    pl.semaphore_wait(barrier, 3)
-
-
-def centre(values):
-    center = values - jnp.mean(values, axis=1, keepdims=True)
-    inverse = lax.rsqrt(jnp.mean(center * center, axis=1, keepdims=True) + norm_floor)
-    return center * inverse, inverse
+        compiler_params=pltpu.CompilerParams(collective_id=0, has_side_effects=True, vmem_limit_bytes=63 * 2**20),
+    )(small_own, time_weight, ada_own, ada_bias, head_shard, unit_shard, tokens, cotangent, hot, head_rows, qkv_bias, seg_col, seg_row)
 
 
 def feed_kernel(
-    branch_part,
-    token_blocks,
+    branch_full,
+    tokens_full,
     cot_blocks,
     hot,
     hot_keep,
@@ -520,7 +643,6 @@
     unit_full,
     up_bias,
     chan_rows,
-    branch_full,
     mlp_part,
     two_full,
     unit_grads,
@@ -544,33 +666,27 @@
 ):
     mdl_at = lax.axis_index("mdl")
     rows, width = two_full.shape
-    chunks = near_in.shape[1]
+    chunks = near_in.shape[0]
     size = rows // chunks
     units = up_bias.shape[1]
-    local_width = token_blocks.shape[2]
+    local_width = cot_blocks.shape[2]
     greet_quad(mdl_at)
-    branch = RowReduce(mdl_at, branch_part, near_in.at[0], own_sum.at[0], far_in.at[0], branch_full, sends.at[0], recvs.at[0])
-    twos = RowReduce(mdl_at, two_part, near_in.at[1], own_sum.at[1], far_in.at[1], two_full, sends.at[1], recvs.at[1])
+    twos = RowReduce(mdl_at, two_part, near_in, own_sum, far_in, two_full, sends, recvs)
 
     def span(chunk):
         return pl.ds(pl.multiple_of(chunk * size, 128), size)
 
     def loads(chunk, slot):
         return (
-            pltpu.make_async_copy(token_blocks.at[:, span(chunk), :], token_buf.at[slot], load_sems.at[0, slot]),
+            pltpu.make_async_copy(tokens_full.at[span(chunk), :], token_buf.at[slot], load_sems.at[0, slot]),
             pltpu.make_async_copy(cot_blocks.at[:, span(chunk), :], cot_buf.at[slot], load_sems.at[1, slot]),
         )
 
     def store(chunk, slot):
         return pltpu.make_async_copy(mlp_buf.at[slot], mlp_part.at[:, span(chunk), :], store_sems.at[slot])
 
-    for chunk in range(chunks):
-        branch.first(chunk)
     for copy in loads(0, 0):
         copy.start()
-    for chunk in range(chunks):
-        branch.second(chunk)
-    branch.third(0)
     up_bias_grad[...] = jnp.zeros_like(up_bias_grad)
     mlp_sums[...] = jnp.zeros_like(mlp_sums)
 
@@ -581,18 +697,16 @@
         def _():
             for copy in loads(chunk + 1, 1 - slot):
                 copy.start()
-            branch.third(chunk + 1)
 
         for copy in loads(chunk, slot):
             copy.wait()
-        branch.fourth(chunk)
         here = span(chunk)
         hot_now = hot[here, :]
 
         def spread(part):
             return mm(hot_now, pieces[part], ((1,), (0,)))
 
-        token_rows = jnp.concatenate([token_buf[slot, at] for at in range(4)], axis=1).astype(f32)
+        token_rows = token_buf[slot].astype(f32)
         middle = token_rows + spread(2) * (branch_full[here, :].astype(f32) + out_bias[...])
         normed, inverse = centre(middle)
         mod_rows[here, :] = (normed * (1.0 + spread(4)) + spread(3)).astype(bf16)
@@ -641,15 +755,14 @@
     for chunk in range(chunks):
         twos.fourth(chunk)
         twos.wait_send(chunk)
-        branch.wait_send(chunk)
     store(chunks - 2, (chunks - 2) % 2).wait()
     store(chunks - 1, (chunks - 1) % 2).wait()
 
 
-def feed(branch_part, token_blocks, cot_blocks, hot, hot_keep, pieces, out_bias, unit_full, up_bias, chan_rows):
-    rows, width = branch_part.shape
+def feed(branch_full, tokens_full, cot_blocks, hot, hot_keep, pieces, out_bias, unit_full, up_bias, chan_rows):
+    rows, width = branch_full.shape
     units = up_bias.shape[1]
-    local_width = token_blocks.shape[2]
+    local_width = cot_blocks.shape[2]
     chunks = 5
     size = rows // chunks
     dma = pltpu.SemaphoreType.DMA
@@ -659,7 +772,6 @@
     return pl.pallas_call(
         feed_kernel,
         out_shape=(
-            jax.ShapeDtypeStruct((rows, width), bf16),
             jax.ShapeDtypeStruct((4, rows, local_width), bf16),
             jax.ShapeDtypeStruct((rows, width), bf16),
             jax.ShapeDtypeStruct((width, 2 * units), bf16),
@@ -667,9 +779,9 @@
             jax.ShapeDtypeStruct((1, width), f32),
         ),
         in_specs=[vmem, anywhere, anywhere] + [vmem] * 7,
-        out_specs=(vmem, anywhere, vmem, vmem, vmem, vmem),
+        out_specs=(anywhere, vmem, vmem, vmem, vmem),
         scratch_shapes=[
-            low(2, 4, size, local_width),
+            low(2, size, width),
             low(2, 4, size, local_width),
             low(rows, width),
             low(rows, units),
@@ -677,16 +789,16 @@
             low(rows, width),
             low(rows, width),
             low(2, 4, size, local_width),
-            low(2, chunks, size // 2, width),
-            low(2, chunks, size // 2, width),
-            low(2, chunks, size // 2, width),
-            dma((2, 3, chunks)),
-            dma((2, 3, chunks)),
+            low(chunks, size // 2, width),
+            low(chunks, size // 2, width),
+            low(chunks, size // 2, width),
+            dma((3, chunks)),
+            dma((3, chunks)),
             dma((2, 2)),
             dma((2,)),
         ],
         compiler_params=pltpu.CompilerParams(collective_id=2, has_side_effects=True, vmem_limit_bytes=63 * 2**20),
-    )(branch_part, token_blocks, cot_blocks, hot, hot_keep, pieces, out_bias, unit_full, up_bias, chan_rows)
+    )(branch_full, tokens_full, cot_blocks, hot, hot_keep, pieces, out_bias, unit_full, up_bias, chan_rows)
 
 
 class ColumnReduce:
@@ -844,7 +956,7 @@
 def back_kernel(
     two_full,
     branch_full,
-    token_blocks,
+    tokens_full,
     cot_blocks,
     mlp_blocks,
     unit_grads,
@@ -937,7 +1049,7 @@
 
     def loads(chunk, slot):
         return (
-            pltpu.make_async_copy(token_blocks.at[:, span(chunk), :], token_buf.at[slot], load_sems.at[0, slot]),
+            pltpu.make_async_copy(tokens_full.at[span(chunk), :], token_buf.at[slot], load_sems.at[0, slot]),
             pltpu.make_async_copy(cot_blocks.at[:, span(chunk), :], cot_buf.at[slot], load_sems.at[1, slot]),
         )
 
@@ -968,7 +1080,7 @@
         def spread(part):
             return mm(hot_now, pieces[part], ((1,), (0,)))
 
-        token_rows = jnp.concatenate([token_buf[slot, at] for at in range(4)], axis=1).astype(f32)
+        token_rows = token_buf[slot].astype(f32)
         gate_one = spread(2)
         middle = token_rows + gate_one * (branch_full[here, :].astype(f32) + out_bias[...])
         row_mean = jnp.mean(middle, axis=1, keepdims=True)
@@ -1051,7 +1163,7 @@
         mlps.wait_send(chunk)
 
 
-def back(two_full, branch_full, token_blocks, cot_blocks, mlp_blocks, unit_grads, hot, pieces, out_bias, out_full, head_rows, attended, q_heads, k_heads, v_heads, logsum, seg_col, seg_row, tok_count):
+def back(two_full, branch_full, tokens_full, cot_blocks, mlp_blocks, unit_grads, hot, pieces, out_bias, out_full, head_rows, attended, q_heads, k_heads, v_heads, logsum, seg_col, seg_row, tok_count):
     rows, width = two_full.shape
     units = unit_grads.shape[1] // 2
     heads, _, head_width = q_heads.shape
@@ -1082,7 +1194,7 @@
         in_specs=[vmem, vmem, anywhere, anywhere, anywhere] + [vmem] * 13,
         out_specs=(vmem,) * 11,
         scratch_shapes=[
-            low(2, 4, size, local_width),
+            low(2, size, width),
             low(2, 4, size, local_width),
             low(heads, rows, head_width),
             low(heads, head_width, rows),
@@ -1105,7 +1217,7 @@
             dma((3, chunks)),
         ],
         compiler_params=pltpu.CompilerParams(collective_id=3, has_side_effects=True, vmem_limit_bytes=63 * 2**20),
-    )(two_full, branch_full, token_blocks, cot_blocks, mlp_blocks, unit_grads, hot, pieces, out_bias, out_full, head_rows, attended, q_heads, k_heads, v_heads, logsum, seg_col, seg_row)
+    )(two_full, branch_full, tokens_full, cot_blocks, mlp_blocks, unit_grads, hot, pieces, out_bias, out_full, head_rows, attended, q_heads, k_heads, v_heads, logsum, seg_col, seg_row)
 
 
 def tail_kernel(
@@ -1497,71 +1609,54 @@
     )
     head_shard = jnp.concatenate([qkv_weight.reshape(own_rows, 3 * local_width), out_weight.T], axis=1)
     unit_shard = jnp.concatenate([up_weight, down_weight.T], axis=1)
-    small_all, embedding, cond_own, mod_full, pieces, head_full, unit_full, token_blocks, cot_blocks = gather_all(
-        small_own, time_weight, ada_own, bias_rows, head_shard, unit_shard, tokens, cotangent, tok_count
+    inside, segment = crop_layout(lengths, padding, row_len)
+    crop_hot = inside[0].astype(bf16)
+    hot_one = jnp.pad(crop_hot, ((0, 0), (0, slots - slot_count)))
+    hot = jnp.concatenate([hot_one] * 3 + [jnp.zeros_like(hot_one)], axis=1)
+    hot_keep = hot * keep_mask.astype(bf16)[:, None]
+
+    def rows32(rows_low):
+        return jnp.pad(rows_low, ((0, 4 * slots - slot_count), (0, 0)))
+
+    chan_rows = rows32(jnp.repeat(chan_mask[0].astype(bf16), units_here // groups_here, axis=1))
+    head_rows = rows32(jnp.repeat(head_mask[0].astype(bf16), head_width, axis=1))
+    qkv_bias = jnp.concatenate([qv_bias[0], jnp.zeros_like(qv_bias[0]), qv_bias[1]]).astype(f32)[None]
+    (
+        small_all,
+        embedding,
+        cond_own,
+        mod_full,
+        pieces,
+        unit_full,
+        cot_blocks,
+        tokens_full,
+        qkv_full,
+        out_full,
+        modulated_one,
+        stats_one,
+        q_heads,
+        k_heads,
+        v_heads,
+        logsum_rows,
+        attended,
+        branch_low,
+    ) = front(
+        small_own, time_weight, ada_own, bias_rows, head_shard, unit_shard, tokens, cotangent, hot, head_rows, qkv_bias,
+        segment[0][:, None], segment, heads_here, tok_count,
     )
     all_crops = tok_count * slots
     real_crop = (jnp.arange(all_crops, dtype=jnp.int32) % slots < slot_count)[:, None]
     step_feats = small_all[:, :, :freq_count].reshape(all_crops, freq_count)
     label_all = small_all[:, :, freq_count + local_width].reshape(all_crops).astype(jnp.int32)
     label_hot = ((label_all[:, None] == jnp.arange(class_table.shape[0], dtype=jnp.int32)[None, :]) & real_crop).astype(f32)
-    tokens_full = jnp.concatenate([token_blocks[at] for at in range(4)], axis=1)
-    qkv_full, out_full = head_full[:, : 3 * local_width], head_full[:, 3 * local_width :]
-    out_bias_full = mod_full[0, slot_count :slot_count + 1]
-    mod_rows = jnp.transpose(mod_full[:, :slot_count], (1, 0, 2))
-
-    inside, segment = crop_layout(lengths, padding, row_len)
-    crop_hot = inside[0].astype(bf16)
-    crop_hot32 = inside[0].astype(f32)
-
-    def spread(part):
-        return exact_dot(crop_hot32, mod_rows[:, part])
-
-    head_tok = mm(crop_hot, head_mask[0].astype(bf16), ((1,), (0,)))
-    head_units = jnp.repeat(head_tok, head_width, axis=1).astype(bf16)
-    chan_tok = mm(crop_hot, chan_mask[0].astype(bf16), ((1,), (0,)))
-    chan_units = jnp.repeat(chan_tok, units_here // groups_here, axis=1)
-    keep_rows = keep_mask.astype(f32)[:, None]
-
-    hot_one = jnp.pad(crop_hot, ((0, 0), (0, slots - slot_count)))
-    hot = jnp.concatenate([hot_one] * 3 + [jnp.zeros_like(hot_one)], axis=1)
-    hot_keep = hot * keep_mask.astype(bf16)[:, None]
-
-    def rows32(rows_low):
-        return jnp.pad(rows_low, ((0, 4 * slots - slot_count), (0, 0)))
-
-    chan_rows = rows32(jnp.repeat(chan_mask[0].astype(bf16), units_here // groups_here, axis=1))
-
-    start_rows = tokens_full.astype(f32)
-    mean_one = jnp.mean(start_rows, axis=1, keepdims=True)
-    normed_one, inverse_one = norm_rows(start_rows)
-    modulated_one = (normed_one * (1.0 + spread(1)) + spread(0)).astype(bf16)
-    projected = mm(modulated_one, qkv_full, ((1,), (0,)))
-    qv_bias32 = qv_bias.astype(f32)
-    queries = (projected[:, :local_width] + qv_bias32[0]).astype(bf16)
-    key_rows = projected[:, local_width : 2 * local_width].astype(bf16)
-    value_rows = (projected[:, 2 * local_width :] + qv_bias32[1]).astype(bf16)
-
-    def heads(rows):
-        return rows.reshape(row_len, heads_here, head_width)
-
-    attend_now, logsum_rows = attend_row(
-        heads(queries), heads(key_rows), heads(value_rows), segment[0], score_scale
-    )
-    attended = (attend_now.reshape(row_len, local_width) * head_units.astype(f32)).astype(bf16)
-    branch_part = mm(attended, out_full, ((1,), (1,))).astype(bf16)
-    branch_low, mlp_blocks, two_low, unit_grads, grad_up_bias, mlp_sums = feed(
-        branch_part, token_blocks, cot_blocks, hot, hot_keep, pieces, out_bias_full, unit_full, up_bias.astype(f32)[None], chan_rows
+    out_bias_full = mod_full[0, slot_count : slot_count + 1]
+    mlp_blocks, two_low, unit_grads, grad_up_bias, mlp_sums = feed(
+        branch_low, tokens_full, cot_blocks, hot, hot_keep, pieces, out_bias_full, unit_full, up_bias.astype(f32)[None], chan_rows
     )
     grad_up_bias = grad_up_bias[0]
-    head_rows = rows32(jnp.repeat(head_mask[0].astype(bf16), head_width, axis=1))
-
-    def by_head(rows_low):
-        return jnp.transpose(heads(rows_low), (1, 0, 2))
-
     grad_up, grad_down, mlp_own, grad_out, dq_heads, dk_heads, dv_heads, branch_own, two_own, stats, attn_sums = back(
-        two_low, branch_low, token_blocks, cot_blocks, mlp_blocks, unit_grads, hot, pieces, out_bias_full, out_full, head_rows,
-        attended, by_head(queries), by_head(key_rows), by_head(value_rows), logsum_rows, segment[0][:, None], segment, tok_count,
+        two_low, branch_low, tokens_full, cot_blocks, mlp_blocks, unit_grads, hot, pieces, out_bias_full, out_full, head_rows,
+        attended, q_heads, k_heads, v_heads, logsum_rows, segment[0][:, None], segment, tok_count,
     )
     own_pieces = lax.dynamic_slice_in_dim(pieces, mdl_at * local_width, local_width, axis=2)
     bias_row = jnp.concatenate(
@@ -1569,7 +1664,6 @@
     )
     bias_row = jnp.pad(bias_row, (0, 2 * 6 * local_width - bias_row.shape[0])).reshape(2, 6 * local_width)
     bias_sums = jnp.pad(bias_row, ((slot_count, 0), (0, 0)))
-    stats_one = jnp.concatenate([mean_one, inverse_one], axis=1)
     output, grad_tokens, grad_heads, gmod_all, grad_ada, grad_embed = tail(
         dq_heads, dk_heads, dv_heads, modulated_one, qkv_full, grad_out, tokens, cotangent, branch_own, two_own, mlp_own,
         stats_one, stats, hot, hot_keep, own_pieces, out_bias.astype(f32)[None], down_bias.astype(f32)[None], bias_sums,

time: 506 us -> 417 us (0.82)
  the two profiles are of different devices: /device:TPU:25 before, /device:TPU:0 now
where the time goes in v6:
time: 417 us; the launch traced here: 415 us
  Pallas kernels  374 us (90%)
  local copies, waits for them, and re-layouts  28.2 us (7%)
  other arithmetic  7.79 us (2%)
  matrix products  4.47 us (1%)
    pallas_call x1, Pallas kernels, front(): pl.pallas_call(front_kernel, out_shape=(shape((tok_count, slots, small_wi...  132 us
    pallas_call x1, Pallas kernels, tail(): pl.pallas_call(tail_kernel, out_shape=(jax.ShapeDtypeStruct((rows, local_...  97.9 us
    pallas_call x1, Pallas kernels, back(): pl.pallas_call(back_kernel, out_shape=(jax.ShapeDtypeStruct((own_rows, un...  87.6 us
    pallas_call x1, Pallas kernels, feed(): pl.pallas_call(feed_kernel, out_shape=(jax.ShapeDtypeStruct((4, rows, loc...  56.2 us
    unnamed x70, local copies, waits for them, and re-layouts  10.2 us

profile of v6, /device:TPU:0, one launch (start us, length us, event | category | flops | bytes accessed | tf_op | source)
XLA Modules:
  0.0 415.1 jit_solution(198819921866902702)
XLA Ops:
  0.7 0.8 add.38
  1.6 0.7 subtract_bitcast_fusion
  2.6 0.9 copy.85.hot
  3.6 1.1 broadcast_in_dim_squeeze.6.seg_col
  5.3 0.7 convert_bitcast_fusion.2
  6.1 0.9 fusion.8
  7.1 0.7 select_maximum_fusion.1.small_own
  8.7 1.4 reshape.253.ada_own
  10.1 1.3 copy.83.tokens
  11.4 1.3 copy.84.cotangent
  14.8 0.8 pad_maximum_fusion.1.head_shard
  15.7 0.9 pad_maximum_fusion.unit_shard
  16.6 131.8 %shard_map.308 = (f32[8,8,640]{2,1,0:T(8,128)}, f32[64,288]{1,0:T(8,128)}, bf16[64,144]{1,0:T(8,128)(2,1)}, f32[6,8,1152]{2,1,0:T(8,128)}, bf16[6,32,1152]{2,1,0...) custom-call(f32[8,640]{1,0:T(8,128)} %select_maximum_fusion.1.small_, ...), custom_call_target="tpu_custom_call" | custom-call | tf_op jit(solution)/shard_map/pallas_call | solution.py:575
  148.4 1.4 slice_bitcast_fusion.2.out_bias
  149.8 1.0 broadcast_multiply_fusion.hot_keep
  152.3 56.2 %shard_map.309 = (bf16[4,1280,288]{2,1,0:T(8,128)(2,1)}, bf16[1280,1152]{1,0:T(8,128)(2,1)}, bf16[1152,2304]{1,0:T(8,128)(2,1)}, f32[1,1152]{1,0:T(1,128)}, f32[1,1152]{1,0:T(1,128)}) custom-call(bf16[1280,1152]{1,0:T(8,128)(2,1)} %get-tuple-element.54.branch_full, bf16[1280,1152]{1,0:T(8,128)(2,1)} %get-tuple-element.55.tokens_full, ...), custom_call_target="tpu_custom_call" | custom-call | tf_op jit(solution)/shard_map/pallas_call | solution.py:772
  208.6 87.6 %shard_map.310 = (f32[144,1152]{1,0:T(8,128)}, f32[144,1152]{1,0:T(8,128)}, f32[1280,288]{1,0:T(8,128)}, bf16[1152,288]{1,0:T(8,128)(2,1)}, bf16[4,1280,72]{2,1,...) custom-call(bf16[1280,1152]{1,0:T(8,128)(2,1)} %get-tuple-element.60, ...), custom_call_target="tpu_custom_call" | custom-call | tf_op jit(solution)/shard_map/pallas_call | solution.py:1179
  296.2 0.8 dynamic-slice_reduce_fusion
  297.9 1.7 constant_dynamic-slice_fusion.own_pieces
  300.1 97.9 %shard_map.311 = (bf16[1280,288]{1,0:T(8,128)(2,1)}, f32[1280,288]{1,0:T(8,128)}, f32[144,1152]{1,0:T(8,128)}, f32[8,8,1728]{2,1,0:T(8,128)}, f32[144,1728]{1,0:T(8,128)}, /*index=5*/f32[64,288]{1,0:T(8,128)}) custom-call(bf16[4,1280,72]{2,1,0:T(8,128)(2,1)} %get-tuple-element.69.dq_heads, bf16[4,1280,72]{2,1,0:T(8,128)(2,1)} %get-tuple-element.70.dk_heads, ...), custom_call_target="tpu_custom_call" | custom-call | tf_op jit(solution)/shard_map/pallas_call | solution.py:1500
  398.5 2.6 fusion.1
  401.1 0.9 fusion.6
  402.1 0.7 reshape.260
  402.8 1.3 copy.98
  404.6 0.9 copy.97
  405.8 1.6 copy.96
  407.5 1.2 copy.95
  408.7 1.8 slice_bitcast_fusion
  411.4 0.7 slice.58
  412.7 0.7 reshape.261
  413.4 0.8 copy.101
  414.3 0.8 copy.102
  (114 shorter events, 10.2 us)
Async XLA Ops:
  0.6 5.4 %copy-start = (bf16[1000,288]{0,1:T(8,128)(2,1)S(1)}, bf16[1000,288]{0,1:T(8,128)(2,1)}, u32[]{:S(2)}) copy-start(bf16[1000,288]{0,1:T(8,128)(2,1)} %param.41) | copy-start | bytes 1728004
  0.7 6.3 %copy-start.29 = (s32[1,6]{1,0:T(1,128)S(1)}, s32[1,6]{1,0:T(1,128)}, u32[]{:S(2)}) copy-start(s32[1,6]{1,0:T(1,128)} %param.26) | copy-start | bytes 76
  0.7 7.1 %copy-start.22 = (bf16[2,288]{1,0:T(2,128)(2,1)S(1)}, bf16[2,288]{1,0:T(2,128)(2,1)}, u32[]{:S(2)}) copy-start(bf16[2,288]{1,0:T(2,128)(2,1)} %param.31) | copy-start | bytes 3460
  0.7 7.8 %copy-start.12 = (bf16[144,6,288]{2,0,1:T(8,128)(2,1)S(1)}, bf16[144,6,288]{2,0,1:T(8,128)(2,1)}, u32[]{:S(2)}) copy-start(bf16[144,6,288]{2,0,1:T(8,128)(2,1)} %param.38) | copy-start | bytes 1492996
  8.5 1.6 copy-start.7
  8.7 2.7 copy-start.8
  10.1 2.6 copy-start.27
  10.1 2.6 copy-start.21
  10.1 3.4 copy-start.25
  10.1 4.3 %copy-start.14 = (bf16[144,3,288]{2,0,1:T(8,128)(2,1)S(1)}, bf16[144,3,288]{2,0,1:T(8,128)(2,1)}, u32[]{:S(2)}) copy-start(bf16[144,3,288]{2,0,1:T(8,128)(2,1)} %param.30) | copy-start | bytes 746500
  11.4 3.4 copy-start.17
  12.7 2.9 copy-start.15
  12.7 2.9 copy-start.16
  12.7 3.8 copy-start.19
  16.5 133.2 %copy-start.20 = (s32[1280]{0:T(1024)S(1)}, s32[1280]{0:T(1024)}, u32[]{:S(2)}) copy-start(s32[1280]{0:T(1024)} %param.29) | copy-start | bytes 15364
  16.5 133.2 %copy-start.2 = (bf16[1280,32]{1,0:T(8,128)(2,1)S(1)}, bf16[1280,32]{1,0:T(8,128)(2,1)}, u32[]{:S(2)}) copy-start(bf16[1280,32]{1,0:T(8,128)(2,1)} %copy.85.hot) | copy-start | bytes 245764
  16.6 134.2 %copy-start.26 = (s32[1,6,4]{1,2,0:T(4,128)S(1)}, s32[1,6,4]{1,2,0:T(4,128)}, u32[]{:S(2)}) copy-start(s32[1,6,4]{1,2,0:T(4,128)} %param.28) | copy-start | bytes 292
  16.6 135.2 %copy-start.24 = (bf16[1152]{0:T(1024)(128)(2,1)S(1)}, bf16[1152]{0:T(1024)(128)(2,1)}, u32[]{:S(2)}) copy-start(bf16[1152]{0:T(1024)(128)(2,1)} %param.35) | copy-start | bytes 6916
  208.5 88.5 %copy-start.23 = (f32[1,1152]{1,0:T(1,128)S(1)}, f32[1,1152]{1,0:T(1,128)}, u32[]{:S(2)}) copy-start(f32[1,1152]{1,0:T(1,128)} %get-tuple-element.81) | copy-start | bytes 13828
  208.6 91.0 %copy-start.28 = (bf16[288]{0:T(512)(128)(2,1)S(1)}, bf16[288]{0:T(512)(128)(2,1)}, u32[]{:S(2)}) copy-start(bf16[288]{0:T(512)(128)(2,1)} %param.37) | copy-start | bytes 1732
  300.1 98.0 %copy-start.18 = (f32[8,8,640]{2,1,0:T(8,128)S(1)}, f32[8,8,640]{2,1,0:T(8,128)}, u32[]{:S(2)}) copy-start(f32[8,8,640]{2,1,0:T(8,128)} %get-tuple-element.92) | copy-start | bytes 491524
  398.1 3.0 copy-start.13
  398.1 4.0 copy-start.4
  402.8 1.3 copy-start.6
  404.1 1.7 copy-start.3
  405.8 1.6 copy-start.5
  407.5 3.1 copy-start.9
  407.5 5.9 %copy-start.11 = (f32[144,1152]{1,0:T(8,128)S(1)}, f32[144,1152]{1,0:T(8,128)}, u32[]{:S(2)}) copy-start(f32[144,1152]{1,0:T(8,128)} %get-tuple-element.180) | copy-start | bytes 1990660
  408.7 5.5 %copy-start.10 = (f32[144,1152]{1,0:T(8,128)S(1)}, f32[144,1152]{1,0:T(8,128)}, u32[]{:S(2)}) copy-start(f32[144,1152]{1,0:T(8,128)} %get-tuple-element.90) | copy-start | bytes 1990660
  412.7 2.4 copy-start.1

commit v7 on v6

--- a/solution.py
+++ b/solution.py
@@ -851,15 +851,18 @@
 
 
 class LineScatter:
-    def __init__(self, tok_at, grads, columns, cross_in, sums, above, below, sends, recvs, rows):
+    def __init__(self, tok_at, grads, columns, cross_in, passed, sends, recvs, rows):
         self.tok_at, self.grads, self.columns, self.rows = tok_at, grads, columns, rows
-        self.cross_in, self.sums, self.above, self.below = cross_in, sums, above, below
+        self.cross_in, self.passed = cross_in, passed
         self.sends, self.recvs = sends, recvs
         self.line = lax.div(tok_at, 2)
         self.side = lax.rem(tok_at, 2)
 
     def shard(self, owner):
         return self.grads.at[pl.ds(pl.multiple_of(owner * self.rows, 16), self.rows), self.columns]
+
+    def own_shard(self, place):
+        return self.shard(2 * place + self.side)
 
     def cross_copy(self, place):
         return remote(
@@ -872,80 +875,60 @@
 
     def down_copy(self, place):
         return remote(
-            self.sums.at[place], self.above.at[place], self.sends.at[1, place], self.recvs.at[1, place], peer(tok=self.tok_at - 2)
+            self.cross_in.at[place], self.passed.at[place], self.sends.at[1, place], self.recvs.at[1, place], peer(tok=self.tok_at - 2)
         )
 
-    def up_copy(self, place):
+    def up_copy(self, place, line):
+        slot = jnp.where(line == place, 4, place)
         return remote(
-            self.sums.at[place], self.below.at[place], self.sends.at[1, place], self.recvs.at[2, place], peer(tok=self.tok_at + 2)
+            self.cross_in.at[place], self.passed.at[slot], self.sends.at[1, place], self.recvs.at[2, place], peer(tok=self.tok_at + 2)
         )
 
     def start(self, places=(0, 3, 1, 2)):
         for place in places:
             self.cross_copy(place).start()
 
-    def fold(self, place):
+    def fold(self, place, own):
         self.cross_copy(place).wait_recv()
-        own = self.shard(2 * place + self.side)[...].astype(f32)
-        self.sums[place] = (own + self.cross_in[place].astype(f32)).astype(bf16)
-
-    def pass_on(self, place):
-        @pl.when(self.line > place)
+        self.cross_in[place] = (own.astype(f32) + self.cross_in[place].astype(f32)).astype(bf16)
+
+    def add_passed(self, place):
+        self.cross_in[place] = (self.cross_in[place].astype(f32) + self.passed[place].astype(f32)).astype(bf16)
+
+    def pass_on(self, place, hop):
+        @pl.when((self.line > place) & (self.line == 3 - hop))
         def _():
-            @pl.when(self.line < 3)
-            def _():
+            if hop:
                 self.down_copy(place).wait_recv()
-                self.sums[place] = (self.sums[place].astype(f32) + self.above[place].astype(f32)).astype(bf16)
-
+                self.add_passed(place)
             self.down_copy(place).start()
 
-        @pl.when(self.line < place)
+        @pl.when((self.line < place) & (self.line == hop))
         def _():
-            @pl.when(self.line > 0)
-            def _():
-                self.up_copy(place).wait_recv()
-                self.sums[place] = (self.sums[place].astype(f32) + self.below[place].astype(f32)).astype(bf16)
-
-            self.up_copy(place).start()
+            if hop:
+                self.up_copy(place, self.line).wait_recv()
+                self.add_passed(place)
+            self.up_copy(place, self.line + 1).start()
 
     def finish(self, out):
         own = self.line
-        out[...] = self.sums[own].astype(f32)
+        out[...] = self.cross_in[own].astype(f32)
 
         @pl.when(self.line < 3)
         def _():
             self.down_copy(own).wait_recv()
-            out[...] += self.above[own].astype(f32)
+            out[...] += self.passed[own].astype(f32)
 
         @pl.when(self.line > 0)
         def _():
-            self.up_copy(own).wait_recv()
-            out[...] += self.below[own].astype(f32)
+            self.up_copy(own, self.line).wait_recv()
+            out[...] += self.passed[4].astype(f32)
 
     def wait_send(self):
         for place in range(4):
             self.cross_copy(place).wait_send()
             pl.when(self.line > place)(lambda: self.down_copy(place).wait_send())
-            pl.when(self.line < place)(lambda: self.up_copy(place).wait_send())
-
-
-def greet_line(tok_at, mdl_at):
-    line, side = lax.div(tok_at, 2), lax.rem(tok_at, 2)
-    barrier = pltpu.get_barrier_semaphore()
-    mesh_id = pl.DeviceIdType.MESH
-    pl.semaphore_signal(barrier, inc=1, device_id=peer(tok=tok_at + 1 - 2 * side), device_id_type=mesh_id)
-    for step in range(1, 4):
-        pl.semaphore_signal(barrier, inc=1, device_id=peer(mdl=lax.rem(mdl_at + step, 4)), device_id_type=mesh_id)
-
-    @pl.when(line > 0)
-    def _():
-        pl.semaphore_signal(barrier, inc=1, device_id=peer(tok=tok_at - 2), device_id_type=mesh_id)
-
-    @pl.when(line < 3)
-    def _():
-        pl.semaphore_signal(barrier, inc=1, device_id=peer(tok=tok_at + 2), device_id_type=mesh_id)
-
-    pl.semaphore_wait(barrier, jnp.where((line > 0) & (line < 3), 6, 5))
+            pl.when(self.line < place)(lambda: self.up_copy(place, self.line + 1).wait_send())
 
 
 def own_block(mdl_at, values, width, act):
@@ -953,118 +936,247 @@
         pl.when(mdl_at == at)(lambda at=at: act(values[:, at * width : (at + 1) * width]))
 
 
-def back_kernel(
+def rear_kernel(
     two_full,
     branch_full,
     tokens_full,
     cot_blocks,
     mlp_blocks,
     unit_grads,
+    q_any,
+    k_any,
+    v_any,
+    mod_any,
+    qkv_any,
+    out_any,
+    att_any,
     hot,
+    hot_keep,
     pieces,
+    own_pieces,
+    out_bias_full,
     out_bias,
-    out_full,
+    down_bias,
     head_rows,
-    attended,
+    logsum,
+    seg_col,
+    seg_row,
+    tokens,
+    cotangent,
+    stats_one,
+    up_bias_sum,
+    mlp_sum,
+    ada_own,
+    cond_own,
+    embedding,
+    output,
+    grad_tokens,
+    up_out,
+    down_out,
+    head_grads,
+    gmod_all,
+    grad_ada,
+    grad_embed,
+    token_buf,
+    cot_buf,
+    two_buf,
+    branch_buf,
     q_heads,
     k_heads,
     v_heads,
-    logsum,
-    seg_col,
-    seg_row,
-    up_out,
-    down_out,
-    mlp_own,
-    grad_out,
-    dq_heads,
-    dk_heads,
-    dv_heads,
-    branch_own,
-    two_own,
-    stats,
-    attn_sums,
-    token_buf,
-    cot_buf,
+    mod_buf,
+    qkv_full,
+    out_full,
+    attended,
     g_heads,
     key_flip,
     dk_sum,
     dv_sum,
     out_sum,
-    cross_in,
-    sums,
-    above,
-    below,
-    mlp_parts,
-    mlp_near,
-    mlp_out,
-    mlp_far,
+    attn_sums,
+    branch_own,
+    two_own,
+    mlp_own,
+    stats_two,
+    unit_cross,
+    unit_passed,
+    unit_own,
+    head_cross,
+    head_passed,
+    qkv_rows,
+    full_grads,
+    col_blocks,
+    col_near,
+    col_out,
+    col_far,
+    gmod_own,
+    gmod_low,
+    row_sums,
+    part_own,
+    part_slots,
+    cond_slots,
     load_sems,
+    fetch_sems,
+    mod_sems,
     part_sems,
-    line_sends,
-    line_recvs,
-    col_sends,
-    col_recvs,
+    own_sems,
+    unit_sends,
+    unit_recvs,
+    head_sends,
+    head_recvs,
+    mlp_sends,
+    mlp_recvs,
+    one_sends,
+    one_recvs,
+    row_send,
+    row_recv,
+    gmod_send,
+    gmod_recv,
+    part_send,
+    part_recv,
+    cond_send,
+    cond_recv,
+    free_sem,
 ):
     tok_at = lax.axis_index("tok")
     mdl_at = lax.axis_index("mdl")
-    rows, width = two_full.shape
-    chunks = col_sends.shape[1]
+    far_at = lax.rem(mdl_at + 2, 4)
+    near_at = mdl_at + 1 - 2 * lax.rem(mdl_at, 2)
+    tok_count, slots = gmod_all.shape[0], gmod_all.shape[1]
+    rows, local_width = tokens.shape
+    width = qkv_full.shape[0]
+    units = up_out.shape[1]
+    own_rows = head_grads.shape[0]
+    heads, _, head_width = q_heads.shape
+    chunks = mlp_sends.shape[1]
     size = rows // chunks
-    units = up_out.shape[1]
-    heads, _, head_width = q_heads.shape
-    local_width = heads * head_width
     score_scale = 1.0 / math.sqrt(head_width)
-    greet_line(tok_at, mdl_at)
-    scatters = [
+    third = width // 3
+    unit_pieces = unit_sends.shape[0]
+    unit_piece = 2 * units // unit_pieces
+    head_pieces = head_sends.shape[0]
+    head_piece = head_grads.shape[1] // head_pieces
+
+    def span(chunk):
+        return pl.ds(pl.multiple_of(chunk * size, 128), size)
+
+    def loads(chunk, slot):
+        return (
+            pltpu.make_async_copy(tokens_full.at[span(chunk), :], token_buf.at[slot], load_sems.at[0, slot]),
+            pltpu.make_async_copy(cot_blocks.at[:, span(chunk), :], cot_buf.at[slot], load_sems.at[1, slot]),
+            pltpu.make_async_copy(two_full.at[span(chunk), :], two_buf.at[slot], load_sems.at[2, slot]),
+            pltpu.make_async_copy(branch_full.at[span(chunk), :], branch_buf.at[slot], load_sems.at[3, slot]),
+        )
+
+    def mod_load(index):
+        at = pl.ds(pl.multiple_of(index * third, 128), third)
+        slot = lax.rem(index, 2)
+        return pltpu.make_async_copy(mod_any.at[:, at], mod_buf.at[slot], mod_sems.at[slot])
+
+    fetches = [
+        pltpu.make_async_copy(source, target, fetch_sems.at[index])
+        for index, (source, target) in enumerate(
+            (
+                (out_any, out_full),
+                (att_any, attended),
+                (k_any, k_heads),
+                (q_any, q_heads),
+                (v_any, v_heads),
+                (qkv_any, qkv_full),
+            )
+        )
+    ]
+    for copy in loads(0, 0):
+        copy.start()
+    for copy in fetches[:3]:
+        copy.start()
+    greet(tok_at, mdl_at, tok_count, 4)
+    unit_scatters = [
         LineScatter(
             tok_at,
             unit_grads,
-            pl.ds(part * units, units),
-            cross_in.at[part],
-            sums.at[part],
-            above.at[part],
-            below.at[part],
-            line_sends.at[part],
-            line_recvs.at[part],
-            up_out.shape[0],
+            pl.ds(part * unit_piece, unit_piece),
+            unit_cross.at[part],
+            unit_passed.at[part],
+            unit_sends.at[part],
+            unit_recvs.at[part],
+            own_rows,
         )
-        for part in range(2)
+        for part in range(unit_pieces)
     ]
+    head_scatters = [
+        LineScatter(
+            tok_at,
+            full_grads,
+            pl.ds(part * head_piece, head_piece),
+            head_cross.at[part],
+            head_passed.at[part],
+            head_sends.at[part],
+            head_recvs.at[part],
+            own_rows,
+        )
+        for part in range(head_pieces)
+    ]
+    places = (0, 3, 1, 2)
+    unit_count = unit_pieces * len(places)
+    order = tuple((scatter, place) for scatter in unit_scatters + head_scatters for place in places)
+    lag = 4
+    steps = len(order) + 2 * lag
+
+    def own_load(index):
+        scatter, place = order[index]
+        return pltpu.make_async_copy(scatter.own_shard(place), unit_own.at[index % 2], own_sems.at[index % 2])
+
+    def serve(index):
+        if index < len(order):
+            scatter, place = order[index]
+            if index < unit_count:
+                own_load(index).wait()
+                if index + 1 < unit_count:
+                    own_load(index + 1).start()
+                scatter.fold(place, unit_own[index % 2])
+            else:
+                scatter.fold(place, scatter.own_shard(place)[...])
+        for hop in range(3):
+            if 0 <= index - hop * lag < len(order):
+                scatter, place = order[index - hop * lag]
+                scatter.pass_on(place, hop)
+
+    def serve_at(here, schedule):
+        for at, index in schedule:
+            pl.when(here == at)(lambda index=index: serve(index))
+
     mlps = ColumnReduce(
-        mdl_at, mlp_blocks, mlp_parts.at[0], mlp_parts.at[1], mlp_near, mlp_out, mlp_far, col_sends, col_recvs, size
-    )
-    for scatter in scatters:
+        mdl_at, mlp_blocks, col_blocks.at[mdl_at], col_blocks.at[far_at], col_near, col_out, col_far, mlp_sends, mlp_recvs, size
+    )
+    ones = ColumnReduce(
+        mdl_at, col_blocks, col_blocks.at[mdl_at], col_blocks.at[far_at], col_near, col_out, col_far, one_sends, one_recvs, size
+    )
+    for scatter in unit_scatters:
         scatter.start()
     for chunk in range(chunks):
         mlps.first(chunk)
     part_loads = [
-        pltpu.make_async_copy(mlp_blocks.at[mdl_at], mlp_parts.at[0], part_sems.at[0]),
-        pltpu.make_async_copy(mlp_blocks.at[lax.rem(mdl_at + 2, 4)], mlp_parts.at[1], part_sems.at[1]),
+        pltpu.make_async_copy(mlp_blocks.at[mdl_at], col_blocks.at[mdl_at], part_sems.at[0]),
+        pltpu.make_async_copy(mlp_blocks.at[far_at], col_blocks.at[far_at], part_sems.at[1]),
     ]
     for copy in part_loads:
         copy.start()
-
-    def span(chunk):
-        return pl.ds(pl.multiple_of(chunk * size, 128), size)
-
-    def loads(chunk, slot):
-        return (
-            pltpu.make_async_copy(tokens_full.at[span(chunk), :], token_buf.at[slot], load_sems.at[0, slot]),
-            pltpu.make_async_copy(cot_blocks.at[:, span(chunk), :], cot_buf.at[slot], load_sems.at[1, slot]),
-        )
-
-    for copy in loads(0, 0):
+    own_load(0).start()
+    for copy in fetches[3:]:
         copy.start()
+    mod_load(0).start()
+    mod_load(1).start()
+    attn_sums[...] = jnp.zeros_like(attn_sums)
+    out_sum[...] = jnp.zeros_like(out_sum)
+    for copy in fetches[:3]:
+        copy.wait()
     for head in range(heads):
         key_flip[head] = k_heads[head].T
-    attn_sums[...] = jnp.zeros_like(attn_sums)
-    out_sum[...] = jnp.zeros_like(out_sum)
     for copy in part_loads:
         copy.wait()
-    for chunk in range(chunks):
-        mlps.second(chunk)
-
-    def step(chunk, carry):
+
+    def back_step(chunk, carry):
         slot = lax.rem(chunk, 2)
 
         @pl.when(chunk + 1 < chunks)
@@ -1074,18 +1186,18 @@
 
         for copy in loads(chunk, slot):
             copy.wait()
+        mlps.second(chunk)
         here = span(chunk)
         hot_now = hot[here, :]
 
         def spread(part):
             return mm(hot_now, pieces[part], ((1,), (0,)))
 
-        token_rows = token_buf[slot].astype(f32)
         gate_one = spread(2)
-        middle = token_rows + gate_one * (branch_full[here, :].astype(f32) + out_bias[...])
+        middle = token_buf[slot].astype(f32) + gate_one * (branch_buf[slot].astype(f32) + out_bias_full[...])
         row_mean = jnp.mean(middle, axis=1, keepdims=True)
         normed, inverse = centre(middle)
-        grad_norm = two_full[here, :].astype(f32) * (1.0 + spread(4))
+        grad_norm = two_buf[slot].astype(f32) * (1.0 + spread(4))
         mean_one = jnp.mean(grad_norm, axis=1, keepdims=True)
         mean_two = jnp.mean(grad_norm * normed, axis=1, keepdims=True)
         cot_rows = jnp.concatenate([cot_buf[slot, at] for at in range(4)], axis=1).astype(f32)
@@ -1098,7 +1210,7 @@
             g_heads[head, here, :] = grad_att[:, head * head_width : (head + 1) * head_width]
         out_sum[...] += mm(grad_attn, attended[here, :], ((0,), (0,)))
         for column, value in enumerate((row_mean, inverse, mean_one, mean_two)):
-            stats[here, column : column + 1] = value
+            stats_two[here, column : column + 1] = value
 
         def keep(ref):
             def act(part):
@@ -1106,16 +1218,15 @@
 
             return act
 
-        own_block(mdl_at, branch_full[here, :], local_width, keep(branch_own))
-        own_block(mdl_at, two_full[here, :], local_width, keep(two_own))
+        own_block(mdl_at, branch_buf[slot], local_width, keep(branch_own))
+        own_block(mdl_at, two_buf[slot], local_width, keep(two_own))
+        serve_at(chunk, tuple((index + 1, index) for index in range(chunks - 1)))
         return carry
 
-    lax.fori_loop(0, chunks, step, 0)
-    grad_out[...] = out_sum[...].astype(bf16)
-    for chunk in range(chunks):
-        mlp_own[pl.ds(chunk * size, size), :] = mlps.third(chunk)
-
-    order = ((0, 0), (0, 3), (0, 1), (0, 2), (1, 0), (1, 3), (1, 1), (1, 2))
+    lax.fori_loop(0, chunks, back_step, 0)
+    served = chunks - 1
+    for copy in fetches[3:]:
+        copy.wait()
 
     def attend_step(at, carry):
         head = lax.div(at, chunks)
@@ -1138,188 +1249,47 @@
         grad_scores = (product - probs * jnp.sum(product, axis=0, keepdims=True)).astype(bf16)
         dk_sum[...] += mm(grad_scores, query, ((1,), (0,)))
         flipped = mm(key_flip[head], grad_scores, ((1,), (0,)))
-        dq_heads[head, here, :] = (flipped.T * score_scale).astype(bf16)
+        q_heads[head, here, :] = (flipped.T * score_scale).astype(bf16)
 
         @pl.when(chunk == chunks - 1)
         def _():
-            dk_heads[head] = (dk_sum[...] * score_scale).astype(bf16)
-            dv_heads[head] = dv_sum[...].astype(bf16)
-
-        for index, (part, place) in enumerate(order):
-
-            @pl.when(at == index)
-            def _():
-                scatters[part].fold(place)
-                scatters[part].pass_on(place)
-
+            k_heads[head] = (dk_sum[...] * score_scale).astype(bf16)
+            v_heads[head] = dv_sum[...].astype(bf16)
+
+        @pl.when(at < chunks)
+        def _():
+            mlp_own[span(at), :] = mlps.third(at).astype(bf16)
+
+        serve_at(at, tuple((2 * index + 1, served + index) for index in range(heads * chunks // 2)))
         return carry
 
     lax.fori_loop(0, chunks * heads, attend_step, 0)
-    scatters[0].finish(up_out)
-    scatters[1].finish(down_out)
-    for scatter in scatters:
-        scatter.wait_send()
+    served += heads * chunks // 2
     for chunk in range(chunks):
         mlps.wait_send(chunk)
-
-
-def back(two_full, branch_full, tokens_full, cot_blocks, mlp_blocks, unit_grads, hot, pieces, out_bias, out_full, head_rows, attended, q_heads, k_heads, v_heads, logsum, seg_col, seg_row, tok_count):
-    rows, width = two_full.shape
-    units = unit_grads.shape[1] // 2
-    heads, _, head_width = q_heads.shape
-    local_width = heads * head_width
-    own_rows = width // tok_count
-    chunks = 5
-    size = rows // chunks
-    dma = pltpu.SemaphoreType.DMA
-    vmem = pl.BlockSpec(memory_space=pltpu.VMEM)
-    anywhere = pl.BlockSpec(memory_space=pl.ANY)
-    low = lambda *shape: pltpu.VMEM(shape, bf16)
-    head_shape = jax.ShapeDtypeStruct((heads, rows, head_width), bf16)
-    return pl.pallas_call(
-        back_kernel,
-        out_shape=(
-            jax.ShapeDtypeStruct((own_rows, units), f32),
-            jax.ShapeDtypeStruct((own_rows, units), f32),
-            jax.ShapeDtypeStruct((rows, local_width), f32),
-            jax.ShapeDtypeStruct((width, local_width), bf16),
-            head_shape,
-            head_shape,
-            head_shape,
-            jax.ShapeDtypeStruct((rows, local_width), bf16),
-            jax.ShapeDtypeStruct((rows, local_width), bf16),
-            jax.ShapeDtypeStruct((rows, 128), f32),
-            jax.ShapeDtypeStruct((1, width), f32),
-        ),
-        in_specs=[vmem, vmem, anywhere, anywhere, anywhere] + [vmem] * 13,
-        out_specs=(vmem,) * 11,
-        scratch_shapes=[
-            low(2, size, width),
-            low(2, 4, size, local_width),
-            low(heads, rows, head_width),
-            low(heads, head_width, rows),
-            pltpu.VMEM((rows, head_width), f32),
-            pltpu.VMEM((rows, head_width), f32),
-            pltpu.VMEM((width, local_width), f32),
-            low(2, 4, own_rows, units),
-            low(2, 4, own_rows, units),
-            low(2, 4, own_rows, units),
-            low(2, 4, own_rows, units),
-            low(2, rows, local_width),
-            low(2, rows, local_width),
-            low(rows, local_width),
-            low(rows, local_width),
-            dma((2, 2)),
-            dma((2,)),
-            dma((2, 2, 4)),
-            dma((2, 3, 4)),
-            dma((3, chunks)),
-            dma((3, chunks)),
-        ],
-        compiler_params=pltpu.CompilerParams(collective_id=3, has_side_effects=True, vmem_limit_bytes=63 * 2**20),
-    )(two_full, branch_full, tokens_full, cot_blocks, mlp_blocks, unit_grads, hot, pieces, out_bias, out_full, head_rows, attended, q_heads, k_heads, v_heads, logsum, seg_col, seg_row)
-
-
-def tail_kernel(
-    dq_heads,
-    dk_heads,
-    dv_heads,
-    mod_one,
-    qkv_full,
-    grad_out,
-    tokens,
-    cotangent,
-    branch_own,
-    two_own,
-    mlp_own,
-    stats_one,
-    stats_two,
-    hot,
-    hot_keep,
-    own_pieces,
-    out_bias,
-    down_bias,
-    bias_sums,
-    ada_own,
-    cond_own,
-    embedding,
-    output,
-    grad_tokens,
-    head_grads,
-    gmod_all,
-    grad_ada,
-    grad_embed,
-    qkv_rows,
-    full_grads,
-    one_blocks,
-    one_near,
-    one_out,
-    one_far,
-    one_own,
-    gmod_own,
-    row_sums,
-    cross_in,
-    sums,
-    above,
-    below,
-    part_own,
-    part_slots,
-    cond_slots,
-    line_sends,
-    line_recvs,
-    col_sends,
-    col_recvs,
-    row_send,
-    row_recv,
-    gmod_send,
-    gmod_recv,
-    part_send,
-    part_recv,
-    cond_send,
-    cond_recv,
-):
-    tok_at = lax.axis_index("tok")
-    mdl_at = lax.axis_index("mdl")
-    tok_count, slots = gmod_all.shape[0], gmod_all.shape[1]
-    rows, local_width = tokens.shape
-    width = qkv_full.shape[0]
-    own_rows = head_grads.shape[0]
-    heads, _, head_width = dq_heads.shape
-    chunks = col_sends.shape[1]
-    size = rows // chunks
-    pieces_count = line_sends.shape[0]
-    piece = head_grads.shape[1] // pieces_count
-    greet(tok_at, mdl_at, tok_count, 4)
-    scatters = [
-        LineScatter(
-            tok_at,
-            full_grads,
-            pl.ds(part * piece, piece),
-            cross_in.at[part],
-            sums.at[part],
-            above.at[part],
-            below.at[part],
-            line_sends.at[part],
-            line_recvs.at[part],
-            own_rows,
-        )
-        for part in range(pieces_count)
-    ]
-    ones = ColumnReduce(
-        mdl_at, one_blocks, one_blocks.at[mdl_at], one_blocks.at[lax.rem(mdl_at + 2, 4)], one_near, one_out, one_far, col_sends, col_recvs, size
-    )
-    row_peers = AllToPeers("mdl", mdl_at, 4, row_send, row_recv)
-    gmods = AllToPeers("tok", tok_at, tok_count, gmod_send, gmod_recv)
-
-    def span(chunk):
-        return pl.ds(pl.multiple_of(chunk * size, 128), size)
-
-    gmod_own[...] = bias_sums[...]
+    for other in (near_at, far_at):
+        pl.semaphore_signal(free_sem, inc=1, device_id=peer(mdl=other), device_id_type=pl.DeviceIdType.MESH)
+
+    gmod_own[...] = jnp.zeros_like(gmod_own)
+    up_sum = up_bias_sum[...]
+    split = 6 * local_width - 3 * local_width
+    gmod_own[slots - 2 : slots - 1, 3 * local_width :] = up_sum[:, :split]
+    gmod_own[slots - 1 : slots, : units - split] = up_sum[:, split:]
+
+    def keep_sum(row, start):
+        def act(part):
+            gmod_own[row : row + 1, start : start + local_width] = part
+
+        return act
+
+    own_block(mdl_at, attn_sums[...], local_width, keep_sum(slots - 2, 2 * local_width))
+    own_block(mdl_at, mlp_sum[...], local_width, keep_sum(slots - 1, units - split))
 
     def gather_rows(chunk, carry):
         here = span(chunk)
-        parts = [part[head, here, :] for part in (dq_heads, dk_heads, dv_heads) for head in range(heads)]
-        joined = jnp.concatenate(parts, axis=1)
+        joined = jnp.concatenate(
+            [part[head, here, :] for part in (q_heads, k_heads, v_heads) for head in range(heads)], axis=1
+        )
         qkv_rows[here, :] = joined
         total = jnp.sum(joined.astype(f32), axis=0, keepdims=True)
         gmod_own[slots - 2 : slots - 1, :local_width] += total[:, :local_width]
@@ -1327,31 +1297,38 @@
         return carry
 
     lax.fori_loop(0, chunks, gather_rows, 0)
-    third = width // 3
-
-    def grads(index, carry):
-        at = pl.ds(pl.multiple_of(index * third, 128), third)
-        full_grads[at, :] = jnp.concatenate(
-            [mm(mod_one[:, at], qkv_rows[...], ((0,), (0,))).astype(bf16), grad_out[at, :]], axis=1
-        )
-        return carry
-
-    lax.fori_loop(0, 3, grads, 0)
-    for scatter in scatters:
-        scatter.start()
+    serve(served)
+    serve(served + 1)
+    served += 2
+    pl.semaphore_wait(free_sem, 2)
 
     def ones_step(chunk, carry):
         here = span(chunk)
         part = mm(qkv_rows[here, :], qkv_full[...], ((1,), (1,))).astype(bf16)
         for at in range(4):
-            one_blocks[at, here, :] = part[:, at * local_width : (at + 1) * local_width]
+            col_blocks[at, here, :] = part[:, at * local_width : (at + 1) * local_width]
         ones.first(chunk)
         pl.when(chunk >= 1)(lambda: ones.second(chunk - 1))
+        serve_at(chunk, ((1, served), (3, served + 1)))
         return carry
 
     lax.fori_loop(0, chunks, ones_step, 0)
     ones.second(chunks - 1)
-    order = tuple((part, place) for part in range(pieces_count) for place in (0, 3, 1, 2))
+    served += 2
+
+    def grads(index, carry):
+        at = pl.ds(pl.multiple_of(index * third, 128), third)
+        mod_load(index).wait()
+        weight = mm(mod_buf[lax.rem(index, 2)], qkv_rows[...], ((0,), (0,))).astype(bf16)
+        full_grads[at, :] = jnp.concatenate([weight, out_sum[at, :].astype(bf16)], axis=1)
+        pl.when(index == 0)(lambda: mod_load(2).start())
+        serve_at(index, ((0, served), (1, served + 1), (2, served + 2)))
+        return carry
+
+    lax.fori_loop(0, 3, grads, 0)
+    for scatter in head_scatters[:-1]:
+        scatter.start()
+    served += 3
     pick = lax.broadcasted_iota(jnp.int32, (8, local_width), 0)
     first_row = jnp.where(pick == 0, 1.0, 0.0).astype(bf16)
     second_row = jnp.where(pick == 1, 1.0, 0.0).astype(bf16)
@@ -1367,7 +1344,7 @@
 
         token_rows = tokens[here, :].astype(f32)
         branch = branch_own[here, :].astype(f32) + out_bias[...]
-        mlp = mlp_own[here, :] + down_bias[...]
+        mlp = mlp_own[here, :].astype(f32) + down_bias[...]
         cot_rows = cotangent[here, :].astype(f32)
         grad_two = two_own[here, :].astype(f32)
         middle = token_rows + spread(2) * branch
@@ -1379,7 +1356,6 @@
         )
         grad_tokens[here, :] = grad_middle
         grad_one = ones.third(chunk)
-        one_own[here, :] = grad_one
         normed_one = (token_rows - stats_one[here, 0:1]) * stats_one[here, 1:2]
         grad_norm = grad_one * (1.0 + spread(1))
         total = jnp.zeros((8, size), f32)
@@ -1400,22 +1376,23 @@
             gmod_own[:, part * local_width : (part + 1) * local_width] += mm(chosen, high, ((0,), (0,))) + mm(
                 chosen, rest, ((0,), (0,))
             )
-        for index, (part, place) in enumerate(order[: 2 * chunks]):
-
-            @pl.when(chunk == index // 2)
-            def _():
-                scatters[part].fold(place)
-                scatters[part].pass_on(place)
-
+        serve_at(chunk, ((0, served), (1, served + 1), (1, served + 2), (2, served + 3), (3, served + 4), (4, served + 5)))
         return carry
 
     lax.fori_loop(0, chunks, final_step, 0)
+    served += 6
+    row_peers = AllToPeers("mdl", mdl_at, 4, row_send, row_recv)
+    gmods = AllToPeers("tok", tok_at, tok_count, gmod_send, gmod_recv)
     row_peers.start(lambda other: row_sums.at[mdl_at], row_sums)
-    gmods.start(lambda other: gmod_own, gmod_all)
-    gmod_all[tok_at] = gmod_own[...]
-    for part, place in order[2 * chunks :]:
-        scatters[part].fold(place)
-        scatters[part].pass_on(place)
+    turn = gmod_low.shape[2]
+    gmod_low[tok_at] = jnp.zeros_like(gmod_low[tok_at])
+    gmod_low[tok_at, :slots, :] = gmod_own[:, :turn].astype(bf16)
+    gmod_low[tok_at, slots:, : 6 * local_width - turn] = gmod_own[:, turn:].astype(bf16)
+    gmods.start(lambda other: gmod_low.at[tok_at], gmod_low)
+    head_scatters[-1].start()
+    serve(served)
+    serve(served + 1)
+    served += 2
     row_peers.wait_recv(lambda other: row_sums.at[mdl_at], row_sums)
     totals = ((row_sums[0] + row_sums[1] + row_sums[2] + row_sums[3]) * (1.0 / width)).T
     for chunk in range(chunks):
@@ -1423,12 +1400,19 @@
         flip = totals[chunk * size : (chunk + 1) * size]
         inverse_one = stats_one[here, 1:2]
         normed_one = (tokens[here, :].astype(f32) - stats_one[here, 0:1]) * inverse_one
-        grad_norm = one_own[here, :] * (1.0 + mm(hot[here, :], own_pieces[1], ((1,), (0,))))
+        grad_one = col_blocks[mdl_at, here, :].astype(f32) + col_near[0, here, :].astype(f32) + col_far[here, :].astype(f32)
+        grad_norm = grad_one * (1.0 + mm(hot[here, :], own_pieces[1], ((1,), (0,))))
         grad_tokens[here, :] += inverse_one * (grad_norm - flip[:, 0:1] - normed_one * flip[:, 1:2])
-    gmods.wait_recv(lambda other: gmod_own, gmod_all)
-    high, rest = split_two(gmod_all[...].reshape(tok_count * slots, gmod_all.shape[2]))
-    ada = ada_own[...]
-    part_own[...] = mm(high, ada, ((1,), (1,))) + mm(rest, ada, ((1,), (1,)))
+    serve(served)
+    serve(served + 1)
+    served += 2
+    gmods.wait_recv(lambda other: gmod_low.at[tok_at], gmod_low)
+    for at in range(tok_count):
+        gmod_all[at] = jnp.concatenate(
+            [gmod_low[at, :slots, :].astype(f32), gmod_low[at, slots:, : 6 * local_width - turn].astype(f32)], axis=1
+        )
+    gathered = gmod_all[...].reshape(tok_count * slots, gmod_all.shape[2]).astype(bf16)
+    part_own[...] = mm(gathered, ada_own[...], ((1,), (1,)))
     owner = lax.div(tok_at, 2)
     half = lax.rem(tok_at, 2)
 
@@ -1437,7 +1421,7 @@
 
     pl.when(mdl_at != owner)(lambda: part_copy(mdl_at).start())
     cond = cond_own[...]
-    grad_ada[...] = mm(cond, high, ((0,), (0,))) + mm(cond, rest, ((0,), (0,)))
+    grad_ada[...] = mm(cond, gathered, ((0,), (0,)))
 
     def cond_copy(step):
         other = lax.rem(tok_at + step, tok_count)
@@ -1454,8 +1438,12 @@
         for step in range(1, tok_count):
             cond_copy(step).start()
 
-    for part, scatter in enumerate(scatters):
-        scatter.finish(head_grads.at[:, pl.ds(part * piece, piece)])
+    for index in range(served, steps):
+        serve(index)
+    for part, scatter in enumerate(unit_scatters):
+        at = part * unit_piece
+        target = up_out if at < units else down_out
+        scatter.finish(target.at[:, pl.ds(at % units, unit_piece)])
     for side in range(2):
         giver = 2 * mdl_at + side
 
@@ -1467,7 +1455,9 @@
     embed = embedding[...]
     gate = 1.0 / (1.0 + jnp.exp(-embed))
     grad_embed[...] = grad_cond * gate * (1.0 + embed * (1.0 - gate))
-    gmods.wait_send(lambda other: gmod_own, gmod_all)
+    for part, scatter in enumerate(head_scatters):
+        scatter.finish(head_grads.at[:, pl.ds(part * head_piece, head_piece)])
+    gmods.wait_send(lambda other: gmod_low.at[tok_at], gmod_low)
     row_peers.wait_send(lambda other: row_sums.at[mdl_at], row_sums)
     pl.when(mdl_at != owner)(lambda: part_copy(mdl_at).wait_send())
 
@@ -1476,58 +1466,99 @@
         for step in range(1, tok_count):
             cond_copy(step).wait_send()
 
-    for scatter in scatters:
+    for scatter in unit_scatters + head_scatters:
         scatter.wait_send()
     for chunk in range(chunks):
         ones.wait_send(chunk)
 
 
-def tail(
-    dq_heads, dk_heads, dv_heads, mod_one, qkv_full, grad_out, tokens, cotangent, branch_own, two_own, mlp_own, stats_one, stats_two,
-    hot, hot_keep, own_pieces, out_bias, down_bias, bias_sums, ada_own, cond_own, embedding, tok_count,
+def rear(
+    two_full, branch_full, tokens_full, cot_blocks, mlp_blocks, unit_grads, q_heads, k_heads, v_heads, mod_one, qkv_full, out_full, attended,
+    hot, hot_keep, pieces, own_pieces, out_bias_full, out_bias, down_bias, head_rows, logsum, seg_col, seg_row, tokens, cotangent, stats_one,
+    up_bias_sum, mlp_sum, ada_own, cond_own, embedding, tok_count,
 ):
     rows, local_width = tokens.shape
     width, three = qkv_full.shape
+    units = unit_grads.shape[1] // 2
     own_rows = width // tok_count
-    slots, mod_width = bias_sums.shape
+    slots = 8
+    mod_width = ada_own.shape[1]
     crops = cond_own.shape[0]
-    chunks, pieces_count = 5, 3
-    total = three + grad_out.shape[1]
-    piece = total // pieces_count
+    heads, _, head_width = q_heads.shape
+    chunks, unit_pieces, head_pieces = 5, 6, 3
+    size = rows // chunks
+    total = three + local_width
     dma = pltpu.SemaphoreType.DMA
     vmem = pl.BlockSpec(memory_space=pltpu.VMEM)
+    anywhere = pl.BlockSpec(memory_space=pl.ANY)
     low = lambda *shape: pltpu.VMEM(shape, bf16)
+    wide = lambda *shape: pltpu.VMEM(shape, f32)
+    shape = jax.ShapeDtypeStruct
+    unit_piece, head_piece = 2 * units // unit_pieces, total // head_pieces
     return pl.pallas_call(
-        tail_kernel,
+        rear_kernel,
         out_shape=(
-            jax.ShapeDtypeStruct((rows, local_width), bf16),
-            jax.ShapeDtypeStruct((rows, local_width), f32),
-            jax.ShapeDtypeStruct((own_rows, total), f32),
-            jax.ShapeDtypeStruct((tok_count, slots, mod_width), f32),
-            jax.ShapeDtypeStruct((own_rows, mod_width), f32),
-            jax.ShapeDtypeStruct(embedding.shape, f32),
+            shape((rows, local_width), bf16),
+            shape((rows, local_width), f32),
+            shape((own_rows, units), f32),
+            shape((own_rows, units), f32),
+            shape((own_rows, total), f32),
+            shape((tok_count, slots, mod_width), f32),
+            shape((own_rows, mod_width), f32),
+            shape(embedding.shape, f32),
         ),
-        in_specs=[vmem] * 22,
-        out_specs=(vmem,) * 6,
+        in_specs=[anywhere] * 13 + [vmem] * 19,
+        out_specs=(vmem,) * 8,
         scratch_shapes=[
+            low(2, size, width),
+            low(2, 4, size, local_width),
+            low(2, size, width),
+            low(2, size, width),
+            low(heads, rows, head_width),
+            low(heads, rows, head_width),
+            low(heads, rows, head_width),
+            low(2, rows, width // 3),
+            low(width, three),
+            low(width, local_width),
+            low(rows, local_width),
+            low(heads, rows, head_width),
+            low(heads, head_width, rows),
+            wide(rows, head_width),
+            wide(rows, head_width),
+            wide(width, local_width),
+            wide(1, width),
+            low(rows, local_width),
+            low(rows, local_width),
+            low(rows, local_width),
+            wide(rows, 128),
+            low(unit_pieces, 4, own_rows, unit_piece),
+            low(unit_pieces, 5, own_rows, unit_piece),
+            low(2, own_rows, unit_piece),
+            low(head_pieces, 4, own_rows, head_piece),
+            low(head_pieces, 5, own_rows, head_piece),
             low(rows, three),
             low(width, total),
             low(4, rows, local_width),
             low(2, rows, local_width),
             low(rows, local_width),
             low(rows, local_width),
-            pltpu.VMEM((rows, local_width), f32),
-            pltpu.VMEM((slots, mod_width), f32),
-            pltpu.VMEM((4, 8, rows), f32),
-            low(pieces_count, 4, own_rows, piece),
-            low(pieces_count, 4, own_rows, piece),
-            low(pieces_count, 4, own_rows, piece),
-            low(pieces_count, 4, own_rows, piece),
-            pltpu.VMEM((crops, own_rows), f32),
-            pltpu.VMEM((4, crops, own_rows), f32),
-            pltpu.VMEM((2, crops, own_rows), f32),
-            dma((pieces_count, 2, 4)),
-            dma((pieces_count, 3, 4)),
+            wide(slots, mod_width),
+            low(tok_count, 2 * slots, -(-mod_width // 256) * 128),
+            wide(4, 8, rows),
+            wide(crops, own_rows),
+            wide(4, crops, own_rows),
+            wide(2, crops, own_rows),
+            dma((4, 2)),
+            dma((6,)),
+            dma((2,)),
+            dma((2,)),
+            dma((2,)),
+            dma((unit_pieces, 2, 4)),
+            dma((unit_pieces, 3, 4)),
+            dma((head_pieces, 2, 4)),
+            dma((head_pieces, 3, 4)),
+            dma((3, chunks)),
+            dma((3, chunks)),
             dma((3, chunks)),
             dma((3, chunks)),
             dma((4,)),
@@ -1538,11 +1569,13 @@
             dma((4,)),
             dma((tok_count,)),
             dma((2,)),
+            pltpu.SemaphoreType.REGULAR,
         ],
-        compiler_params=pltpu.CompilerParams(collective_id=1, has_side_effects=True, vmem_limit_bytes=63 * 2**20),
+        compiler_params=pltpu.CompilerParams(collective_id=1, has_side_effects=True, vmem_limit_bytes=67043328),
     )(
-        dq_heads, dk_heads, dv_heads, mod_one, qkv_full, grad_out, tokens, cotangent, branch_own, two_own, mlp_own, stats_one, stats_two,
-        hot, hot_keep, own_pieces, out_bias, down_bias, bias_sums, ada_own, cond_own, embedding,
+        two_full, branch_full, tokens_full, cot_blocks, mlp_blocks, unit_grads, q_heads, k_heads, v_heads, mod_one, qkv_full, out_full, attended,
+        hot, hot_keep, pieces, own_pieces, out_bias_full, out_bias, down_bias, head_rows, logsum, seg_col, seg_row, tokens, cotangent, stats_one,
+        up_bias_sum, mlp_sum, ada_own, cond_own, embedding,
     )
 
 
@@ -1653,21 +1686,11 @@
     mlp_blocks, two_low, unit_grads, grad_up_bias, mlp_sums = feed(
         branch_low, tokens_full, cot_blocks, hot, hot_keep, pieces, out_bias_full, unit_full, up_bias.astype(f32)[None], chan_rows
     )
-    grad_up_bias = grad_up_bias[0]
-    grad_up, grad_down, mlp_own, grad_out, dq_heads, dk_heads, dv_heads, branch_own, two_own, stats, attn_sums = back(
-        two_low, branch_low, tokens_full, cot_blocks, mlp_blocks, unit_grads, hot, pieces, out_bias_full, out_full, head_rows,
-        attended, q_heads, k_heads, v_heads, logsum_rows, segment[0][:, None], segment, tok_count,
-    )
     own_pieces = lax.dynamic_slice_in_dim(pieces, mdl_at * local_width, local_width, axis=2)
-    bias_row = jnp.concatenate(
-        [jnp.zeros((2 * local_width,), f32), own_cols(attn_sums)[0], grad_up_bias, own_cols(mlp_sums)[0]]
-    )
-    bias_row = jnp.pad(bias_row, (0, 2 * 6 * local_width - bias_row.shape[0])).reshape(2, 6 * local_width)
-    bias_sums = jnp.pad(bias_row, ((slot_count, 0), (0, 0)))
-    output, grad_tokens, grad_heads, gmod_all, grad_ada, grad_embed = tail(
-        dq_heads, dk_heads, dv_heads, modulated_one, qkv_full, grad_out, tokens, cotangent, branch_own, two_own, mlp_own,
-        stats_one, stats, hot, hot_keep, own_pieces, out_bias.astype(f32)[None], down_bias.astype(f32)[None], bias_sums,
-        ada_own, cond_own, embedding, tok_count,
+    output, grad_tokens, grad_up, grad_down, grad_heads, gmod_all, grad_ada, grad_embed = rear(
+        two_low, branch_low, tokens_full, cot_blocks, mlp_blocks, unit_grads, q_heads, k_heads, v_heads, modulated_one, qkv_full, out_full,
+        attended, hot, hot_keep, pieces, own_pieces, out_bias_full, out_bias.astype(f32)[None], down_bias.astype(f32)[None], head_rows,
+        logsum_rows, segment[0][:, None], segment, tokens, cotangent, stats_one, grad_up_bias, mlp_sums, ada_own, cond_own, embedding, tok_count,
     )
     grad_ada = grad_ada.reshape(own_rows, 6, local_width)
     grad_ada_bias = jnp.sum(gmod_all[:, :slot_count], axis=(0, 1)).reshape(6, local_width)

time: 417 us -> 360 us (0.86)
  Pallas kernels: 374 us -> 307 us
    pallas_call x2 -> x1, Pallas kernels: 186 us -> 119 us  [rear(): pl.pallas_call(rear_kernel, out_shape=(shape((rows, local_width), bf16),...]
    unnamed x70 -> x46, local copies, waits for them, and re-layouts: 10.2 us -> 11.4 us
where the time goes in v7:
time: 360 us; the launch traced here: 356 us
  Pallas kernels  307 us (85%)
  local copies, waits for them, and re-layouts  31.6 us (9%)
  other arithmetic  11.7 us (3%)
  matrix products  5.03 us (1%)
    pallas_call x1, Pallas kernels, front(): pl.pallas_call(front_kernel, out_shape=(shape((tok_count, slots, small_wi...  132 us
    pallas_call x1, Pallas kernels, rear(): pl.pallas_call(rear_kernel, out_shape=(shape((rows, local_width), bf16),...  119 us
    pallas_call x1, Pallas kernels, feed(): pl.pallas_call(feed_kernel, out_shape=(jax.ShapeDtypeStruct((4, rows, loc...  56.2 us
    unnamed x46, local copies, waits for them, and re-layouts  11.4 us

profile of v7, /device:TPU:0, one launch (start us, length us, event | category | flops | bytes accessed | tf_op | source)
XLA Modules:
  0.0 356.5 jit_solution(15560757219338330656)
XLA Ops:
  0.7 0.7 add.32
  6.5 1.2 reshape.262.down_bias
  7.8 0.8 fusion.16
  9.4 0.7 convert_element_type.76
  10.1 1.3 reshape.261.up_bias
  12.3 0.8 reshape.259
  13.1 1.4 fusion.8
  14.5 0.7 select_maximum_fusion.1.small_own
  17.6 1.0 broadcast_multiply_fusion.hot_keep
  19.0 0.8 pad_maximum_fusion.1.head_shard
  19.9 1.1 broadcast_in_dim_squeeze.6.seg_col
  20.9 0.9 pad_maximum_fusion.unit_shard
  22.0 1.4 reshape.250.ada_own
  23.4 1.8 copy.82.tokens
  25.2 1.3 copy.83.cotangent
  26.5 131.7 %shard_map.308 = (f32[8,8,640]{2,1,0:T(8,128)}, f32[64,288]{1,0:T(8,128)}, bf16[64,144]{1,0:T(8,128)(2,1)}, f32[6,8,1152]{2,1,0:T(8,128)}, bf16[6,32,1152]{2,1,0...) custom-call(f32[8,640]{1,0:T(8,128)} %select_maximum_fusion.1.small_, ...), custom_call_target="tpu_custom_call" | custom-call | tf_op jit(solution)/shard_map/pallas_call | solution.py:575
  158.2 1.4 slice_bitcast_fusion.2.out_bias.out_bias_full
  159.6 1.0 convert_reduce_fusion
  160.6 1.5 slice_bitcast_fusion.1
  162.7 1.7 constant_dynamic-slice_fusion.own_pieces
  164.4 56.2 %shard_map.309 = (bf16[4,1280,288]{2,1,0:T(8,128)(2,1)}, bf16[1280,1152]{1,0:T(8,128)(2,1)}, bf16[1152,2304]{1,0:T(8,128)(2,1)}, f32[1,1152]{1,0:T(1,128)}, f32[1,1152]{1,0:T(1,128)}) custom-call(bf16[1280,1152]{1,0:T(8,128)(2,1)} %get-tuple-element.45.branch_full, bf16[1280,1152]{1,0:T(8,128)(2,1)} %get-tuple-element.46.tokens_full, ...), custom_call_target="tpu_custom_call" | custom-call | tf_op jit(solution)/shard_map/pallas_call | solution.py:772
  220.7 119.1 %shard_map.310 = (bf16[1280,288]{1,0:T(8,128)(2,1)}, f32[1280,288]{1,0:T(8,128)}, f32[144,1152]{1,0:T(8,128)}, f32[144,1152]{1,0:T(8,128)}, f32[144,1152]{1,0:T(...) custom-call(bf16[1280,1152]{1,0:T(8,128)(2,1)} %get-tuple-element.51.two_full, ...), custom_call_target="tpu_custom_call" | custom-call | tf_op jit(solution)/shard_map/pallas_call | solution.py:1498
  339.8 1.9 fusion.6
  341.7 2.4 copy.93
  347.0 0.8 slice_bitcast_fusion
  348.3 0.9 copy.95
  349.2 1.7 fusion.1
  350.9 1.6 copy.94
  352.5 0.7 reshape.256
  353.2 1.3 copy.96
  354.5 0.8 copy.99
  355.4 0.8 copy.100
  (82 shorter events, 14.0 us)
Async XLA Ops:
  0.6 17.9 %copy-start.11 = (bf16[144,3,288]{2,0,1:T(8,128)(2,1)S(1)}, bf16[144,3,288]{2,0,1:T(8,128)(2,1)}, u32[]{:S(2)}) copy-start(bf16[144,3,288]{2,0,1:T(8,128)(2,1)} %param.30) | copy-start | bytes 746500
  6.5 10.1 %copy-start.15 = (f32[1,288]{1,0:T(1,128)}, f32[1,288]{1,0:T(1,128)S(1)}, u32[]{:S(2)}) copy-start(f32[1,288]{1,0:T(1,128)S(1)} %reshape.260.out_bias) | copy-start | bytes 3460
  13.1 5.9 %copy-start.14 = (bf16[288,144]{0,1:T(8,128)(2,1)S(1)}, bf16[288,144]{0,1:T(8,128)(2,1)}, u32[]{:S(2)}) copy-start(bf16[288,144]{0,1:T(8,128)(2,1)} %param.32) | copy-start | bytes 248836
  17.6 4.3 %copy-start = (bf16[1280,32]{1,0:T(8,128)(2,1)}, bf16[1280,32]{1,0:T(8,128)(2,1)S(1)}, u32[]{:S(2)}) copy-start(bf16[1280,32]{1,0:T(8,128)(2,1)S(1)} %copy.84.hot) | copy-start | bytes 245764
  17.6 3.4 copy-start.12
  17.6 3.3 copy-start.13
  18.7 3.1 copy-start.9
  21.8 1.6 copy-start.4
  22.0 3.2 copy-start.5
  339.7 4.3 %copy-start.6 = (f32[8,8,1728]{2,1,0:T(8,128)S(1)}, f32[8,8,1728]{2,1,0:T(8,128)}, u32[]{:S(2)}) copy-start(f32[8,8,1728]{2,1,0:T(8,128)} %get-tuple-element.70) | copy-start | bytes 1327108
  339.7 7.2 %copy-start.3 = (f32[144,1152]{1,0:T(8,128)S(1)}, f32[144,1152]{1,0:T(8,128)}, u32[]{:S(2)}) copy-start(f32[144,1152]{1,0:T(8,128)} %get-tuple-element.69) | copy-start | bytes 1990660
  347.8 1.4 copy-start.10
  347.8 1.4 copy-start.16
  347.8 1.4 copy-start.17
  347.8 3.1 copy-start.1
  350.9 1.6 copy-start.2
  353.2 1.3 copy-start.8
  353.2 2.2 copy-start.7
